TPU v7x, 32 devices: a whole 2x2x4 slice. The times are simulated.
32 devices in a mesh: space: 16 (over z, x, core), chan: 2 (over y).
Axes of the slice: x: 2, y: 2, z: 4, core: 2. Of those that a mesh axis runs over, the one named last changes fastest.
Arguments:
- features: bfloat16 [65536, 256], P('space'), may hold values from -6 to 6
- grad_out: bfloat16 [65536, 256], P('space', 'chan'), may hold values from -6 to 6
- weights: bfloat16 [27, 256, 256], P(None, None, 'chan'), may hold values from -0.078125 to 0.078125
- occupancy: int32 [65536], P('space'), may hold values 0 or 1
- block_list: int32 [16, 8], P('space'), may hold values from 0 to 7, each once within a row
- block_count: int32 [16], P('space'), may hold values from 1 to 8, as said below
Outputs:
- grad_features: bfloat16 [65536, 256], P('space', 'chan')
- grad_weights: float32 [6912, 256], P('space', 'chan')
Inputs may be any that keep to these rules, and one draw needn't show every extreme that they name: `block_count`: some region has all 8 blocks active.
All inputs are finite; a program needn't handle non-finite values. No bound on the sum of `occupancy` on one device may be relied on, other than what follows from the above.
Results may differ from a plain program's by a relative error of at most 0.001.
Values may be sent and summed in bfloat16 or wider, within the bound.
No kernel may reach another device: no remote copies, remote signals or barrier semaphores. Data moves between devices by JAX's collectives and lax.ppermute only.
A program may use at most 64 MiB of HBM per device.

v0:
```python
import math

import jax
import jax.numpy as jnp
from jax import lax
from jax.sharding import PartitionSpec as P

EDGE = 8
LAYERZ = 2
NBLK = 8


OFFSETS = [
    (first, second, third) for first in (-1, 0, 1) for second in (-1, 0, 1) for third in (-1, 0, 1)
]


def shifted(block, axis, distance):
    devices = range(lax.axis_size(axis))
    route = [(i - distance, i) for i in devices if i - distance in devices]
    return lax.ppermute(block, axis, route)


def locate_side(device_total):
    plane_side = 1
    for candidate in range(1, 33):
        if 2 * candidate**3 == device_total:
            plane_side = candidate
    return plane_side


def extend_faces(feat, grad, dim, stride, coord, region_count):
    length = feat.shape[dim]
    feat_low = lax.slice_in_dim(feat, 0, 1, axis=dim)
    grad_low = lax.slice_in_dim(grad, 0, 1, axis=dim)
    feat_high = lax.slice_in_dim(feat, length - 1, length, axis=dim)
    grad_high = lax.slice_in_dim(grad, length - 1, length, axis=dim)
    below_feat, below_grad = shifted((feat_high, grad_high), "space", stride)
    above_feat, above_grad = shifted((feat_low, grad_low), "space", -stride)
    keep_below = (coord > 0).astype(jnp.bfloat16)
    keep_above = (coord < region_count - 1).astype(jnp.bfloat16)
    feat = jnp.concatenate([below_feat * keep_below, feat, above_feat * keep_above], axis=dim)
    grad = jnp.concatenate([below_grad * keep_below, grad, above_grad * keep_above], axis=dim)
    return (feat, grad)


def body(features, grad_out, weights, occupancy, block_list, block_count):
    device_total = lax.axis_size("space")
    plane_side = locate_side(device_total)
    depth_count = 2 * plane_side
    cells, cin_total = features.shape
    cout_half = grad_out.shape[1]
    span_xy = 2 * EDGE
    span_z = LAYERZ * EDGE
    dev_index = lax.axis_index("space")
    coord_z = dev_index % depth_count
    coord_y = dev_index // depth_count % plane_side
    coord_x = dev_index // (depth_count * plane_side)
    block_order = block_list[0]
    live_count = block_count[0]
    block_slots = jnp.arange(NBLK, dtype=jnp.int32)
    position = jnp.sum(
        jnp.where(block_order[:, None] == block_slots[None, :], block_slots[:, None], 0), axis=0
    )
    active_flag = (position < live_count).astype(jnp.float32)
    block_grid = jnp.broadcast_to(
        active_flag.reshape(2, 1, 2, 1, LAYERZ, 1), (2, EDGE, 2, EDGE, LAYERZ, EDGE)
    ).reshape(span_xy, span_xy, span_z)
    cell_mask = (block_grid * occupancy.reshape(span_xy, span_xy, span_z).astype(jnp.float32))[
        ..., None
    ]
    mask_bf = cell_mask.astype(jnp.bfloat16)
    feat_masked = features.reshape(span_xy, span_xy, span_z, cin_total) * mask_bf
    grad_masked = grad_out.reshape(span_xy, span_xy, span_z, cout_half) * mask_bf
    weight_matrix = weights.transpose(0, 2, 1).reshape(27 * cout_half, cin_total)
    own_start = jnp.int32(0)
    feat_pad, grad_pad = extend_faces(
        feat_masked, grad_masked, 0, depth_count * plane_side, coord_x, plane_side
    )
    feat_pad, grad_pad = extend_faces(feat_pad, grad_pad, 1, depth_count, coord_y, plane_side)
    feat_pad, grad_pad = extend_faces(feat_pad, grad_pad, 2, 1, coord_z, depth_count)
    grad_width = grad_pad.shape[3]
    out_width = weight_matrix.shape[1]
    window = EDGE + 2

    def visit_block(turn_index, running):
        data_acc, weight_acc = running
        block_id = block_order[turn_index]
        block_x = block_id // (2 * LAYERZ)
        block_y = block_id // LAYERZ % 2
        block_z = block_id % LAYERZ
        anchor_x = block_x * EDGE
        anchor_y = block_y * EDGE
        anchor_z = block_z * EDGE
        zero_index = jnp.int32(0)
        feat_window = lax.dynamic_slice(
            feat_pad,
            (anchor_x, anchor_y, anchor_z, zero_index),
            (window, window, window, cin_total),
        )
        grad_window = lax.dynamic_slice(
            grad_pad,
            (anchor_x, anchor_y, anchor_z, zero_index),
            (window, window, window, grad_width),
        )
        grad_centre = grad_window[1:-1, 1:-1, 1:-1].reshape(-1, cout_half)
        feat_columns = jnp.concatenate(
            [
                feat_window[
                    1 + off_x : 1 + off_x + EDGE,
                    1 + off_y : 1 + off_y + EDGE,
                    1 + off_z : 1 + off_z + EDGE,
                ].reshape(-1, cin_total)
                for off_x, off_y, off_z in OFFSETS
            ],
            axis=1,
        )
        grad_columns = jnp.concatenate(
            [
                grad_window[
                    1 - off_x : 1 - off_x + EDGE,
                    1 - off_y : 1 - off_y + EDGE,
                    1 - off_z : 1 - off_z + EDGE,
                ].reshape(-1, grad_width)
                for off_x, off_y, off_z in OFFSETS
            ],
            axis=1,
        )
        weight_acc = weight_acc + lax.dot_general(
            feat_columns, grad_centre, (((0,), (0,)), ((), ())), preferred_element_type=jnp.float32
        )
        block_grad = jnp.dot(
            grad_columns, weight_matrix, preferred_element_type=jnp.float32
        ).reshape(EDGE, EDGE, EDGE, out_width)
        data_acc = lax.dynamic_update_slice(
            data_acc, block_grad, (anchor_x, anchor_y, anchor_z, zero_index)
        )
        return (data_acc, weight_acc)

    data_init = jnp.zeros((span_xy, span_xy, span_z, out_width), jnp.float32)
    weight_init = jnp.zeros((27 * cin_total, cout_half), jnp.float32)
    data_acc, weight_acc = lax.fori_loop(0, live_count, visit_block, (data_init, weight_init))
    data_grad = (data_acc * cell_mask).reshape(cells, out_width)
    data_grad = lax.psum_scatter(data_grad, "chan", scatter_dimension=1, tiled=True)
    weight_grad = lax.psum_scatter(weight_acc, "space", scatter_dimension=0, tiled=True) * (
        1.0 / math.sqrt(cells * device_total)
    )
    return (data_grad.astype(jnp.bfloat16), weight_grad)


def solution(mesh):
    placed = (
        P("space", None),
        P("space", "chan"),
        P(None, None, "chan"),
        P("space"),
        P("space", None),
        P("space"),
    )
    return jax.shard_map(
        body,
        mesh=mesh,
        in_specs=placed,
        out_specs=(P("space", "chan"), P("space", "chan")),
        check_vma=False,
    )
```

profile of v0, /device:TPU:0, one launch (start us, length us, event | category | flops | bytes accessed | tf_op | source)
XLA Modules:
  0.0 429.2 jit_solution(17219824723073720689)
XLA Ops:
  7.2 0.7 select_reduce_fusion
  9.0 0.7 convert_element_type.54
  9.9 0.7 fusion
  10.5 1.7 broadcast_multiply_fusion.2
  12.3 0.6 fusion.2
  12.9 1.3 collective-permute-start.1
  14.2 0.7 broadcast_multiply_fusion.1
  14.9 0.7 fusion.1
  15.6 1.3 collective-permute-start.7
  16.9 6.6 %collective-permute-start.6 = (bf16[1,16,16,256]{3,2,1,0:T(8,128)(2,1)}, bf16[1,16,16,256]{3,2,1,0:T(8,128)(2,1)}, u32[]{:S(2)}, u32[]{:S(2)}) collective-permute-start(bf16[1,16,16,256]{3,2,1,0:T(8,128)(2,1)} %get-tuple-element.220), channel_id=1, source_target_pairs={{0,16},{2,18},{4,20},{6,22},{8,24},{10,26},{12,28},{14,30},{1,17},... | collective-permute-start | bytes 393224 | tf_op jit(solution)/shard_map/ppermute | solution.py:21
  23.5 1.9 collective-permute-start
  25.4 3.8 copy.9
  29.3 0.8 broadcast_multiply_fusion.15
  30.2 1.3 collective-permute-start.3
  31.5 6.2 %collective-permute-start.2 = (bf16[18,1,16,128]{3,2,1,0:T(8,128)(2,1)S(1)}, bf16[18,1,16,128]{3,2,1,0:T(8,128)(2,1)S(1)}, u32[]{:S(2)}, u32[]{:S(2)}) collective-permute-start(bf16[18,1,16,128]{3,2,1,0:T(8,128)(2,1)S(1)} %get-tuple-element.224), channel_id=1, source_target_pairs={{0,8},{2,10},{4,12},{6,14},{8,16},{10,18},{12,20},{14,22},{16,24},... | collective-permute-start | bytes 221192 | tf_op jit(solution)/shard_map/ppermute | solution.py:21
  37.8 0.9 broadcast_multiply_fusion.11
  38.7 1.0 collective-permute-done.2
  40.0 1.3 collective-permute-start.4
  41.3 1.3 collective-permute-start.9
  42.6 5.5 %collective-permute-start.8 = (bf16[18,1,16,256]{3,2,1,0:T(8,128)(2,1)S(1)}, bf16[18,1,16,256]{3,2,1,0:T(8,128)(2,1)S(1)}, u32[]{:S(2)}, u32[]{:S(2)}) collective-permute-start(bf16[18,1,16,256]{3,2,1,0:T(8,128)(2,1)S(1)} %get-tuple-element.218), channel_id=1, source_target_pairs={{0,8},{2,10},{4,12},{6,14},{8,16},{10,18},{12,20},{14,22},{16,24},... | collective-permute-start | bytes 442376 | tf_op jit(solution)/shard_map/ppermute | solution.py:21
  48.2 1.3 collective-permute-start.5
  49.7 3.3 collective-permute-done.5
  53.2 0.7 pad_maximum_fusion.6
  53.9 5.8 %collective-permute-start.10 = (bf16[18,18,1,256]{3,2,1,0:T(2,128)(2,1)S(1)}, bf16[18,18,1,256]{3,2,1,0:T(2,128)(2,1)S(1)}, u32[]{:S(2)}, u32[]{:S(2)}) collective-permute-start(bf16[18,18,1,256]{3,2,1,0:T(2,128)(2,1)S(1)} %get-tuple-element.216), channel_id=1, source_target_pairs={{0,2},{2,4},{4,6},{6,8},{8,10},{10,12},{12,14},{14,16},{16,18},{18... | collective-permute-start | bytes 497672 | tf_op jit(solution)/shard_map/ppermute | solution.py:21
  59.7 2.9 pad_maximum_fusion.1
  62.7 1.3 collective-permute-start.11
  64.3 1.9 collective-permute-done.11
  66.5 4.3 %pad_maximum_fusion = bf16[18,18,18,256]{3,2,1,0:T(8,128)(2,1)} fusion(bf16[18,18,1,256]{3,2,1,0:T(2,128)(2,1)S(1)} %broadcast_multiply_fusion.3, bf16[18,1,16,256]{3,2,1,0:T(8,128)(2,1)S(1)} %broadcast_multiply_fusion.8, bf16[1,16,16,256]{3,2,1,0:T(8,128)(2,1)S(1)} %broadcast_multiply_fusion.10, bf16[16,16,16,256]{3,2,1,0:T(8,128)(2,1)S(1)} %broadcast_multiply_fusion.1, ...), kind=kLoop, calls=%fused_computation.110 | loop fusion | flops 20901888 | bytes 5971968 | tf_op jit(solution)/shard_map/concatenate | solution.py:42
  70.9 2.5 broadcast_in_dim.26
  73.6 107.7 %while.15 = (s32[]{:T(128)}, f32[16,16,16,256]{3,2,1,0:T(8,128)}, f32[6912,128]{1,0:T(8,128)S(1)}, s32[]{:T(128)}, s32[8]{0:T(128)S(1)}, /*index=5*/bf16[18,18,1...) while((s32[]{:T(128)}, f32[16,16,16,256]{3,2,1,0:T(8,128)}, ...), condition=%wide.region_2.3_spmd, body=%wide.region_1.2_spmd.sunk | while | flops 1812824064 | bytes 76686344 | solution.py:142
  74.5 0.6 dynamic_slice.22
  77.7 11.0 %constant_dynamic-slice_fusion.57 = (bf16[8,8,8,256]{3,2,1,0:T(8,128)(2,1)S(1)}, bf16[8,8,8,256]{3,2,1,0:T(8,128)(2,1)S(1)}, bf16[8,8,8,256]{3,2,1,0:T(8,128)(2,...) fusion(bf16[18,18,18,256]{3,2,1,0:T(8,128)(2,1)} %get-tuple-ele, ...), kind=kLoop, calls=%fused_computation.107.clone.1 | loop fusion | bytes 14155812 | tf_op jit(solution)/shard_map/while/body/slice | solution.py:109
  89.5 1.1 copy-done.1
  90.6 1.4 constant_dynamic-slice_fusion.56
  92.1 2.7 convolution_add_fusion.2
  96.3 1.9 fusion.17
  98.2 1.9 constant_dynamic-update-slice_fusion.137
  100.8 0.6 dynamic_slice.22
  104.0 11.4 %constant_dynamic-slice_fusion.57 = (bf16[8,8,8,256]{3,2,1,0:T(8,128)(2,1)S(1)}, bf16[8,8,8,256]{3,2,1,0:T(8,128)(2,1)S(1)}, bf16[8,8,8,256]{3,2,1,0:T(8,128)(2,...) fusion(bf16[18,18,18,256]{3,2,1,0:T(8,128)(2,1)} %get-tuple-ele, ...), kind=kLoop, calls=%fused_computation.107.clone.1 | loop fusion | bytes 14155812 | tf_op jit(solution)/shard_map/while/body/slice | solution.py:109
  116.2 1.1 copy-done.1
  117.3 1.4 constant_dynamic-slice_fusion.56
  118.8 2.7 convolution_add_fusion.2
  123.0 1.9 fusion.17
  124.9 1.9 constant_dynamic-update-slice_fusion.137
  127.5 0.6 dynamic_slice.22
  130.8 11.3 %constant_dynamic-slice_fusion.57 = (bf16[8,8,8,256]{3,2,1,0:T(8,128)(2,1)S(1)}, bf16[8,8,8,256]{3,2,1,0:T(8,128)(2,1)S(1)}, bf16[8,8,8,256]{3,2,1,0:T(8,128)(2,...) fusion(bf16[18,18,18,256]{3,2,1,0:T(8,128)(2,1)} %get-tuple-ele, ...), kind=kLoop, calls=%fused_computation.107.clone.1 | loop fusion | bytes 14155812 | tf_op jit(solution)/shard_map/while/body/slice | solution.py:109
  142.8 1.1 copy-done.1
  143.9 1.4 constant_dynamic-slice_fusion.56
  145.4 2.7 convolution_add_fusion.2
  149.6 1.9 fusion.17
  151.5 1.9 constant_dynamic-update-slice_fusion.137
  154.0 0.6 dynamic_slice.22
  157.3 12.1 %constant_dynamic-slice_fusion.57 = (bf16[8,8,8,256]{3,2,1,0:T(8,128)(2,1)S(1)}, bf16[8,8,8,256]{3,2,1,0:T(8,128)(2,1)S(1)}, bf16[8,8,8,256]{3,2,1,0:T(8,128)(2,...) fusion(bf16[18,18,18,256]{3,2,1,0:T(8,128)(2,1)} %get-tuple-ele, ...), kind=kLoop, calls=%fused_computation.107.clone.1 | loop fusion | bytes 14155812 | tf_op jit(solution)/shard_map/while/body/slice | solution.py:109
  170.1 1.1 copy-done.1
  171.3 1.4 constant_dynamic-slice_fusion.56
  172.7 2.7 convolution_add_fusion.2
  176.9 1.9 fusion.17
  178.8 1.9 constant_dynamic-update-slice_fusion.137
  181.4 1.7 copy-done
  183.2 3.9 broadcast_multiply_fusion
  187.1 177.0 %reduce-scatter.5.cloned.1.call-done = f32[432,128]{1,0:T(8,128)} async-done(((f32[6912,128]{1,0:T(8,128)}), f32[432,128]{1,0:T(8,128)}) %reduce-scatter.5.cloned.1.call-update) | async-done | bytes 221200 | tf_op jit(solution)/shard_map/reduce_scatter | solution.py:145
  364.2 1.6 broadcast_multiply_fusion.5
  365.8 53.9 %reduce-scatter.3.cloned.1.call-done = f32[4096,128]{1,0:T(8,128)} async-done(((f32[4096,256]{1,0:T(8,128)}), f32[4096,128]{1,0:T(8,128)}) %reduce-scatter.3.cloned.1.call-update) | async-done | bytes 2097168 | tf_op jit(solution)/shard_map/reduce_scatter | solution.py:144
  419.7 2.7 convert_element_type.63
  (265 shorter events, 9.5 us)
Async XLA Ops:
  7.2 357.0 %reduce-scatter.5.cloned.1.call-start = ((), (), s32[]{:S(2)}) async-start(), calls=%async_computation.3 | async-start | bytes 3760128 | tf_op jit(solution)/shard_map/reduce_scatter | solution.py:145
  9.8 4.4 %copy-start.2 = (bf16[4096,256]{1,0:T(8,128)(2,1)S(1)}, bf16[4096,256]{1,0:T(8,128)(2,1)}, u32[]{:S(2)}) copy-start(bf16[4096,256]{1,0:T(8,128)(2,1)} %param.8) | copy-start | bytes 6291460
  12.9 16.3 %collective-permute-start.1 = (bf16[1,16,16,128]{3,2,1,0:T(8,128)(2,1)S(1)}, bf16[1,16,16,128]{3,2,1,0:T(8,128)(2,1)S(1)}, u32[]{:S(2)}, u32[]{:S(2)}) collective-permute-start(bf16[1,16,16,128]{3,2,1,0:T(8,128)(2,1)S(1)} %get-tuple-element.227), channel_id=1, source_target_pairs={{16,0},{18,2},{20,4},{22,6},{24,8},{26,10},{28,12},{30,14},{17,1},... | collective-permute-start | bytes 196616 | tf_op jit(solution)/shard_map/ppermute | solution.py:21
  15.6 22.1 %collective-permute-start.7 = (bf16[1,16,16,256]{3,2,1,0:T(8,128)(2,1)S(1)}, bf16[1,16,16,256]{3,2,1,0:T(8,128)(2,1)S(1)}, u32[]{:S(2)}, u32[]{:S(2)}) collective-permute-start(bf16[1,16,16,256]{3,2,1,0:T(8,128)(2,1)S(1)} %get-tuple-element.221), channel_id=1, source_target_pairs={{16,0},{18,2},{20,4},{22,6},{24,8},{26,10},{28,12},{30,14},{17,1},... | collective-permute-start | bytes 393224 | tf_op jit(solution)/shard_map/ppermute | solution.py:21
  16.9 20.8 %collective-permute-start.6 = (bf16[1,16,16,256]{3,2,1,0:T(8,128)(2,1)}, bf16[1,16,16,256]{3,2,1,0:T(8,128)(2,1)}, u32[]{:S(2)}, u32[]{:S(2)}) collective-permute-start(bf16[1,16,16,256]{3,2,1,0:T(8,128)(2,1)} %get-tuple-element.220), channel_id=1, source_target_pairs={{0,16},{2,18},{4,20},{6,22},{8,24},{10,26},{12,28},{14,30},{1,17},... | collective-permute-start | bytes 393224 | tf_op jit(solution)/shard_map/ppermute | solution.py:21
  23.5 5.8 %collective-permute-start = (bf16[1,16,16,128]{3,2,1,0:T(8,128)(2,1)}, bf16[1,16,16,128]{3,2,1,0:T(8,128)(2,1)}, u32[]{:S(2)}, u32[]{:S(2)}) collective-permute-start(bf16[1,16,16,128]{3,2,1,0:T(8,128)(2,1)} %get-tuple-element.226), channel_id=1, source_target_pairs={{0,16},{2,18},{4,20},{6,22},{8,24},{10,26},{12,28},{14,30},{1,17},... | collective-permute-start | bytes 196616 | tf_op jit(solution)/shard_map/ppermute | solution.py:21
  30.2 8.5 %collective-permute-start.3 = (bf16[18,1,16,128]{3,2,1,0:T(8,128)(2,1)S(1)}, bf16[18,1,16,128]{3,2,1,0:T(8,128)(2,1)S(1)}, u32[]{:S(2)}, u32[]{:S(2)}) collective-permute-start(bf16[18,1,16,128]{3,2,1,0:T(8,128)(2,1)S(1)} %get-tuple-element.225), channel_id=1, source_target_pairs={{8,0},{10,2},{12,4},{14,6},{16,8},{18,10},{20,12},{22,14},{24,16},... | collective-permute-start | bytes 221192 | tf_op jit(solution)/shard_map/ppermute | solution.py:21
  31.5 8.2 %collective-permute-start.2 = (bf16[18,1,16,128]{3,2,1,0:T(8,128)(2,1)S(1)}, bf16[18,1,16,128]{3,2,1,0:T(8,128)(2,1)S(1)}, u32[]{:S(2)}, u32[]{:S(2)}) collective-permute-start(bf16[18,1,16,128]{3,2,1,0:T(8,128)(2,1)S(1)} %get-tuple-element.224), channel_id=1, source_target_pairs={{0,8},{2,10},{4,12},{6,14},{8,16},{10,18},{12,20},{14,22},{16,24},... | collective-permute-start | bytes 221192 | tf_op jit(solution)/shard_map/ppermute | solution.py:21
  40.0 9.5 %collective-permute-start.4 = (bf16[18,18,1,128]{3,2,1,0:T(2,128)(2,1)S(1)}, bf16[18,18,1,128]{3,2,1,0:T(2,128)(2,1)S(1)}, u32[]{:S(2)}, u32[]{:S(2)}) collective-permute-start(bf16[18,18,1,128]{3,2,1,0:T(2,128)(2,1)S(1)} %get-tuple-element.222), channel_id=1, source_target_pairs={{0,2},{2,4},{4,6},{6,8},{8,10},{10,12},{12,14},{14,16},{16,18},{18... | collective-permute-start | bytes 248840 | tf_op jit(solution)/shard_map/ppermute | solution.py:21
  41.3 11.8 %collective-permute-start.9 = (bf16[18,1,16,256]{3,2,1,0:T(8,128)(2,1)S(1)}, bf16[18,1,16,256]{3,2,1,0:T(8,128)(2,1)S(1)}, u32[]{:S(2)}, u32[]{:S(2)}) collective-permute-start(bf16[18,1,16,256]{3,2,1,0:T(8,128)(2,1)S(1)} %get-tuple-element.219), channel_id=1, source_target_pairs={{8,0},{10,2},{12,4},{14,6},{16,8},{18,10},{20,12},{22,14},{24,16},... | collective-permute-start | bytes 442376 | tf_op jit(solution)/shard_map/ppermute | solution.py:21
  42.6 10.5 %collective-permute-start.8 = (bf16[18,1,16,256]{3,2,1,0:T(8,128)(2,1)S(1)}, bf16[18,1,16,256]{3,2,1,0:T(8,128)(2,1)S(1)}, u32[]{:S(2)}, u32[]{:S(2)}) collective-permute-start(bf16[18,1,16,256]{3,2,1,0:T(8,128)(2,1)S(1)} %get-tuple-element.218), channel_id=1, source_target_pairs={{0,8},{2,10},{4,12},{6,14},{8,16},{10,18},{12,20},{14,22},{16,24},... | collective-permute-start | bytes 442376 | tf_op jit(solution)/shard_map/ppermute | solution.py:21
  48.2 4.8 %collective-permute-start.5 = (bf16[18,18,1,128]{3,2,1,0:T(2,128)(2,1)S(1)}, bf16[18,18,1,128]{3,2,1,0:T(2,128)(2,1)S(1)}, u32[]{:S(2)}, u32[]{:S(2)}) collective-permute-start(bf16[18,18,1,128]{3,2,1,0:T(2,128)(2,1)S(1)} %get-tuple-element.223), channel_id=1, source_target_pairs={{2,0},{4,2},{6,4},{8,6},{10,8},{12,10},{14,12},{16,14},{18,16},{20... | collective-permute-start | bytes 248840 | tf_op jit(solution)/shard_map/ppermute | solution.py:21
  53.9 10.0 %collective-permute-start.10 = (bf16[18,18,1,256]{3,2,1,0:T(2,128)(2,1)S(1)}, bf16[18,18,1,256]{3,2,1,0:T(2,128)(2,1)S(1)}, u32[]{:S(2)}, u32[]{:S(2)}) collective-permute-start(bf16[18,18,1,256]{3,2,1,0:T(2,128)(2,1)S(1)} %get-tuple-element.216), channel_id=1, source_target_pairs={{0,2},{2,4},{4,6},{6,8},{8,10},{10,12},{12,14},{14,16},{16,18},{18... | collective-permute-start | bytes 497672 | tf_op jit(solution)/shard_map/ppermute | solution.py:21
  62.7 3.5 collective-permute-start.11
  70.9 2.8 copy-start.4
  89.1 1.6 copy-start.1
  94.8 1.5 copy-start.3
  115.8 1.6 copy-start.1
  121.5 1.5 copy-start.3
  142.3 1.6 copy-start.1
  148.1 1.5 copy-start.3
  169.7 1.6 copy-start.1
  175.4 1.5 copy-start.3
  181.4 1.8 copy-start
  183.2 236.6 %reduce-scatter.3.cloned.1.call-start = ((), (), s32[]{:S(2)}) async-start(), calls=%async_computation.2 | async-start | bytes 6291456 | tf_op jit(solution)/shard_map/reduce_scatter | solution.py:144
Sparse Core Ops, SparseCore 0:
  183.3 180.8 reduce-scatter.4
  366.4 53.2 reduce-scatter.2
where the time goes:
time: 433 us; the launch traced here: 429 us
  waiting for transfers between devices  237 us (55%)
  local copies, waits for them, and re-layouts  83.4 us (19%)
  starting transfers between devices  35.2 us (8%)
  other arithmetic  24 us (6%)
  matrix products  18.5 us (4%)
  loops' own time  16 us (4%)
  between operations  15 us (3%)
    reduce_scatter x1, waiting for transfers between devices, body(): lax.psum_scatter(weight_acc, 'space', scatter_dimension=0, tiled=True)  177 us
    reduce_scatter x1, waiting for transfers between devices, body(): lax.psum_scatter(data_grad, 'chan', scatter_dimension=1, tiled=True)  53.9 us
    slice x4, local copies, waits for them, and re-layouts, visit_block(): feat_window[1 + off_x:1 + off_x + EDGE, 1 + off_y:1 + off_y + EDGE, 1 + o...  45.7 us
    ppermute x12, starting transfers between devices, shifted(): return lax.ppermute(block, axis, route)  35.1 us
    another operation x1, loops' own time, body(): lax.fori_loop(0, live_count, visit_block, (data_init, weight_init))  16 us
    while x224, local copies, waits for them, and re-layouts  11.5 us
    dot_general x4, matrix products, visit_block(): lax.dot_general(feat_columns, grad_centre, (((0,), (0,)), ((), ())), pref...  10.9 us
  transfers between devices with their start and end apart: 14, of which 5 were waited for; matrix products, arithmetic and copies ran while one was open for 4% of the time, Pallas kernels for 0%

commit v1 on v0

v1 whole, which is shorter than its diff:
```python
import functools
import math

import jax
import jax.numpy as jnp
from jax import lax
from jax.experimental import pallas as pl
from jax.experimental.pallas import tpu as pltpu
from jax.sharding import PartitionSpec as P

EDGE = 8
LAYERZ = 2
NBLK = 8
SPAN = 2 * EDGE
PLANE = SPAN * SPAN
HALF = 128
BF = jnp.bfloat16
F32 = jnp.float32

SHIFTS = [(a, b) for a in (-1, 0, 1) for b in (-1, 0, 1)]
PAIRS = [(0, 1), (2, 3), (4, 5), (6, 7), (8,)]


def locate_side(device_total):
    plane_side = 1
    for candidate in range(1, 33):
        if 2 * candidate**3 == device_total:
            plane_side = candidate
    return plane_side


def prep_kernel(feat_ref, mask_ref, f_ref, fz_ref):
    lane = lax.broadcasted_iota(jnp.int32, (1, PLANE), 1) % SPAN
    keep_low = (lane != SPAN - 1).astype(F32)
    keep_high = (lane != 0).astype(F32)

    def plane(x, _):
        rows = pl.ds(pl.multiple_of(x * PLANE, PLANE), PLANE)
        block = feat_ref[rows, :].astype(F32).T * mask_ref[pl.ds(x, 1), :]
        cols = pl.ds(pl.multiple_of(x * PLANE, PLANE), PLANE)
        cin = block.shape[0]
        f_ref[0:cin, cols] = (pltpu.roll(block, 1, 1) * keep_high).astype(BF)
        f_ref[cin : 2 * cin, cols] = block.astype(BF)
        f_ref[2 * cin :, cols] = (pltpu.roll(block, PLANE - 1, 1) * keep_low).astype(BF)
        return 0

    lax.fori_loop(0, SPAN, plane, 0)


def prep(features, mask_rows):
    cells, cin = features.shape
    return pl.pallas_call(
        lambda a, m, f: prep_kernel(a, m, f, None),
        out_shape=jax.ShapeDtypeStruct((3 * cin, cells), BF),
        compiler_params=pltpu.CompilerParams(vmem_limit_bytes=56 << 20),
        cost_estimate=pl.CostEstimate(flops=0, bytes_accessed=cells * cin * 8, transcendentals=0),
        name="prep",
    )(features, mask_rows)


def weight_kernel(f_ref, fz_ref, gp_ref, zp_ref, out_ref, *, scale):
    cin = out_ref.shape[1]

    def source(shift):
        a, b = SHIFTS[shift]
        block = gp_ref[1 - a : 1 - a + SPAN, 1 - b : 1 - b + SPAN]
        return block.reshape(SPAN * PLANE, HALF)

    def face(side, shift):
        a, b = SHIFTS[shift]
        return zp_ref[side, b + 1, 1 - a : 1 - a + SPAN].reshape(PLANE, HALF)

    for pair in PAIRS:
        right = jnp.concatenate([source(s) for s in pair], axis=1)
        acc = jnp.dot(f_ref[...], right, preferred_element_type=F32)
        low = jnp.concatenate([face(0, s) for s in pair], axis=1)
        high = jnp.concatenate([face(1, s) for s in pair], axis=1)
        parts = [
            acc[0:cin] + jnp.dot(fz_ref[1], high, preferred_element_type=F32),
            acc[cin : 2 * cin],
            acc[2 * cin :] + jnp.dot(fz_ref[0], low, preferred_element_type=F32),
        ]
        for c in range(3):
            for k, s in enumerate(pair):
                out_ref[3 * s + c] = parts[c][:, HALF * k : HALF * (k + 1)] * scale


def weight_grad_local(f_all, fz, gp, zp, scale):
    cin = f_all.shape[0] // 3
    return pl.pallas_call(
        functools.partial(weight_kernel, scale=scale),
        out_shape=jax.ShapeDtypeStruct((27, cin, HALF), F32),
        compiler_params=pltpu.CompilerParams(vmem_limit_bytes=60 << 20),
        cost_estimate=pl.CostEstimate(
            flops=2 * 27 * cin * HALF * SPAN * PLANE, bytes_accessed=12 << 20, transcendentals=0
        ),
        name="weight_grad",
    )(f_all, fz, gp, zp)


def data_kernel(ga_ref, gb_ref, za_ref, zb_ref, wa_ref, wb_ref, mask_ref, out_ref, wt_ref, h_ref):
    for s in range(9):
        for half, ref in enumerate((wa_ref, wb_ref)):
            for c in range(3):
                tile = ref[3 * s + c].astype(F32).T.astype(BF)
                row = (2 * s + half) * HALF
                wt_ref[row : row + HALF, c * HALF : (c + 1) * HALF] = tile

    for side, c in ((0, 2), (1, 0)):
        cols = []
        for s in range(9):
            a, b = SHIFTS[s]
            for ref in (za_ref, zb_ref):
                cols.append(ref[side, b + 1, 1 - a : 1 - a + SPAN].reshape(PLANE, HALF))
        h_ref[side] = jnp.dot(
            jnp.concatenate(cols, axis=1),
            wt_ref[:, c * HALF : (c + 1) * HALF],
            preferred_element_type=F32,
        ).reshape(SPAN, SPAN, HALF)

    zpos = lax.broadcasted_iota(jnp.int32, (SPAN, SPAN, HALF), 1)

    def plane(x, _):
        cols = []
        for s in range(9):
            a, b = SHIFTS[s]
            for ref in (ga_ref, gb_ref):
                block = ref[pl.ds(x + 1 - a, 1), 1 - b : 1 - b + SPAN]
                cols.append(block.reshape(PLANE, HALF))
        prod = jnp.dot(
            jnp.concatenate(cols, axis=1), wt_ref[...], preferred_element_type=F32
        )
        down = pltpu.roll(prod[:, 0:HALF], PLANE - 1, 0).reshape(SPAN, SPAN, HALF)
        mid = prod[:, HALF : 2 * HALF].reshape(SPAN, SPAN, HALF)
        up = pltpu.roll(prod[:, 2 * HALF :], 1, 0).reshape(SPAN, SPAN, HALF)
        low = h_ref[0, pl.ds(x, 1)].reshape(SPAN, 1, HALF)
        high = h_ref[1, pl.ds(x, 1)].reshape(SPAN, 1, HALF)
        total = mid + jnp.where(zpos == 0, low, up) + jnp.where(zpos == SPAN - 1, high, down)
        keep = jnp.broadcast_to(mask_ref[pl.ds(x, 1), :], (8, PLANE)).T[:, 0:1]
        rows = pl.ds(pl.multiple_of(x * PLANE, PLANE), PLANE)
        out_ref[rows, :] = (total.reshape(PLANE, HALF) * keep).astype(BF)
        return 0

    lax.fori_loop(0, SPAN, plane, 0)


def data_grad_local(ga, gb, za, zb, wa, wb, mask_rows):
    return pl.pallas_call(
        data_kernel,
        out_shape=jax.ShapeDtypeStruct((SPAN * PLANE, HALF), BF),
        scratch_shapes=[
            pltpu.VMEM((18 * HALF, 3 * HALF), BF),
            pltpu.VMEM((2, SPAN, SPAN, HALF), F32),
        ],
        compiler_params=pltpu.CompilerParams(vmem_limit_bytes=56 << 20),
        cost_estimate=pl.CostEstimate(
            flops=2 * 27 * 2 * HALF * HALF * SPAN * PLANE, bytes_accessed=8 << 20, transcendentals=0
        ),
        name="data_grad",
    )(ga, gb, za, zb, wa, wb, mask_rows)


def extend(block, dim, stride, coords, side):
    total = lax.axis_size("space")
    length = block.shape[dim]
    first = lax.slice_in_dim(block, 0, 1, axis=dim)
    last = lax.slice_in_dim(block, length - 1, length, axis=dim)
    up = [(i, i + stride) for i in range(total) if coords(i) < side - 1]
    down = [(i + stride, i) for i, _ in [(j, 0) for j in range(total) if coords(j) < side - 1]]
    below = lax.ppermute(last, "space", up)
    above = lax.ppermute(first, "space", down)
    return jnp.concatenate([below, block, above], axis=dim)


def halo(grad, plane_side, depth):
    low = lax.slice_in_dim(grad, 0, 1, axis=2)
    block = extend(grad, 2, 1, lambda i: i % depth, depth)
    block = extend(block, 1, depth, lambda i: i // depth % plane_side, plane_side)
    block = extend(block, 0, depth * plane_side, lambda i: i // (depth * plane_side), plane_side)
    return block


def split_z(block):
    inner = block[:, :, 1 : 1 + SPAN]
    faces = jnp.stack([block[:, :, 0], block[:, :, SPAN + 1]])
    turned = jnp.stack([faces[:, :, 1 - b : 1 - b + SPAN] for b in (-1, 0, 1)], axis=1)
    return inner, turned


def swap_bit(block, bit, total):
    return lax.ppermute(block, "space", [(i, i ^ (1 << bit)) for i in range(total)])


def halve(block, axis, bit, index, total):
    mine = index // (1 << bit) % 2
    send = lax.dynamic_index_in_dim(block, 1 - mine, axis, keepdims=False)
    keep = lax.dynamic_index_in_dim(block, mine, axis, keepdims=False)
    return keep + swap_bit(send, bit, total)


def scatter_sum(partial, index, total):
    bits = total.bit_length() - 1
    rows = partial.shape[0] // total
    block = partial.reshape((2,) * bits + (rows, HALF))
    block = halve(block, bits - 1, 0, index, total)
    cut = rows // 2
    left = list(range(1, bits))
    first, second = block[..., :cut, :], block[..., cut:, :]
    have = sorted(left, reverse=True)
    for bit in left:
        first = halve(first, have.index(bit), bit, index, total)
        have.remove(bit)
    have = sorted(left, reverse=True)
    for bit in left[1:] + left[:1]:
        second = halve(second, have.index(bit), bit, index, total)
        have.remove(bit)
    return jnp.concatenate([first, second], axis=0)


def body(features, grad_out, weights, occupancy, block_list, block_count):
    total = lax.axis_size("space")
    plane_side = locate_side(total)
    depth = 2 * plane_side
    cells, cin = features.shape
    index = lax.axis_index("space")
    column = lax.axis_index("chan")

    block_order = block_list[0]
    live_count = block_count[0]
    slots = jnp.arange(NBLK, dtype=jnp.int32)
    position = jnp.sum(
        jnp.where(block_order[:, None] == slots[None, :], slots[:, None], 0), axis=0
    )
    active = (position < live_count).astype(F32)
    grid = jnp.broadcast_to(
        active.reshape(2, 1, 2, 1, LAYERZ, 1), (2, EDGE, 2, EDGE, LAYERZ, EDGE)
    ).reshape(SPAN, PLANE)
    mask_rows = grid * occupancy.reshape(SPAN, PLANE).astype(F32)
    grad = grad_out.reshape(SPAN, SPAN, SPAN, HALF) * mask_rows.astype(BF).reshape(
        SPAN, SPAN, SPAN, 1
    )

    theirs = lax.dynamic_slice_in_dim(weights, (1 - column) * HALF, HALF, axis=1)
    own_w = lax.dynamic_slice_in_dim(weights, column * HALF, HALF, axis=1)
    swap = [(0, 1), (1, 0)]
    other_w = lax.ppermute(theirs, "chan", swap)

    full = halo(grad, plane_side, depth)
    gp, zp = split_z(full)
    other = lax.ppermute(full, "chan", swap)
    ogp, ozp = split_z(other)

    f_all = prep(features, mask_rows)
    plain = f_all[cin : 2 * cin].reshape(cin, PLANE, SPAN)
    fz = jnp.stack([plain[:, :, 0], plain[:, :, SPAN - 1]])
    scale = 1.0 / math.sqrt(cells * total)
    partial = weight_grad_local(f_all, fz, gp, zp, scale).reshape(27 * cin, HALF)
    weight_out = scatter_sum(partial, index, total)

    data_out = data_grad_local(gp, ogp, zp, ozp, own_w, other_w, mask_rows)
    return data_out, weight_out


def solution(mesh):
    placed = (
        P("space", None),
        P("space", "chan"),
        P(None, None, "chan"),
        P("space"),
        P("space", None),
        P("space"),
    )
    return jax.shard_map(
        body,
        mesh=mesh,
        in_specs=placed,
        out_specs=(P("space", "chan"), P("space", "chan")),
        check_vma=False,
    )
```

time: 433 us -> 151 us (0.35)
  waiting for transfers between devices: 237 us -> 40 us
  local copies, waits for them, and re-layouts: 83.4 us -> 21.9 us
  Pallas kernels: 0 us -> 39.5 us
  matrix products: 18.5 us -> 0 us
  loops' own time: 16 us -> 0 us
  other arithmetic: 24 us -> 10.3 us
  between operations: 15 us -> 1.6 us
    reduce_scatter x2 -> x0, waiting for transfers between devices: 231 us -> none  [the longest x1 177 us: body(): lax.psum_scatter(weight_acc, 'space', scatter_dimension=0, tiled=True)]
    slice x10, local copies, waits for them, and re-layouts: 52.8 us -> 11.2 us  [the longest x4 4.97 us: split_z(): inner = block[:, :, 1:1 + SPAN]]
    pallas_call x0 -> x3, Pallas kernels: none -> 39.5 us  [the longest x1 17.1 us: data_grad_local(): pl.pallas_call(data_kernel, out_shape=jax.ShapeDtypeStruct((SPAN * PLANE,...]
    ppermute x12 -> x15, waiting for transfers between devices: 6.14 us -> 40 us  [the longest x1 20.8 us: body(): other = lax.ppermute(full, 'chan', swap)]
    dot_general x8 -> x0, matrix products: 18.5 us -> none  [the longest x4 10.9 us: visit_block(): lax.dot_general(feat_columns, grad_centre, (((0,), (0,)), ((), ())), pref...]
    another operation x1 -> x0, loops' own time: 16 us -> none  [body(): lax.fori_loop(0, live_count, visit_block, (data_init, weight_init))]
    while x224 -> x0, local copies, waits for them, and re-layouts: 11.5 us -> none
    mul x16 -> x2, other arithmetic: 10.9 us -> 1.32 us  [the longest x1 0.71 us: body(): grad_out.reshape(SPAN, SPAN, SPAN, HALF)]
  transfers between devices with their start and end apart: 14 -> 15, of which waited for: 5 -> 6; matrix products, arithmetic and copies ran while one was open for 4% -> 16% of each run, Pallas kernels for 0% -> 26%
where the time goes in v1:
time: 151 us; the launch traced here: 150 us
  waiting for transfers between devices  40 us (26%)
  Pallas kernels  39.5 us (26%)
  starting transfers between devices  36.9 us (24%)
  local copies, waits for them, and re-layouts  21.9 us (15%)
  other arithmetic  10.3 us (7%)
  between operations  1.6 us (1%)
    ppermute x1, waiting for transfers between devices, body(): other = lax.ppermute(full, 'chan', swap)  20.8 us
    pallas_call x1, Pallas kernels, data_grad_local(): pl.pallas_call(data_kernel, out_shape=jax.ShapeDtypeStruct((SPAN * PLANE,...  17.1 us
    ppermute x7, starting transfers between devices, swap_bit(): lax.ppermute(block, 'space', [(i, i ^ 1 << bit) for i in range(total)])  16.2 us
    ppermute x3, starting transfers between devices, extend(): below = lax.ppermute(last, 'space', up)  14.5 us
    pallas_call x1, Pallas kernels, weight_grad_local(): pl.pallas_call(functools.partial(weight_kernel, scale=scale), out_shape=j...  13.8 us
    ppermute x7, waiting for transfers between devices, swap_bit(): lax.ppermute(block, 'space', [(i, i ^ 1 << bit) for i in range(total)])  9.36 us
    pallas_call x1, Pallas kernels, prep(): pl.pallas_call(lambda a, m, f: prep_kernel(a, m, f, None), out_shape=jax....  8.7 us
    ppermute x1, waiting for transfers between devices, body(): other_w = lax.ppermute(theirs, 'chan', swap)  6.05 us
  transfers between devices with their start and end apart: 15, of which 6 were waited for; matrix products, arithmetic and copies ran while one was open for 16% of the time, Pallas kernels for 26%

profile of v1, /device:TPU:0, one launch (start us, length us, event | category | flops | bytes accessed | tf_op | source)
XLA Modules:
  0.0 150.3 jit_solution(10195284034067641375)
XLA Ops:
  0.6 0.8 select_reduce_fusion
  2.1 0.1 reshape.46
  2.2 0.1 broadcast_in_dim.21
  2.4 0.2 reshape.43
  2.5 0.7 convert_element_type.32
  3.3 0.1 convert_element_type.33
  3.4 0.1 copy.28
  3.5 0.7 copy_multiply_fusion
  4.3 1.3 collective-permute-start.1
  5.6 3.0 %collective-permute-start = (bf16[16,16,1,128]{3,1,0,2:T(8,128)(2,1)S(1)}, bf16[16,16,1,128]{3,1,0,2:T(8,128)(2,1)S(1)}, u32[]{:S(2)}, u32[]{:S(2)}) collective-permute-start(bf16[16,16,1,128]{3,1,0,2:T(8,128)(2,1)S(1)} %get-tuple-element.18), channel_id=1, source_target_pairs={{0,2},{2,4},{4,6},{8,10},{10,12},{12,14},{16,18},{18,20},{20,22},{... | collective-permute-start | bytes 196616 | tf_op jit(solution)/shard_map/ppermute | solution.py:170
  8.6 0.4 reshape.44
  9.0 0.6 mul.24.mask_ref.m
  9.6 8.7 %prep.1.f_ref = bf16[768,4096]{1,0:T(8,128)(2,1)} custom-call(bf16[4096,256]{1,0:T(8,128)(2,1)} %a.1, f32[16,256]{1,0:T(8,128)} %mul.24.mask_ref.m), custom_call_target="tpu_custom_call" | custom-call | bytes 8388608 | tf_op jit(solution)/shard_map/prep/pallas_call | solution.py:52
  18.3 1.6 %slice-done = bf16[256,4096]{1,0:T(8,128)(2,1)S(1)} async-done(((bf16[768,4096]{1,0:T(8,128)(2,1)}), bf16[256,4096]{1,0:T(8,128)(2,1)S(1)}, s32[]{:S(2)}) %slice-start) | async-done | bytes 2097176 | tf_op jit(solution)/shard_map/slice | solution.py:254
  19.9 2.5 %copy.35 = bf16[256,4096]{0,1:T(8,128)(2,1)} copy(bf16[256,4096]{1,0:T(8,128)(2,1)S(1)} %slice-done) | data formatting | bytes 4194304 | tf_op jit(solution)/shard_map/slice | solution.py:254
  22.4 0.2 pad_maximum_fusion.9
  22.7 1.3 collective-permute-start.3
  24.0 4.9 %collective-permute-start.2 = (bf16[16,1,18,128]{3,1,0,2:T(2,128)(2,1)S(1)}, bf16[16,1,18,128]{3,1,0,2:T(2,128)(2,1)S(1)}, u32[]{:S(2)}, u32[]{:S(2)}) collective-permute-start(bf16[16,1,18,128]{3,1,0,2:T(2,128)(2,1)S(1)} %get-tuple-element.16), channel_id=1, source_target_pairs={{0,8},{2,10},{4,12},{6,14},{16,24},{18,26},{20,28},{22,30},{1,9},{... | collective-permute-start | bytes 221192 | tf_op jit(solution)/shard_map/ppermute | solution.py:170
  28.9 2.0 %fusion.10 = (bf16[256,256,1]{0,2,1:T(2,128)(2,1)S(1)}, bf16[256,256,1]{0,2,1:T(2,128)(2,1)S(1)}) fusion(bf16[256,256,16]{0,2,1:T(8,128)(2,1)} %bitcast.62), kind=kLoop, calls=%fused_computation.60 | loop fusion | bytes 524288 | tf_op jit(solution)/shard_map/slice | solution.py:255
  30.9 0.1 copy.42
  31.0 0.1 copy.41
  31.2 0.0 collective-permute-done.3
  31.2 1.0 collective-permute-done.2
  32.2 0.1 pad_maximum_fusion.14
  32.3 1.3 collective-permute-start.5
  33.6 6.5 %collective-permute-start.4 = (bf16[1,18,18,128]{3,1,0,2:T(8,128)(2,1)S(1)}, bf16[1,18,18,128]{3,1,0,2:T(8,128)(2,1)S(1)}, u32[]{:S(2)}, u32[]{:S(2)}) collective-permute-start(bf16[1,18,18,128]{3,1,0,2:T(8,128)(2,1)S(1)} %get-tuple-element.14), channel_id=1, source_target_pairs={{0,16},{2,18},{4,20},{6,22},{8,24},{10,26},{12,28},{14,30},{1,17},... | collective-permute-start | bytes 248840 | tf_op jit(solution)/shard_map/ppermute | solution.py:170
  40.2 0.7 pad_maximum_fusion.3.fz_ref
  40.9 2.7 %collective-permute-done.5 = bf16[1,18,18,128]{3,1,0,2:T(8,128)(2,1)S(1)} collective-permute-done((bf16[1,18,18,128]{3,1,0,2:T(8,128)(2,1)S(1)}, bf16[1,18,18,128]{3,1,0,2:T(8,128)(2,1)S(1)}, u32[]{:S(2)}, u32[]{:S(2)}) %collective-permute-start.5) | collective-permute-done | bytes 82976 | tf_op jit(solution)/shard_map/ppermute | solution.py:171
  43.6 0.0 collective-permute-done.4
  43.6 2.7 %pad_maximum_fusion = bf16[18,18,18,128]{3,1,0,2:T(8,128)(2,1)S(1)} fusion(bf16[1,18,18,128]{3,1,0,2:T(8,128)(2,1)S(1)} %collective-permute-done.5, bf16[16,1,18,128]{3,1,0,2:T(2,128)(2,1)S(1)} %collective-permute-done.3, bf16[16,16,1,128]{3,1,0,2:T(8,128)(2,1)S(1)} %collective-permute-done.1, bf16[16,16,16,128]{3,1,0,2:T(8,128)(2,1)S(1)} %copy_multiply_fusion, ...), kind=kLoop, calls=%fused_computation | loop fusion | flops 10450944 | bytes 2985984 | tf_op jit(solution)/shard_map/concatenate | solution.py:172
  46.3 0.3 slice.94
  46.6 2.3 %collective-permute-start.6 = (bf16[18,18,18,128]{3,1,0,2:T(8,128)(2,1)S(1)}, bf16[18,18,18,128]{3,1,0,2:T(8,128)(2,1)}, u32[]{:S(2)}, u32[]{:S(2)}) collective-permute-start(bf16[18,18,18,128]{3,1,0,2:T(8,128)(2,1)S(1)} %pad_maximum_fusion), channel_id=1, source_target_pairs={{0,1},{1,0},{2,3},{3,2},{4,5},{5,4},{6,7},{7,6},{8,9},{9,8},{10,11... | collective-permute-start | bytes 4478984 | tf_op jit(solution)/shard_map/ppermute | solution.py:250
  48.9 1.5 copy.32.ga_ref.gp_ref
  50.4 0.1 fusion.7
  50.5 0.8 pad_maximum_fusion.1.za_ref.zp_ref
  51.3 13.8 %weight_grad.1 = f32[27,256,128]{2,1,0:T(8,128)} custom-call(bf16[768,4096]{1,0:T(8,128)(2,1)} %prep.1.f_ref, bf16[2,256,256]{2,1,0:T(8,128)(2,1)} %pad_maximum_fusion.3.fz_ref, bf16[18,18,16,128]{3,2,1,0:T(8,128)(2,1)} %copy.32.ga_ref.gp_ref, bf16[2,3,18,16,128]{4,3,2,1,0:T(8,128)(2,1)} %pad_maximum_fusion.1.za_ref.zp_ref), custom_call_target="tpu_custom_call" | custom-call | flops 7247757312 | bytes 12582912 | tf_op jit(solution)/shard_map/weight_grad/pallas_call | solution.py:90
  65.0 3.5 %constant_dynamic-slice_fusion.1 = (f32[2,2,2,1,432,128]{5,4,3,2,1,0:T(8,128)}, f32[2,2,2,1,432,128]{5,4,3,2,1,0:T(8,128)S(1)}) fusion(f32[2,2,2,2,432,128]{5,4,3,2,1,0:T(8,128)} %bitcast.61, s32[]{:T(128)S(6)} %select_n.89, s32[]{:T(128)S(6)} %select_n.90), kind=kLoop, calls=%fused_computation.55 | loop fusion | bytes 7077896 | tf_op jit(solution)/shard_map/jit(dynamic_index_in_dim)/dynamic_slice | solution.py:197
  68.5 1.3 copy.46
  69.9 0.0 collective-permute-start.8
  69.9 2.5 %constant_dynamic-slice_fusion.2 = (bf16[27,128,128]{2,1,0:T(8,128)(2,1)S(1)}, bf16[27,128,128]{2,1,0:T(8,128)(2,1)}) fusion(bf16[27,256,128]{2,1,0:T(8,128)(2,1)} %param.8, s32[]{:T(128)S(6)} %select_n.87, s32[]{:T(128)S(6)} %select_n.86), kind=kLoop, calls=%fused_computation.56 | loop fusion | bytes 3538952 | tf_op jit(solution)/shard_map/dynamic_slice | solution.py:243
  72.4 0.0 collective-permute-start.7
  72.4 20.8 %collective-permute-done.6 = bf16[18,18,18,128]{3,1,0,2:T(8,128)(2,1)} collective-permute-done((bf16[18,18,18,128]{3,1,0,2:T(8,128)(2,1)S(1)}, bf16[18,18,18,128]{3,1,0,2:T(8,128)(2,1)}, u32[]{:S(2)}, u32[]{:S(2)}) %collective-permute-start.6) | collective-permute-done | bytes 1493024 | tf_op jit(solution)/shard_map/ppermute | solution.py:250
  93.2 1.8 %slice.95 = bf16[18,18,16,128]{3,1,0,2:T(8,128)(2,1)S(1)} slice(bf16[18,18,18,128]{3,1,0,2:T(8,128)(2,1)} %collective-permute-done.6), slice={[0:18], [0:18], [1:17], [0:128]} | slice | bytes 2654208 | tf_op jit(solution)/shard_map/slice | solution.py:184
  95.0 1.4 copy.33.gb_ref
  96.4 1.1 slice_bitcast_fusion.1
  97.5 0.1 fusion.3
  97.6 0.1 pad_maximum_fusion.2
  97.7 0.9 copy.34.zb_ref
  98.5 0.0 collective-permute-done.8
  98.6 1.8 %bitcast_add_fusion = f32[2,2,2,432,128]{4,3,1,0,2:T(8,128)S(1)} fusion(f32[2,2,2,432,128]{4,3,1,0,2:T(8,128)} %collective-permute-done.8, f32[2,2,2,1,432,128]{5,4,3,2,1,0:T(8,128)S(1)} %copy-done), kind=kLoop, calls=%fused_computation.1 | loop fusion | flops 442368 | bytes 5308416 | tf_op jit(solution)/shard_map/add | solution.py:198
  100.3 0.1 fusion.11
  100.5 2.6 %collective-permute-start.12 = (f32[2,2,216,128]{3,2,0,1:T(8,128)S(1)}, f32[2,2,216,128]{3,2,0,1:T(8,128)S(1)}, u32[]{:S(2)}, u32[]{:S(2)}) collective-permute-start(f32[2,2,216,128]{3,2,0,1:T(8,128)S(1)} %dynamic-slice_bitcast_fusion), channel_id=1, source_target_pairs={{0,8},{2,10},{4,12},{6,14},{8,0},{10,2},{12,4},{14,6},{16,24},{18,... | collective-permute-start | bytes 1327112 | tf_op jit(solution)/shard_map/ppermute | solution.py:191
  103.1 0.1 collective-permute-start.9
  103.2 6.1 %collective-permute-done.7.wb_ref = bf16[27,128,128]{2,1,0:T(8,128)(2,1)} collective-permute-done((bf16[27,128,128]{2,1,0:T(8,128)(2,1)S(1)}, bf16[27,128,128]{2,1,0:T(8,128)(2,1)}, u32[]{:S(2)}, u32[]{:S(2)}) %collective-permute-start.7) | collective-permute-done | bytes 884768 | tf_op jit(solution)/shard_map/ppermute | solution.py:246
  109.2 17.1 %data_grad.1 = bf16[4096,128]{1,0:T(8,128)(2,1)} custom-call(bf16[18,18,16,128]{3,2,1,0:T(8,128)(2,1)} %copy.32.ga_ref.gp_ref, bf16[18,18,16,128]{3,2,1,0:T(8,128)(2,1)} %copy.33.gb_ref, bf16[2,3,18,16,128]{4,3,2,1,0:T(8,128)(2,1)} %pad_maximum_fusion.1.za_ref.zp_ref, bf16[2,3,18,16,128]{4,3,2,1,0:T(8,128)(2,1)} %copy.34.zb_ref, ...), custom_call_target="tpu_custom_call" | custom-call | flops 7247757312 | bytes 8388608 | tf_op jit(solution)/shard_map/data_grad/pallas_call | solution.py:148
  126.3 0.0 collective-permute-done.12
  126.4 3.1 %collective-permute-start.13 = (f32[2,216,128]{2,1,0:T(8,128)S(1)}, f32[2,216,128]{2,1,0:T(8,128)S(1)}, u32[]{:S(2)}, u32[]{:S(2)}) collective-permute-start(f32[2,216,128]{2,1,0:T(8,128)S(1)} %dynamic-slice_bitcast_fusion.2), channel_id=1, source_target_pairs={{0,16},{2,18},{4,20},{6,22},{8,24},{10,26},{12,28},{14,30},{16,0},... | collective-permute-start | bytes 663560 | tf_op jit(solution)/shard_map/ppermute | solution.py:191
  129.6 0.0 collective-permute-done.9
  129.6 5.3 %collective-permute-start.10 = (f32[2,216,128]{2,1,0:T(8,128)S(1)}, f32[2,216,128]{2,1,0:T(8,128)S(1)}, u32[]{:S(2)}, u32[]{:S(2)}) collective-permute-start(f32[2,216,128]{2,1,0:T(8,128)S(1)} %dynamic-slice_bitcast_fusion.3), channel_id=1, source_target_pairs={{0,8},{2,10},{4,12},{6,14},{8,0},{10,2},{12,4},{14,6},{16,24},{18,... | collective-permute-start | bytes 663560 | tf_op jit(solution)/shard_map/ppermute | solution.py:191
  134.9 0.2 collective-permute-start.14
  135.2 4.5 %collective-permute-done.10 = f32[2,216,128]{2,1,0:T(8,128)S(1)} collective-permute-done((f32[2,216,128]{2,1,0:T(8,128)S(1)}, f32[2,216,128]{2,1,0:T(8,128)S(1)}, u32[]{:S(2)}, u32[]{:S(2)}) %collective-permute-start.10) | collective-permute-done | bytes 221216 | tf_op jit(solution)/shard_map/ppermute | solution.py:191
  139.7 4.9 %collective-permute-start.11 = (f32[216,128]{1,0:T(8,128)S(1)}, f32[216,128]{1,0:T(8,128)S(1)}, u32[]{:S(2)}, u32[]{:S(2)}) collective-permute-start(f32[216,128]{1,0:T(8,128)S(1)} %dynamic-slice_bitcast_fusion.5), channel_id=1, source_target_pairs={{0,16},{2,18},{4,20},{6,22},{8,24},{10,26},{12,28},{14,30},{16,0},... | collective-permute-start | bytes 331784 | tf_op jit(solution)/shard_map/ppermute | solution.py:191
  144.7 4.8 %collective-permute-done.11 = f32[216,128]{1,0:T(8,128)S(1)} collective-permute-done((f32[216,128]{1,0:T(8,128)S(1)}, f32[216,128]{1,0:T(8,128)S(1)}, u32[]{:S(2)}, u32[]{:S(2)}) %collective-permute-start.11) | collective-permute-done | bytes 110624 | tf_op jit(solution)/shard_map/ppermute | solution.py:191
  149.6 0.7 pad_maximum_fusion.4
  (28 shorter events, 0.4 us)
Async XLA Ops:
  0.6 2.9 %copy-start.1 = (bf16[4096,128]{1,0:T(8,128)(2,1)S(1)}, bf16[4096,128]{1,0:T(8,128)(2,1)}, u32[]{:S(2)}) copy-start(bf16[4096,128]{1,0:T(8,128)(2,1)} %param.7) | copy-start | bytes 3145732
  4.3 18.1 %collective-permute-start.1 = (bf16[16,16,1,128]{3,1,0,2:T(8,128)(2,1)S(1)}, bf16[16,16,1,128]{3,1,0,2:T(8,128)(2,1)S(1)}, u32[]{:S(2)}, u32[]{:S(2)}) collective-permute-start(bf16[16,16,1,128]{3,1,0,2:T(8,128)(2,1)S(1)} %get-tuple-element.19), channel_id=1, source_target_pairs={{2,0},{4,2},{6,4},{10,8},{12,10},{14,12},{18,16},{20,18},{22,20},{... | collective-permute-start | bytes 196616 | tf_op jit(solution)/shard_map/ppermute | solution.py:171
  5.6 16.8 %collective-permute-start = (bf16[16,16,1,128]{3,1,0,2:T(8,128)(2,1)S(1)}, bf16[16,16,1,128]{3,1,0,2:T(8,128)(2,1)S(1)}, u32[]{:S(2)}, u32[]{:S(2)}) collective-permute-start(bf16[16,16,1,128]{3,1,0,2:T(8,128)(2,1)S(1)} %get-tuple-element.18), channel_id=1, source_target_pairs={{0,2},{2,4},{4,6},{8,10},{10,12},{12,14},{16,18},{18,20},{20,22},{... | collective-permute-start | bytes 196616 | tf_op jit(solution)/shard_map/ppermute | solution.py:170
  18.3 1.6 %slice-start = ((bf16[768,4096]{1,0:T(8,128)(2,1)}), bf16[256,4096]{1,0:T(8,128)(2,1)S(1)}, s32[]{:S(2)}) async-start(bf16[768,4096]{1,0:T(8,128)(2,1)} %prep.1.f_ref), calls=%async_computation | async-start | bytes 4194304 | tf_op jit(solution)/shard_map/slice | solution.py:254
  22.7 8.5 %collective-permute-start.3 = (bf16[16,1,18,128]{3,1,0,2:T(2,128)(2,1)S(1)}, bf16[16,1,18,128]{3,1,0,2:T(2,128)(2,1)S(1)}, u32[]{:S(2)}, u32[]{:S(2)}) collective-permute-start(bf16[16,1,18,128]{3,1,0,2:T(2,128)(2,1)S(1)} %get-tuple-element.17), channel_id=1, source_target_pairs={{8,0},{10,2},{12,4},{14,6},{24,16},{26,18},{28,20},{30,22},{9,1},{... | collective-permute-start | bytes 221192 | tf_op jit(solution)/shard_map/ppermute | solution.py:171
  24.0 8.2 %collective-permute-start.2 = (bf16[16,1,18,128]{3,1,0,2:T(2,128)(2,1)S(1)}, bf16[16,1,18,128]{3,1,0,2:T(2,128)(2,1)S(1)}, u32[]{:S(2)}, u32[]{:S(2)}) collective-permute-start(bf16[16,1,18,128]{3,1,0,2:T(2,128)(2,1)S(1)} %get-tuple-element.16), channel_id=1, source_target_pairs={{0,8},{2,10},{4,12},{6,14},{16,24},{18,26},{20,28},{22,30},{1,9},{... | collective-permute-start | bytes 221192 | tf_op jit(solution)/shard_map/ppermute | solution.py:170
  32.2 11.4 %copy-start.2 = (bf16[16,1,18,128]{3,1,0,2:T(2,128)(2,1)}, bf16[16,1,18,128]{3,1,0,2:T(2,128)(2,1)S(1)}, u32[]{:S(2)}) copy-start(bf16[16,1,18,128]{3,1,0,2:T(2,128)(2,1)S(1)} %collective-permute-done.2) | copy-start | bytes 221188
  32.3 11.3 %collective-permute-start.5 = (bf16[1,18,18,128]{3,1,0,2:T(8,128)(2,1)S(1)}, bf16[1,18,18,128]{3,1,0,2:T(8,128)(2,1)S(1)}, u32[]{:S(2)}, u32[]{:S(2)}) collective-permute-start(bf16[1,18,18,128]{3,1,0,2:T(8,128)(2,1)S(1)} %get-tuple-element.15), channel_id=1, source_target_pairs={{16,0},{18,2},{20,4},{22,6},{24,8},{26,10},{28,12},{30,14},{17,1},... | collective-permute-start | bytes 248840 | tf_op jit(solution)/shard_map/ppermute | solution.py:171
  33.6 10.0 %collective-permute-start.4 = (bf16[1,18,18,128]{3,1,0,2:T(8,128)(2,1)S(1)}, bf16[1,18,18,128]{3,1,0,2:T(8,128)(2,1)S(1)}, u32[]{:S(2)}, u32[]{:S(2)}) collective-permute-start(bf16[1,18,18,128]{3,1,0,2:T(8,128)(2,1)S(1)} %get-tuple-element.14), channel_id=1, source_target_pairs={{0,16},{2,18},{4,20},{6,22},{8,24},{10,26},{12,28},{14,30},{1,17},... | collective-permute-start | bytes 248840 | tf_op jit(solution)/shard_map/ppermute | solution.py:170
  46.6 46.6 %collective-permute-start.6 = (bf16[18,18,18,128]{3,1,0,2:T(8,128)(2,1)S(1)}, bf16[18,18,18,128]{3,1,0,2:T(8,128)(2,1)}, u32[]{:S(2)}, u32[]{:S(2)}) collective-permute-start(bf16[18,18,18,128]{3,1,0,2:T(8,128)(2,1)S(1)} %pad_maximum_fusion), channel_id=1, source_target_pairs={{0,1},{1,0},{2,3},{3,2},{4,5},{5,4},{6,7},{7,6},{8,9},{9,8},{10,11... | collective-permute-start | bytes 4478984 | tf_op jit(solution)/shard_map/ppermute | solution.py:250
  69.9 28.7 %collective-permute-start.8 = (f32[2,2,2,432,128]{4,3,1,0,2:T(8,128)}, f32[2,2,2,432,128]{4,3,1,0,2:T(8,128)}, u32[]{:S(2)}, u32[]{:S(2)}) collective-permute-start(f32[2,2,2,432,128]{4,3,1,0,2:T(8,128)} %bitcast.59), channel_id=1, source_target_pairs={{0,2},{2,0},{4,6},{6,4},{8,10},{10,8},{12,14},{14,12},{16,18},{18,... | collective-permute-start | bytes 5308424 | tf_op jit(solution)/shard_map/ppermute | solution.py:191
  72.4 36.9 %collective-permute-start.7 = (bf16[27,128,128]{2,1,0:T(8,128)(2,1)S(1)}, bf16[27,128,128]{2,1,0:T(8,128)(2,1)}, u32[]{:S(2)}, u32[]{:S(2)}) collective-permute-start(bf16[27,128,128]{2,1,0:T(8,128)(2,1)S(1)} %get-tuple-element.12), channel_id=1, source_target_pairs={{0,1},{1,0},{2,3},{3,2},{4,5},{5,4},{6,7},{7,6},{8,9},{9,8},{10,11... | collective-permute-start | bytes 2654216 | tf_op jit(solution)/shard_map/ppermute | solution.py:246
  96.4 2.1 %copy-start = (f32[2,2,2,1,432,128]{5,4,3,2,1,0:T(8,128)S(1)}, f32[2,2,2,1,432,128]{5,4,3,2,1,0:T(8,128)}, u32[]{:S(2)}) copy-start(f32[2,2,2,1,432,128]{5,4,3,2,1,0:T(8,128)} %get-tuple-element.2) | copy-start | bytes 5308420
  100.5 25.9 %collective-permute-start.12 = (f32[2,2,216,128]{3,2,0,1:T(8,128)S(1)}, f32[2,2,216,128]{3,2,0,1:T(8,128)S(1)}, u32[]{:S(2)}, u32[]{:S(2)}) collective-permute-start(f32[2,2,216,128]{3,2,0,1:T(8,128)S(1)} %dynamic-slice_bitcast_fusion), channel_id=1, source_target_pairs={{0,8},{2,10},{4,12},{6,14},{8,0},{10,2},{12,4},{14,6},{16,24},{18,... | collective-permute-start | bytes 1327112 | tf_op jit(solution)/shard_map/ppermute | solution.py:191
  103.1 26.4 %collective-permute-start.9 = (f32[2,2,216,128]{3,2,1,0:T(8,128)S(1)}, f32[2,2,216,128]{3,2,1,0:T(8,128)S(1)}, u32[]{:S(2)}, u32[]{:S(2)}) collective-permute-start(f32[2,2,216,128]{3,2,1,0:T(8,128)S(1)} %dynamic-slice_bitcast_fusion.1), channel_id=1, source_target_pairs={{0,4},{2,6},{4,0},{6,2},{8,12},{10,14},{12,8},{14,10},{16,20},{18,... | collective-permute-start | bytes 1327112 | tf_op jit(solution)/shard_map/ppermute | solution.py:191
  126.4 8.5 %collective-permute-start.13 = (f32[2,216,128]{2,1,0:T(8,128)S(1)}, f32[2,216,128]{2,1,0:T(8,128)S(1)}, u32[]{:S(2)}, u32[]{:S(2)}) collective-permute-start(f32[2,216,128]{2,1,0:T(8,128)S(1)} %dynamic-slice_bitcast_fusion.2), channel_id=1, source_target_pairs={{0,16},{2,18},{4,20},{6,22},{8,24},{10,26},{12,28},{14,30},{16,0},... | collective-permute-start | bytes 663560 | tf_op jit(solution)/shard_map/ppermute | solution.py:191
  129.6 10.1 %collective-permute-start.10 = (f32[2,216,128]{2,1,0:T(8,128)S(1)}, f32[2,216,128]{2,1,0:T(8,128)S(1)}, u32[]{:S(2)}, u32[]{:S(2)}) collective-permute-start(f32[2,216,128]{2,1,0:T(8,128)S(1)} %dynamic-slice_bitcast_fusion.3), channel_id=1, source_target_pairs={{0,8},{2,10},{4,12},{6,14},{8,0},{10,2},{12,4},{14,6},{16,24},{18,... | collective-permute-start | bytes 663560 | tf_op jit(solution)/shard_map/ppermute | solution.py:191
  134.9 9.7 %collective-permute-start.14 = (f32[216,128]{1,0:T(8,128)S(1)}, f32[216,128]{1,0:T(8,128)S(1)}, u32[]{:S(2)}, u32[]{:S(2)}) collective-permute-start(f32[216,128]{1,0:T(8,128)S(1)} %dynamic-slice_bitcast_fusion.4), channel_id=1, source_target_pairs={{0,4},{2,6},{4,0},{6,2},{8,12},{10,14},{12,8},{14,10},{16,20},{18,... | collective-permute-start | bytes 331784 | tf_op jit(solution)/shard_map/ppermute | solution.py:191
  139.7 9.8 %collective-permute-start.11 = (f32[216,128]{1,0:T(8,128)S(1)}, f32[216,128]{1,0:T(8,128)S(1)}, u32[]{:S(2)}, u32[]{:S(2)}) collective-permute-start(f32[216,128]{1,0:T(8,128)S(1)} %dynamic-slice_bitcast_fusion.5), channel_id=1, source_target_pairs={{0,16},{2,18},{4,20},{6,22},{8,24},{10,26},{12,28},{14,30},{16,0},... | collective-permute-start | bytes 331784 | tf_op jit(solution)/shard_map/ppermute | solution.py:191

commit v2 on v1

v2 whole, which is shorter than its diff:
```python
import functools
import math

import jax
import jax.numpy as jnp
from jax import lax
from jax.experimental import pallas as pl
from jax.experimental.pallas import tpu as pltpu
from jax.sharding import PartitionSpec as P

EDGE = 8
LAYERZ = 2
NBLK = 8
SPAN = 2 * EDGE
PLANE = SPAN * SPAN
HALF = 128
BF = jnp.bfloat16
F32 = jnp.float32

SHIFTS = [(a, b) for a in (-1, 0, 1) for b in (-1, 0, 1)]
PAIRS = [(0, 1), (2, 3), (4, 5), (6, 7), (8,)]


def locate_side(device_total):
    plane_side = 1
    for candidate in range(1, 33):
        if 2 * candidate**3 == device_total:
            plane_side = candidate
    return plane_side


def keep_column(mask_ref, x):
    return jnp.broadcast_to(mask_ref[x : x + 1, :], (8, PLANE)).T[:, 0:1]


def assemble(raw_ref, mask_ref, xb_ref, yb_ref, gp_ref):
    gp_ref[0] = xb_ref[0]
    gp_ref[SPAN + 1] = xb_ref[1]
    for x in range(SPAN):
        block = raw_ref[x * PLANE : (x + 1) * PLANE, :].astype(F32) * keep_column(mask_ref, x)
        gp_ref[x + 1, 1 : 1 + SPAN] = block.astype(BF).reshape(SPAN, SPAN, HALF)
        gp_ref[x + 1, 0] = yb_ref[0, x]
        gp_ref[x + 1, SPAN + 1] = yb_ref[1, x]


def prep_kernel(feat_ref, faces_ref, mask_ref, f_ref, fz_ref):
    lane = lax.broadcasted_iota(jnp.int32, (1, PLANE), 1) % SPAN
    keep_low = (lane != SPAN - 1).astype(F32)
    keep_high = (lane != 0).astype(F32)
    cin = fz_ref.shape[1]

    for x in range(SPAN):
        cols = slice(x * PLANE, (x + 1) * PLANE)
        block = feat_ref[cols, :].astype(F32).T * mask_ref[x : x + 1, :]
        f_ref[0:cin, cols] = (pltpu.roll(block, 1, 1) * keep_high).astype(BF)
        f_ref[cin : 2 * cin, cols] = block.astype(BF)
        f_ref[2 * cin :, cols] = (pltpu.roll(block, PLANE - 1, 1) * keep_low).astype(BF)
    for side in range(2):
        fz_ref[side] = faces_ref[side].astype(F32).T.astype(BF)


def prep(features, faces, mask_rows):
    cells, cin = features.shape
    return pl.pallas_call(
        prep_kernel,
        out_shape=(
            jax.ShapeDtypeStruct((3 * cin, cells), BF),
            jax.ShapeDtypeStruct((2, cin, PLANE), BF),
        ),
        compiler_params=pltpu.CompilerParams(vmem_limit_bytes=56 << 20),
        cost_estimate=pl.CostEstimate(flops=0, bytes_accessed=cells * cin * 8, transcendentals=0),
        name="prep",
    )(features, faces, mask_rows)


def weight_kernel(
    mine_ref, f_ref, fz_ref, raw_ref, mask_ref, xb_ref, yb_ref, zp_ref,
    keep_ref, send_ref, gp_ref, acc_ref, sems, *, scale
):
    assemble(raw_ref, mask_ref, xb_ref, yb_ref, gp_ref)
    cin = f_ref.shape[0] // 3
    rows = acc_ref.shape[2]

    def source(shift):
        a, b = SHIFTS[shift]
        block = gp_ref[1 - a : 1 - a + SPAN, 1 - b : 1 - b + SPAN]
        return block.reshape(SPAN * PLANE, HALF)

    def face(side, shift):
        a, b = SHIFTS[shift]
        return zp_ref[side, b + 1, 1 - a : 1 - a + SPAN].reshape(PLANE, HALF)

    def store(tap, value):
        first = tap * cin
        while first < (tap + 1) * cin:
            block, at = divmod(first, rows)
            count = min(rows - at, (tap + 1) * cin - first)
            piece = value[first - tap * cin : first - tap * cin + count]
            acc_ref[block % 2, block // 2, at : at + count] = piece
            first += count

    for pair in PAIRS:
        right = jnp.concatenate([source(s) for s in pair], axis=1)
        acc = jnp.dot(f_ref[...], right, preferred_element_type=F32)
        low = jnp.concatenate([face(0, s) for s in pair], axis=1)
        high = jnp.concatenate([face(1, s) for s in pair], axis=1)
        parts = [
            acc[0:cin] + jnp.dot(fz_ref[1], high, preferred_element_type=F32),
            acc[cin : 2 * cin],
            acc[2 * cin :] + jnp.dot(fz_ref[0], low, preferred_element_type=F32),
        ]
        for c in range(3):
            for k, s in enumerate(pair):
                store(3 * s + c, parts[c][:, HALF * k : HALF * (k + 1)] * scale)

    mine = mine_ref[0]
    out_send = pltpu.make_async_copy(acc_ref.at[1 - mine], send_ref, sems.at[0])
    out_keep = pltpu.make_async_copy(acc_ref.at[mine], keep_ref, sems.at[1])
    out_send.start()
    out_keep.start()
    out_send.wait()
    out_keep.wait()


VMEM_SPEC = pl.BlockSpec(memory_space=pltpu.VMEM)
SMEM_SPEC = pl.BlockSpec(memory_space=pltpu.SMEM)
ANY_SPEC = pl.BlockSpec(memory_space=pl.ANY)


def weight_grad_local(mine, f_all, fz, raw, mask_rows, borders, scale, total):
    cin = f_all.shape[0] // 3
    rows = 27 * cin // total
    out = jax.ShapeDtypeStruct((total // 2, rows, HALF), F32)
    return pl.pallas_call(
        functools.partial(weight_kernel, scale=scale),
        out_shape=(out, out),
        in_specs=[SMEM_SPEC] + [VMEM_SPEC] * 7,
        out_specs=(ANY_SPEC, ANY_SPEC),
        scratch_shapes=[
            pltpu.VMEM((SPAN + 2, SPAN + 2, SPAN, HALF), BF),
            pltpu.VMEM((2, total // 2, rows, HALF), F32),
            pltpu.SemaphoreType.DMA((2,)),
        ],
        compiler_params=pltpu.CompilerParams(vmem_limit_bytes=60 << 20),
        cost_estimate=pl.CostEstimate(
            flops=2 * 27 * cin * HALF * SPAN * PLANE, bytes_accessed=12 << 20, transcendentals=0
        ),
        name="weight_grad",
    )(mine, f_all, fz, raw, mask_rows, *borders)


def data_kernel(raw_ref, mask_ref, xb_ref, yb_ref, zp_ref, w_ref, *refs):
    if len(refs) == 5:
        prev_ref, out_ref, gp_ref, wt_ref, h_ref = refs
    else:
        (out_ref, gp_ref, wt_ref, h_ref), prev_ref = refs, None
    assemble(raw_ref, mask_ref, xb_ref, yb_ref, gp_ref)
    for s in range(9):
        for c in range(3):
            tile = w_ref[3 * s + c].astype(F32).T.astype(BF)
            wt_ref[s * HALF : (s + 1) * HALF, c * HALF : (c + 1) * HALF] = tile

    for side, c in ((0, 2), (1, 0)):
        cols = []
        for s in range(9):
            a, b = SHIFTS[s]
            cols.append(zp_ref[side, b + 1, 1 - a : 1 - a + SPAN].reshape(PLANE, HALF))
        h_ref[side] = jnp.dot(
            jnp.concatenate(cols, axis=1),
            wt_ref[:, c * HALF : (c + 1) * HALF],
            preferred_element_type=F32,
        ).reshape(SPAN, SPAN, HALF)

    zpos = lax.broadcasted_iota(jnp.int32, (SPAN, SPAN, HALF), 1)

    def plane(x, _):
        cols = []
        for s in range(9):
            a, b = SHIFTS[s]
            block = gp_ref[pl.ds(x + 1 - a, 1), 1 - b : 1 - b + SPAN]
            cols.append(block.reshape(PLANE, HALF))
        prod = jnp.dot(jnp.concatenate(cols, axis=1), wt_ref[...], preferred_element_type=F32)
        down = pltpu.roll(prod[:, 0:HALF], PLANE - 1, 0).reshape(SPAN, SPAN, HALF)
        mid = prod[:, HALF : 2 * HALF].reshape(SPAN, SPAN, HALF)
        up = pltpu.roll(prod[:, 2 * HALF :], 1, 0).reshape(SPAN, SPAN, HALF)
        low = h_ref[0, pl.ds(x, 1)].reshape(SPAN, 1, HALF)
        high = h_ref[1, pl.ds(x, 1)].reshape(SPAN, 1, HALF)
        full = mid + jnp.where(zpos == 0, low, up) + jnp.where(zpos == SPAN - 1, high, down)
        full = full.reshape(PLANE, HALF)
        rows = pl.ds(pl.multiple_of(x * PLANE, PLANE), PLANE)
        if prev_ref is None:
            out_ref[rows, :] = full
        else:
            keep = jnp.broadcast_to(mask_ref[pl.ds(x, 1), :], (8, PLANE)).T[:, 0:1]
            out_ref[rows, :] = ((full + prev_ref[rows, :]) * keep).astype(BF)
        return 0

    lax.fori_loop(0, SPAN, plane, 0, unroll=2)


def data_grad_local(raw, mask_rows, borders, tiles, before=None):
    args = (raw, mask_rows, *borders, tiles) + (() if before is None else (before,))
    return pl.pallas_call(
        data_kernel,
        out_shape=jax.ShapeDtypeStruct((SPAN * PLANE, HALF), F32 if before is None else BF),
        in_specs=[VMEM_SPEC] * len(args),
        out_specs=VMEM_SPEC,
        scratch_shapes=[
            pltpu.VMEM((SPAN + 2, SPAN + 2, SPAN, HALF), BF),
            pltpu.VMEM((9 * HALF, 3 * HALF), BF),
            pltpu.VMEM((2, SPAN, SPAN, HALF), F32),
        ],
        compiler_params=pltpu.CompilerParams(vmem_limit_bytes=56 << 20),
        cost_estimate=pl.CostEstimate(
            flops=2 * 27 * HALF * HALF * SPAN * PLANE, bytes_accessed=6 << 20, transcendentals=0
        ),
        name="data_grad",
    )(*args)


def split_kernel(bits_ref, keep_ref, recv_ref, *outs, bounds):
    for k, (low, high, lead) in enumerate(bounds):
        stay_ref, go_ref = outs[2 * k], outs[2 * k + 1]
        shape = keep_ref.shape
        mine = bits_ref[k]
        before = math.prod(shape[:lead])
        for ref, bit in ((stay_ref, mine), (go_ref, 1 - mine)):
            for i in range(before):
                at = []
                for size in reversed(shape[:lead]):
                    i, rest = divmod(i, size)
                    at.insert(0, rest)
                at = tuple(at)
                tail = (slice(None),) * (len(shape) - 3 - lead)
                src = at + (bit,) + tail + (slice(low, high),)
                ref[at] = keep_ref[src] + recv_ref[src]


def split(keep, recv, bits, bounds):
    outs = []
    for low, high, lead in bounds:
        shape = keep.shape[:lead] + keep.shape[lead + 1 : -2] + (high - low, HALF)
        outs += [jax.ShapeDtypeStruct(shape, F32)] * 2
    return pl.pallas_call(
        functools.partial(split_kernel, bounds=bounds),
        out_shape=tuple(outs),
        in_specs=[SMEM_SPEC, VMEM_SPEC, VMEM_SPEC],
        out_specs=tuple(VMEM_SPEC for _ in outs),
        compiler_params=pltpu.CompilerParams(vmem_limit_bytes=32 << 20),
        cost_estimate=pl.CostEstimate(
            flops=keep.size, bytes_accessed=16 * keep.size, transcendentals=0
        ),
        name="add_split",
    )(jnp.stack(bits), keep, recv)


def swap_bit(block, bit, total):
    return lax.ppermute(block, "space", [(i, i ^ (1 << bit)) for i in range(total)])


def bit_of(index, bit):
    return (index // (1 << bit) % 2).astype(jnp.int32)


def extend(block, dim, stride, coords, side):
    total = lax.axis_size("space")
    length = block.shape[dim]
    first = lax.slice_in_dim(block, 0, 1, axis=dim)
    last = lax.slice_in_dim(block, length - 1, length, axis=dim)
    below = lax.ppermute(
        last, "space", [(i, i + stride) for i in range(total) if coords(i) < side - 1]
    )
    above = lax.ppermute(
        first, "space", [(i + stride, i) for i in range(total) if coords(i) < side - 1]
    )
    return jnp.concatenate([below, block, above], axis=dim)


def turned(face):
    return jnp.stack([face[:, 1 - b : 1 - b + SPAN] for b in (-1, 0, 1)])


def wide_borders(masked, zl, zh, plane_side, depth):
    block = jnp.concatenate([zl[:, :, None], masked, zh[:, :, None]], axis=2)
    block = extend(block, 1, depth, lambda i: i // depth % plane_side, plane_side)
    block = extend(block, 0, depth * plane_side, lambda i: i // (depth * plane_side), plane_side)
    inner = block[:, :, 1 : 1 + SPAN]
    xb = jnp.stack([inner[0], inner[SPAN + 1]])
    yb = jnp.stack([inner[1 : 1 + SPAN, 0], inner[1 : 1 + SPAN, SPAN + 1]])
    zp = jnp.stack([turned(block[:, :, 0]), turned(block[:, :, SPAN + 1])])
    return xb, yb, zp


def pair_borders(cx, cy, xh, yh, eh, zl, zh):
    def both(value, coord, axis):
        zero = jnp.zeros_like(value)
        low = jnp.where(coord == 1, value, zero)
        high = jnp.where(coord == 0, value, zero)
        return jnp.expand_dims(low, axis), jnp.expand_dims(high, axis)

    def around(values, corner, axis):
        low, high = both(corner, cy, axis)
        return jnp.concatenate([low, values, high], axis=axis)

    xb = jnp.concatenate(both(around(xh[:SPAN], eh[:SPAN], 0), cx, 0))
    yb = jnp.concatenate(both(yh[:SPAN], cy, 0))

    def face(z, k):
        rows = around(z, yh[k], 1)
        low, high = both(around(xh[k], eh[k], 0), cx, 0)
        return turned(jnp.concatenate([low, rows, high], axis=0))

    zp = jnp.stack([face(zl, SPAN), face(zh, SPAN + 1)])
    return xb, yb, zp


def body(features, grad_out, weights, occupancy, block_list, block_count):
    total = lax.axis_size("space")
    plane_side = locate_side(total)
    depth = 2 * plane_side
    cells, cin = features.shape
    index = lax.axis_index("space")
    column = lax.axis_index("chan")
    swap = [(0, 1), (1, 0)]

    other_raw = lax.ppermute(grad_out, "chan", swap)

    block_order = block_list[0]
    live_count = block_count[0]
    slots = jnp.arange(NBLK, dtype=jnp.int32)
    position = jnp.sum(
        jnp.where(block_order[:, None] == slots[None, :], slots[:, None], 0), axis=0
    )
    active = (position < live_count).astype(F32)
    grid = jnp.broadcast_to(
        active.reshape(2, 1, 2, 1, LAYERZ, 1), (2, EDGE, 2, EDGE, LAYERZ, EDGE)
    ).reshape(SPAN, PLANE)
    mask_rows = grid * occupancy.reshape(SPAN, PLANE).astype(F32)
    mask = mask_rows.reshape(SPAN, SPAN, SPAN, 1).astype(BF)
    cube = grad_out.reshape(SPAN, SPAN, SPAN, HALF)

    even = index % 2 == 0
    low = cube[:, :, 0] * mask[:, :, 0]
    high = cube[:, :, SPAN - 1] * mask[:, :, SPAN - 1]
    inside = [i for i in range(total) if i % depth % 2 == 1 and i % depth < depth - 1]
    second = [(i, i + 1) for i in inside] + [(i + 1, i) for i in inside]
    from_a = swap_bit(jnp.where(even, high, low), 0, total)
    from_b = lax.ppermute(jnp.where(even, low, high), "space", second)
    zl = jnp.where(even, from_b, from_a)
    zh = jnp.where(even, from_a, from_b)

    if plane_side == 2:
        cx = index // (2 * depth)
        cy = index // depth % 2
        sx, sy = 2 * depth, depth

        def at(values, axis, coord):
            size = values.shape[axis]
            return jnp.where(
                coord == 0,
                lax.index_in_dim(values, size - 1, axis, keepdims=False),
                lax.index_in_dim(values, 0, axis, keepdims=False),
            )

        xf = at(cube, 0, cx) * at(mask, 0, cx)
        yf = at(cube, 1, cy) * at(mask, 1, cy)
        ef = at(at(cube, 0, cx), 0, cy) * at(at(mask, 0, cx), 0, cy)
        xs = jnp.concatenate([xf, at(zl, 0, cx)[None], at(zh, 0, cx)[None]])
        ys = jnp.concatenate([yf, at(zl, 1, cy)[None], at(zh, 1, cy)[None]])
        es = jnp.concatenate(
            [ef, at(at(zl, 0, cx), 0, cy)[None], at(at(zh, 0, cx), 0, cy)[None]]
        )
        xh = lax.ppermute(xs, "space", [(i, i ^ sx) for i in range(total)])
        yh = lax.ppermute(ys, "space", [(i, i ^ sy) for i in range(total)])
        eh = lax.ppermute(es, "space", [(i, i ^ sx ^ sy) for i in range(total)])
        borders = pair_borders(cx, cy, xh, yh, eh, zl, zh)
        flat = jnp.concatenate(
            [
                xh.reshape(-1, HALF),
                yh.reshape(-1, HALF),
                zl.reshape(-1, HALF),
                zh.reshape(-1, HALF),
                jnp.pad(eh, ((0, 14), (0, 0))),
            ]
        )
        flat = lax.ppermute(flat, "chan", swap)
        n = (SPAN + 2) * SPAN
        oxh = flat[:n].reshape(SPAN + 2, SPAN, HALF)
        oyh = flat[n : 2 * n].reshape(SPAN + 2, SPAN, HALF)
        ozl = flat[2 * n : 2 * n + PLANE].reshape(SPAN, SPAN, HALF)
        ozh = flat[2 * n + PLANE : 2 * n + 2 * PLANE].reshape(SPAN, SPAN, HALF)
        oeh = flat[2 * n + 2 * PLANE : 2 * n + 2 * PLANE + SPAN + 2]
        other_borders = pair_borders(cx, cy, oxh, oyh, oeh, ozl, ozh)
    else:
        borders = wide_borders(cube * mask, zl, zh, plane_side, depth)
        other_borders = tuple(lax.ppermute(v, "chan", swap) for v in borders)

    theirs = lax.dynamic_slice_in_dim(weights, (1 - column) * HALF, HALF, axis=1)
    own_w = lax.dynamic_slice_in_dim(weights, column * HALF, HALF, axis=1)
    flat_w = theirs.reshape(2, 27 * HALF // 2, HALF)
    core = bit_of(index, 0)
    part = lax.ppermute(
        lax.dynamic_index_in_dim(flat_w, core, 0, keepdims=False), "chan", swap
    )
    part_b = swap_bit(part, 0, total)
    other_w = jnp.concatenate(
        [jnp.where(core == 0, part, part_b), jnp.where(core == 0, part_b, part)]
    ).reshape(27, HALF, HALF)

    by_z = features.reshape(PLANE, SPAN, cin)
    z_mask = mask.reshape(PLANE, SPAN, 1)
    faces = jnp.stack([by_z[:, 0] * z_mask[:, 0], by_z[:, SPAN - 1] * z_mask[:, SPAN - 1]])
    f_all, fz = prep(features, faces, mask_rows)
    scale = 1.0 / math.sqrt(cells * total)
    keep, send = weight_grad_local(
        core[None], f_all, fz, grad_out, mask_rows, borders, scale, total
    )

    recv = swap_bit(send, 0, total)
    bits = total.bit_length() - 1
    rows = keep.shape[1]
    cut = rows // 2
    keep = keep.reshape((2,) * (bits - 1) + (rows, HALF))
    recv = recv.reshape(keep.shape)
    orders = [list(range(1, bits)), list(range(2, bits)) + [1]]
    have = [list(range(bits - 1, 0, -1)) for _ in orders]
    bounds = [
        (0, cut, have[0].index(orders[0][0])),
        (cut, rows, have[1].index(orders[1][0])),
    ]
    stay1, go1, stay2, go2 = split(
        keep, recv, [bit_of(index, order[0]) for order in orders], bounds
    )
    stays, gos = [stay1, stay2], [go1, go2]
    partial_out = None
    for step in range(bits - 1):
        got = [swap_bit(go, order[step], total) for go, order in zip(gos, orders)]
        if step == 0:
            raw, gos[0] = lax.optimization_barrier((grad_out, gos[0]))
            partial_out = data_grad_local(raw, mask_rows, borders, own_w)
            got, partial_out = lax.optimization_barrier((got, partial_out))
        if step == 1:
            data_out = data_grad_local(
                other_raw, mask_rows, other_borders, other_w, partial_out
            )
            got, data_out = lax.optimization_barrier((got, data_out))
        if step == bits - 2:
            weight_out = jnp.concatenate([s + g for s, g in zip(stays, got)], axis=0)
            break
        for k, order in enumerate(orders):
            have[k].remove(order[step])
            nxt = order[step + 1]
            stays[k], gos[k] = split(
                stays[k],
                got[k],
                [bit_of(index, nxt)],
                [(0, stays[k].shape[-2], have[k].index(nxt))],
            )
    return data_out, weight_out

def solution(mesh):
    placed = (
        P("space", None),
        P("space", "chan"),
        P(None, None, "chan"),
        P("space"),
        P("space", None),
        P("space"),
    )
    return jax.shard_map(
        body,
        mesh=mesh,
        in_specs=placed,
        out_specs=(P("space", "chan"), P("space", "chan")),
        check_vma=False,
    )
```

time: 151 us -> 100 us (0.66)
  waiting for transfers between devices: 40 us -> 11.4 us
  starting transfers between devices: 36.9 us -> 21.2 us
  local copies, waits for them, and re-layouts: 21.9 us -> 6.65 us
  Pallas kernels: 39.5 us -> 46.8 us
  other arithmetic: 10.3 us -> 11.9 us
    ppermute x8 -> x7, waiting for transfers between devices: 30.6 us -> 4.6 us  [the longest x1 3.72 us: body(): yh = lax.ppermute(ys, 'space', [(i, i ^ sy) for i in range(total)])]
    ppermute x8 -> x7, starting transfers between devices: 20.7 us -> 10.4 us  [the longest x1 3.67 us: body(): eh = lax.ppermute(es, 'space', [(i, i ^ sx ^ sy) for i in range(total)])]
    slice x10 -> x5, local copies, waits for them, and re-layouts: 11.2 us -> 3.62 us  [the longest x1 1.95 us: body(): by_z[:, 0] * z_mask[:, 0]]
    pallas_call x1 -> x2, Pallas kernels: 17.1 us -> 23.7 us  [data_grad_local(): pl.pallas_call(data_kernel, out_shape=jax.ShapeDtypeStruct((SPAN * PLANE,...]
    ppermute x7 -> x9, starting transfers between devices: 16.2 us -> 10.8 us  [swap_bit(): lax.ppermute(block, 'space', [(i, i ^ 1 << bit) for i in range(total)])]
    dynamic_slice x2 -> x0, local copies, waits for them, and re-layouts: 4.83 us -> none  [the longest x1 3.49 us: halve(): keep = lax.dynamic_index_in_dim(block, mine, axis, keepdims=False)]
    ppermute x7 -> x9, waiting for transfers between devices: 9.36 us -> 6.83 us  [swap_bit(): lax.ppermute(block, 'space', [(i, i ^ 1 << bit) for i in range(total)])]
    add x7 -> x2, other arithmetic: 1.93 us -> 0.03 us  [body(): weight_out = jnp.concatenate([s + g for s, g in zip(stays, got)], axis=0)]
  transfers between devices with their start and end apart: 15 -> 16, of which waited for: 6 -> 5; matrix products, arithmetic and copies ran while one was open for 16% -> 18% of each run, Pallas kernels for 26% -> 47%
where the time goes in v2:
time: 100 us; the launch traced here: 99.9 us
  Pallas kernels  46.8 us (47%)
  starting transfers between devices  21.2 us (21%)
  other arithmetic  11.9 us (12%)
  waiting for transfers between devices  11.4 us (11%)
  local copies, waits for them, and re-layouts  6.65 us (7%)
  between operations  1.89 us (2%)
    pallas_call x2, Pallas kernels, data_grad_local(): pl.pallas_call(data_kernel, out_shape=jax.ShapeDtypeStruct((SPAN * PLANE,...  23.7 us
    pallas_call x1, Pallas kernels, weight_grad_local(): pl.pallas_call(functools.partial(weight_kernel, scale=scale), out_shape=(...  14.9 us
    ppermute x9, starting transfers between devices, swap_bit(): lax.ppermute(block, 'space', [(i, i ^ 1 << bit) for i in range(total)])  10.8 us
    pallas_call x1, Pallas kernels, prep(): pl.pallas_call(prep_kernel, out_shape=(jax.ShapeDtypeStruct((3 * cin, cel...  7.27 us
    ppermute x9, waiting for transfers between devices, swap_bit(): lax.ppermute(block, 'space', [(i, i ^ 1 << bit) for i in range(total)])  6.83 us
    ppermute x1, waiting for transfers between devices, body(): yh = lax.ppermute(ys, 'space', [(i, i ^ sy) for i in range(total)])  3.72 us
    ppermute x1, starting transfers between devices, body(): eh = lax.ppermute(es, 'space', [(i, i ^ sx ^ sy) for i in range(total)])  3.67 us
    ppermute x1, starting transfers between devices, body(): other_raw = lax.ppermute(grad_out, 'chan', swap)  3.03 us
  transfers between devices with their start and end apart: 16, of which 5 were waited for; matrix products, arithmetic and copies ran while one was open for 18% of the time, Pallas kernels for 47%

profile of v2, /device:TPU:0, one launch (start us, length us, event | category | flops | bytes accessed | tf_op | source)
XLA Modules:
  0.0 99.9 jit_solution(6853319967221453903)
XLA Ops:
  0.6 3.0 %collective-permute-start.10 = (bf16[4096,128]{1,0:T(8,128)(2,1)}, bf16[4096,128]{1,0:T(8,128)(2,1)}, u32[]{:S(2)}, u32[]{:S(2)}) collective-permute-start(bf16[4096,128]{1,0:T(8,128)(2,1)} %raw_ref.2), channel_id=1, source_target_pairs={{0,1},{1,0},{2,3},{3,2},{4,5},{5,4},{6,7},{7,6},{8,9},{9,8},{10,11... | collective-permute-start | bytes 3145736 | tf_op jit(solution)/shard_map/ppermute | solution.py:326
  3.7 0.7 select_reduce_fusion
  5.1 0.1 reshape.930
  5.2 0.7 convert_element_type.61
  5.9 0.1 broadcast_in_dim.31.clone
  6.0 0.2 reshape.918
  6.2 0.1 convert_element_type.65
  6.3 0.2 slice_reduce_fusion
  6.6 1.4 %fusion.20 = (bf16[16,16,1,128]{3,2,1,0:T(2,128)(2,1)S(1)}, bf16[16,16,1,128]{3,2,1,0:T(2,128)(2,1)S(1)}) fusion(bf16[16,16,16,128]{3,2,1,0:T(8,128)(2,1)} %bitcast.179), kind=kLoop, calls=%fused_computation.142 | loop fusion | bytes 262144 | tf_op jit(solution)/shard_map/slice | solution.py:344
  8.0 0.1 broadcast_select_fusion.11
  8.1 0.7 collective-permute-start
  8.8 2.9 %collective-permute-start.1 = (bf16[16,16,128]{2,1,0:T(8,128)(2,1)S(1)}, bf16[16,16,128]{2,1,0:T(8,128)(2,1)S(1)}, u32[]{:S(2)}, u32[]{:S(2)}) collective-permute-start(bf16[16,16,128]{2,1,0:T(8,128)(2,1)S(1)} %get-tuple-element.78), channel_id=1, source_target_pairs={{0,2},{2,0},{4,6},{6,4},{8,10},{10,8},{12,14},{14,12},{16,18},{18,... | collective-permute-start | bytes 196616 | tf_op jit(solution)/shard_map/ppermute | solution.py:258
  11.7 1.1 %constant_dynamic-slice_fusion = (bf16[27,128,128]{2,1,0:T(8,128)(2,1)S(1)}, bf16[27,128,128]{2,1,0:T(8,128)(2,1)}) fusion(bf16[27,256,128]{2,1,0:T(8,128)(2,1)S(1)} %copy-done.1, s32[]{:T(128)S(6)} %select_n.669, s32[]{:T(128)S(6)} %select_n.644), kind=kLoop, calls=%fused_computation.127 | loop fusion | bytes 3538952 | tf_op jit(solution)/shard_map/dynamic_slice | solution.py:398
  12.8 0.6 collective-permute-start.12
  13.4 0.1 copy.98
  13.5 0.1 convert_element_type.62
  13.6 0.4 reshape.917
  14.0 0.9 slice_select_fusion
  14.9 2.0 %fusion.19 = (bf16[256,1,256]{2,1,0:T(2,128)(2,1)S(1)}, bf16[256,1,256]{2,1,0:T(2,128)(2,1)S(1)}) fusion(bf16[256,16,256]{2,1,0:T(8,128)(2,1)} %bitcast.168), kind=kLoop, calls=%fused_computation.141 | loop fusion | bytes 524288 | tf_op jit(solution)/shard_map/slice | solution.py:412
  16.9 0.1 broadcast_in_dim.31
  17.0 0.4 reshape.916
  17.4 0.1 copy.99
  17.5 1.0 fusion.4
  18.5 0.1 fusion
  18.7 0.7 pad_maximum_fusion.3.faces_ref
  19.4 0.6 mul.98.mask_ref
  20.0 7.3 %prep.1 = (bf16[768,4096]{1,0:T(8,128)(2,1)}, bf16[2,256,256]{2,1,0:T(8,128)(2,1)}) custom-call(bf16[4096,256]{1,0:T(8,128)(2,1)} %feat_ref.1, bf16[2,256,256]{2,1,0:T(8,128)(2,1)} %pad_maximum_fusion.3.faces_ref, f32[16,256]{1,0:T(8,128)} %mul.98.mask_ref), custom_call_target="tpu_custom_call" | custom-call | bytes 8388608 | tf_op jit(solution)/shard_map/prep/pallas_call | solution.py:64
  27.3 0.1 fusion.7
  27.3 0.1 broadcast_multiply_fusion
  27.4 0.1 pad_add_fusion.bits_ref
  27.7 3.7 %collective-permute-start.2 = (bf16[18,128]{1,0:T(8,128)(2,1)S(1)}, bf16[18,128]{1,0:T(8,128)(2,1)S(1)}, u32[]{:S(2)}, u32[]{:S(2)}) collective-permute-start(bf16[18,128]{1,0:T(8,128)(2,1)S(1)} %pad_maximum_fusion.17), channel_id=1, source_target_pairs={{0,24},{2,26},{4,28},{6,30},{8,16},{10,18},{12,20},{14,22},{16,8},... | collective-permute-start | bytes 13832 | tf_op jit(solution)/shard_map/ppermute | solution.py:375
  31.4 0.1 collective-permute-start.3
  31.5 0.8 collective-permute-start.4
  32.3 0.9 collective-permute-done.2
  33.2 3.7 %collective-permute-done.4 = bf16[18,16,128]{2,1,0:T(8,128)(2,1)S(1)} collective-permute-done((bf16[18,16,128]{2,1,0:T(8,128)(2,1)S(1)}, bf16[18,16,128]{2,1,0:T(8,128)(2,1)S(1)}, u32[]{:S(2)}, u32[]{:S(2)}) %collective-permute-start.4) | collective-permute-done | bytes 73760 | tf_op jit(solution)/shard_map/ppermute | solution.py:374
  37.0 0.1 pad_maximum_fusion.10
  37.1 0.1 pad_maximum_fusion.9
  37.3 1.6 %collective-permute-start.11 = (bf16[1120,128]{1,0:T(8,128)(2,1)S(1)}, bf16[1120,128]{1,0:T(8,128)(2,1)S(1)}, u32[]{:S(2)}, u32[]{:S(2)}) collective-permute-start(bf16[1120,128]{1,0:T(8,128)(2,1)S(1)} %constant_dynamic-update-slice_fusion), channel_id=1, source_target_pairs={{0,1},{1,0},{2,3},{3,2},{4,5},{5,4},{6,7},{7,6},{8,9},{9,8},{10,11... | collective-permute-start | bytes 860168 | tf_op jit(solution)/shard_map/ppermute | solution.py:386
  38.9 0.7 pad_maximum_fusion.5.xb_ref
  39.6 0.7 pad_maximum_fusion.7.yb_ref
  40.3 0.8 pad_maximum_fusion.1.zp_ref
  41.1 14.9 %weight_grad.1 = (f32[8,432,128]{2,1,0:T(8,128)}, f32[8,432,128]{2,1,0:T(8,128)}) custom-call(s32[1]{0:T(128)} %bitcast.2.mine_ref, bf16[768,4096]{1,0:T(8,128)(2,1)} %get-tuple-element.25.f_ref, bf16[2,256,256]{2,1,0:T(8,128)(2,1)} %get-tuple-element.26.fz_ref, bf16[4096,128]{1,0:T(8,128)(2,1)} %raw_ref.2, f32[16,256]{1,0:T(8,128)} %mul.98.mask_ref, ...), custom_call_target="tpu_custom_call" | custom-call | flops 7247757312 | bytes 12582912 | tf_op jit(solution)/shard_map/weight_grad/pallas_call | solution.py:134
  56.1 0.1 collective-permute-start.5
  56.3 0.7 pad_maximum_fusion.8.yb_ref
  57.0 0.1 pad_maximum_fusion.12
  57.1 0.7 pad_maximum_fusion.6.xb_ref
  57.9 0.5 collective-permute-start.13
  58.5 0.8 pad_maximum_fusion.2.zp_ref
  59.3 1.2 %collective-permute-done.13 = bf16[1728,128]{1,0:T(8,128)(2,1)S(1)} collective-permute-done((bf16[1728,128]{1,0:T(8,128)(2,1)S(1)}, bf16[1728,128]{1,0:T(8,128)(2,1)S(1)}, u32[]{:S(2)}, u32[]{:S(2)}) %collective-permute-start.13) | collective-permute-done | bytes 442400 | tf_op jit(solution)/shard_map/ppermute | solution.py:258
  60.5 0.1 broadcast_select_fusion.1
  60.6 0.7 add_split.5
  61.3 0.4 collective-permute-start.6
  61.7 0.1 collective-permute-start.7
  61.8 1.0 pad_maximum_fusion
  62.8 11.4 %data_grad.2.refs_0_ = f32[4096,128]{1,0:T(8,128)} custom-call(bf16[4096,128]{1,0:T(8,128)(2,1)} %raw_ref.2, f32[16,256]{1,0:T(8,128)} %mul.98.mask_ref, bf16[2,18,16,128]{3,2,1,0:T(8,128)(2,1)} %pad_maximum_fusion.5.xb_ref, bf16[2,16,16,128]{3,2,1,0:T(8,128)(2,1)} %pad_maximum_fusion.7.yb_ref, bf16[2,3,18,16,128]{4,3,2,1,0:T(8,128)(2,1)} %pad_maximum_fusion.1.zp_ref, ...), custom_call_target="tpu_custom_call" | custom-call | flops 3623878656 | bytes 6291456 | tf_op jit(solution)/shard_map/data_grad/pallas_call | solution.py:203
  74.2 0.1 add_split.6
  74.3 2.0 %collective-permute-start.8 = (f32[2,216,128]{2,1,0:T(8,128)S(1)}, f32[2,216,128]{2,1,0:T(8,128)S(1)}, u32[]{:S(2)}, u32[]{:S(2)}) collective-permute-start(f32[2,216,128]{2,1,0:T(8,128)S(1)} %get-tuple-element.34), channel_id=1, source_target_pairs={{0,8},{2,10},{4,12},{6,14},{8,0},{10,2},{12,4},{14,6},{16,24},{18,... | collective-permute-start | bytes 663560 | tf_op jit(solution)/shard_map/ppermute | solution.py:258
  76.3 1.7 %collective-permute-start.9 = (f32[2,216,128]{2,1,0:T(8,128)S(1)}, f32[2,216,128]{2,1,0:T(8,128)S(1)}, u32[]{:S(2)}, u32[]{:S(2)}) collective-permute-start(f32[2,216,128]{2,1,0:T(8,128)S(1)} %get-tuple-element.37), channel_id=1, source_target_pairs={{0,16},{2,18},{4,20},{6,22},{8,24},{10,26},{12,28},{14,30},{16,0},... | collective-permute-start | bytes 663560 | tf_op jit(solution)/shard_map/ppermute | solution.py:258
  78.0 12.3 %data_grad.3 = bf16[4096,128]{1,0:T(8,128)(2,1)} custom-call(bf16[4096,128]{1,0:T(8,128)(2,1)} %collective-permute-done.10.raw_ref, f32[16,256]{1,0:T(8,128)} %mul.98.mask_ref, bf16[2,18,16,128]{3,2,1,0:T(8,128)(2,1)} %pad_maximum_fusion.6.xb_ref, bf16[2,16,16,128]{3,2,1,0:T(8,128)(2,1)} %pad_maximum_fusion.8.yb_ref, ...), custom_call_target="tpu_custom_call" | custom-call | flops 3623878656 | bytes 6291456 | tf_op jit(solution)/shard_map/data_grad/pallas_call | solution.py:203
  90.3 2.0 %collective-permute-start.15 = (f32[216,128]{1,0:T(8,128)S(1)}, f32[216,128]{1,0:T(8,128)S(1)}, u32[]{:S(2)}, u32[]{:S(2)}) collective-permute-start(f32[216,128]{1,0:T(8,128)S(1)} %get-tuple-element.47), channel_id=1, source_target_pairs={{0,4},{2,6},{4,0},{6,2},{8,12},{10,14},{12,8},{14,10},{16,20},{18,... | collective-permute-start | bytes 331784 | tf_op jit(solution)/shard_map/ppermute | solution.py:258
  92.4 1.1 %collective-permute-start.14 = (f32[216,128]{1,0:T(8,128)S(1)}, f32[216,128]{1,0:T(8,128)S(1)}, u32[]{:S(2)}, u32[]{:S(2)}) collective-permute-start(f32[216,128]{1,0:T(8,128)S(1)} %get-tuple-element.43), channel_id=1, source_target_pairs={{0,16},{2,18},{4,20},{6,22},{8,24},{10,26},{12,28},{14,30},{16,0},... | collective-permute-start | bytes 331784 | tf_op jit(solution)/shard_map/ppermute | solution.py:258
  93.5 1.7 %collective-permute-done.15 = f32[216,128]{1,0:T(8,128)S(1)} collective-permute-done((f32[216,128]{1,0:T(8,128)S(1)}, f32[216,128]{1,0:T(8,128)S(1)}, u32[]{:S(2)}, u32[]{:S(2)}) %collective-permute-start.15) | collective-permute-done | bytes 110624 | tf_op jit(solution)/shard_map/ppermute | solution.py:258
  95.1 4.0 %collective-permute-done.14 = f32[216,128]{1,0:T(8,128)S(1)} collective-permute-done((f32[216,128]{1,0:T(8,128)S(1)}, f32[216,128]{1,0:T(8,128)S(1)}, u32[]{:S(2)}, u32[]{:S(2)}) %collective-permute-start.14) | collective-permute-done | bytes 110624 | tf_op jit(solution)/shard_map/ppermute | solution.py:258
  99.2 0.7 pad_maximum_fusion.4
  (78 shorter events, 1.1 us)
Async XLA Ops:
  0.6 11.1 %copy-start.1 = (bf16[27,256,128]{2,1,0:T(8,128)(2,1)S(1)}, bf16[27,256,128]{2,1,0:T(8,128)(2,1)}, u32[]{:S(2)}) copy-start(bf16[27,256,128]{2,1,0:T(8,128)(2,1)} %param.8) | copy-start | bytes 5308420
  0.6 77.4 %collective-permute-start.10 = (bf16[4096,128]{1,0:T(8,128)(2,1)}, bf16[4096,128]{1,0:T(8,128)(2,1)}, u32[]{:S(2)}, u32[]{:S(2)}) collective-permute-start(bf16[4096,128]{1,0:T(8,128)(2,1)} %raw_ref.2), channel_id=1, source_target_pairs={{0,1},{1,0},{2,3},{3,2},{4,5},{5,4},{6,7},{7,6},{8,9},{9,8},{10,11... | collective-permute-start | bytes 3145736 | tf_op jit(solution)/shard_map/ppermute | solution.py:326
  8.1 19.4 %collective-permute-start = (bf16[16,16,128]{2,1,0:T(8,128)(2,1)S(1)}, bf16[16,16,128]{2,1,0:T(8,128)(2,1)S(1)}, u32[]{:S(2)}, u32[]{:S(2)}) collective-permute-start(bf16[16,16,128]{2,1,0:T(8,128)(2,1)S(1)} %get-tuple-element.77), channel_id=1, source_target_pairs={{2,4},{10,12},{18,20},{26,28},{4,2},{12,10},{20,18},{28,26},{3,5},... | collective-permute-start | bytes 196616 | tf_op jit(solution)/shard_map/ppermute | solution.py:348
  8.8 18.7 %collective-permute-start.1 = (bf16[16,16,128]{2,1,0:T(8,128)(2,1)S(1)}, bf16[16,16,128]{2,1,0:T(8,128)(2,1)S(1)}, u32[]{:S(2)}, u32[]{:S(2)}) collective-permute-start(bf16[16,16,128]{2,1,0:T(8,128)(2,1)S(1)} %get-tuple-element.78), channel_id=1, source_target_pairs={{0,2},{2,0},{4,6},{6,4},{8,10},{10,8},{12,14},{14,12},{16,18},{18,... | collective-permute-start | bytes 196616 | tf_op jit(solution)/shard_map/ppermute | solution.py:258
  12.8 45.1 %collective-permute-start.12 = (bf16[1728,128]{1,0:T(8,128)(2,1)S(1)}, bf16[1728,128]{1,0:T(8,128)(2,1)S(1)}, u32[]{:S(2)}, u32[]{:S(2)}) collective-permute-start(bf16[1728,128]{1,0:T(8,128)(2,1)S(1)} %dynamic-slice_bitcast_fusion), channel_id=1, source_target_pairs={{0,1},{1,0},{2,3},{3,2},{4,5},{5,4},{6,7},{7,6},{8,9},{9,8},{10,11... | collective-permute-start | bytes 1327112 | tf_op jit(solution)/shard_map/ppermute | solution.py:402
  27.7 5.5 %collective-permute-start.2 = (bf16[18,128]{1,0:T(8,128)(2,1)S(1)}, bf16[18,128]{1,0:T(8,128)(2,1)S(1)}, u32[]{:S(2)}, u32[]{:S(2)}) collective-permute-start(bf16[18,128]{1,0:T(8,128)(2,1)S(1)} %pad_maximum_fusion.17), channel_id=1, source_target_pairs={{0,24},{2,26},{4,28},{6,30},{8,16},{10,18},{12,20},{14,22},{16,8},... | collective-permute-start | bytes 13832 | tf_op jit(solution)/shard_map/ppermute | solution.py:375
  31.4 5.6 %collective-permute-start.3 = (bf16[18,16,128]{2,1,0:T(8,128)(2,1)S(1)}, bf16[18,16,128]{2,1,0:T(8,128)(2,1)S(1)}, u32[]{:S(2)}, u32[]{:S(2)}) collective-permute-start(bf16[18,16,128]{2,1,0:T(8,128)(2,1)S(1)} %pad_maximum_fusion.13), channel_id=1, source_target_pairs={{0,16},{2,18},{4,20},{6,22},{8,24},{10,26},{12,28},{14,30},{16,0},... | collective-permute-start | bytes 221192 | tf_op jit(solution)/shard_map/ppermute | solution.py:373
  31.5 5.4 %collective-permute-start.4 = (bf16[18,16,128]{2,1,0:T(8,128)(2,1)S(1)}, bf16[18,16,128]{2,1,0:T(8,128)(2,1)S(1)}, u32[]{:S(2)}, u32[]{:S(2)}) collective-permute-start(bf16[18,16,128]{2,1,0:T(8,128)(2,1)S(1)} %pad_maximum_fusion.15), channel_id=1, source_target_pairs={{0,8},{2,10},{4,12},{6,14},{8,0},{10,2},{12,4},{14,6},{16,24},{18,... | collective-permute-start | bytes 221192 | tf_op jit(solution)/shard_map/ppermute | solution.py:374
  37.3 18.9 %collective-permute-start.11 = (bf16[1120,128]{1,0:T(8,128)(2,1)S(1)}, bf16[1120,128]{1,0:T(8,128)(2,1)S(1)}, u32[]{:S(2)}, u32[]{:S(2)}) collective-permute-start(bf16[1120,128]{1,0:T(8,128)(2,1)S(1)} %constant_dynamic-update-slice_fusion), channel_id=1, source_target_pairs={{0,1},{1,0},{2,3},{3,2},{4,5},{5,4},{6,7},{7,6},{8,9},{9,8},{10,11... | collective-permute-start | bytes 860168 | tf_op jit(solution)/shard_map/ppermute | solution.py:386
  56.1 4.5 %collective-permute-start.5 = (f32[8,432,128]{2,1,0:T(8,128)}, f32[8,432,128]{2,1,0:T(8,128)S(1)}, u32[]{:S(2)}, u32[]{:S(2)}) collective-permute-start(f32[8,432,128]{2,1,0:T(8,128)} %get-tuple-element.28), channel_id=1, source_target_pairs={{0,2},{2,0},{4,6},{6,4},{8,10},{10,8},{12,14},{14,12},{16,18},{18,... | collective-permute-start | bytes 5308424 | tf_op jit(solution)/shard_map/ppermute | solution.py:258
  57.9 2.7 %copy-start = (f32[8,432,128]{2,1,0:T(8,128)S(1)}, f32[8,432,128]{2,1,0:T(8,128)}, u32[]{:S(2)}) copy-start(f32[8,432,128]{2,1,0:T(8,128)} %get-tuple-element.27) | copy-start | bytes 5308420
  57.9 2.6 %collective-permute-start.13 = (bf16[1728,128]{1,0:T(8,128)(2,1)S(1)}, bf16[1728,128]{1,0:T(8,128)(2,1)S(1)}, u32[]{:S(2)}, u32[]{:S(2)}) collective-permute-start(bf16[1728,128]{1,0:T(8,128)(2,1)S(1)} %collective-permute-done.12), channel_id=1, source_target_pairs={{0,2},{2,0},{4,6},{6,4},{8,10},{10,8},{12,14},{14,12},{16,18},{18,... | collective-permute-start | bytes 1327112 | tf_op jit(solution)/shard_map/ppermute | solution.py:258
  61.3 12.9 %collective-permute-start.6 = (f32[2,2,216,128]{3,2,1,0:T(8,128)S(1)}, f32[2,2,216,128]{3,2,1,0:T(8,128)S(1)}, u32[]{:S(2)}, u32[]{:S(2)}) collective-permute-start(f32[2,2,216,128]{3,2,1,0:T(8,128)S(1)} %get-tuple-element.30), channel_id=1, source_target_pairs={{0,4},{2,6},{4,0},{6,2},{8,12},{10,14},{12,8},{14,10},{16,20},{18,... | collective-permute-start | bytes 1327112 | tf_op jit(solution)/shard_map/ppermute | solution.py:258
  61.7 12.5 %collective-permute-start.7 = (f32[2,2,216,128]{3,2,1,0:T(8,128)S(1)}, f32[2,2,216,128]{3,2,1,0:T(8,128)S(1)}, u32[]{:S(2)}, u32[]{:S(2)}) collective-permute-start(f32[2,2,216,128]{3,2,1,0:T(8,128)S(1)} %get-tuple-element.31), channel_id=1, source_target_pairs={{0,8},{2,10},{4,12},{6,14},{8,0},{10,2},{12,4},{14,6},{16,24},{18,... | collective-permute-start | bytes 1327112 | tf_op jit(solution)/shard_map/ppermute | solution.py:258
  74.3 16.0 %collective-permute-start.8 = (f32[2,216,128]{2,1,0:T(8,128)S(1)}, f32[2,216,128]{2,1,0:T(8,128)S(1)}, u32[]{:S(2)}, u32[]{:S(2)}) collective-permute-start(f32[2,216,128]{2,1,0:T(8,128)S(1)} %get-tuple-element.34), channel_id=1, source_target_pairs={{0,8},{2,10},{4,12},{6,14},{8,0},{10,2},{12,4},{14,6},{16,24},{18,... | collective-permute-start | bytes 663560 | tf_op jit(solution)/shard_map/ppermute | solution.py:258
  76.3 14.0 %collective-permute-start.9 = (f32[2,216,128]{2,1,0:T(8,128)S(1)}, f32[2,216,128]{2,1,0:T(8,128)S(1)}, u32[]{:S(2)}, u32[]{:S(2)}) collective-permute-start(f32[2,216,128]{2,1,0:T(8,128)S(1)} %get-tuple-element.37), channel_id=1, source_target_pairs={{0,16},{2,18},{4,20},{6,22},{8,24},{10,26},{12,28},{14,30},{16,0},... | collective-permute-start | bytes 663560 | tf_op jit(solution)/shard_map/ppermute | solution.py:258
  90.3 4.8 %collective-permute-start.15 = (f32[216,128]{1,0:T(8,128)S(1)}, f32[216,128]{1,0:T(8,128)S(1)}, u32[]{:S(2)}, u32[]{:S(2)}) collective-permute-start(f32[216,128]{1,0:T(8,128)S(1)} %get-tuple-element.47), channel_id=1, source_target_pairs={{0,4},{2,6},{4,0},{6,2},{8,12},{10,14},{12,8},{14,10},{16,20},{18,... | collective-permute-start | bytes 331784 | tf_op jit(solution)/shard_map/ppermute | solution.py:258
  92.4 6.8 %collective-permute-start.14 = (f32[216,128]{1,0:T(8,128)S(1)}, f32[216,128]{1,0:T(8,128)S(1)}, u32[]{:S(2)}, u32[]{:S(2)}) collective-permute-start(f32[216,128]{1,0:T(8,128)S(1)} %get-tuple-element.43), channel_id=1, source_target_pairs={{0,16},{2,18},{4,20},{6,22},{8,24},{10,26},{12,28},{14,30},{16,0},... | collective-permute-start | bytes 331784 | tf_op jit(solution)/shard_map/ppermute | solution.py:258

commit v3 on v2

v3 whole, which is shorter than its diff:
```python
import functools
import math

import jax
import jax.numpy as jnp
from jax import lax
from jax.experimental import pallas as pl
from jax.experimental.pallas import tpu as pltpu
from jax.sharding import PartitionSpec as P

EDGE = 8
LAYERZ = 2
NBLK = 8
SPAN = 2 * EDGE
PLANE = SPAN * SPAN
HALF = 128
BF = jnp.bfloat16
F32 = jnp.float32

SHIFTS = [(a, b) for a in (-1, 0, 1) for b in (-1, 0, 1)]
PAIRS = [(0, 1), (2, 3), (4, 5), (6, 7), (8,)]


def locate_side(device_total):
    plane_side = 1
    for candidate in range(1, 33):
        if 2 * candidate**3 == device_total:
            plane_side = candidate
    return plane_side


VMEM_SPEC = pl.BlockSpec(memory_space=pltpu.VMEM)
SMEM_SPEC = pl.BlockSpec(memory_space=pltpu.SMEM)
HBM_SPEC = pl.BlockSpec(memory_space=pltpu.HBM)
ANY_SPEC = pl.BlockSpec(memory_space=pl.ANY)
TAPS = 14
COST = pl.CostEstimate(flops=1, bytes_accessed=1, transcendentals=0)
MARK = jax.ShapeDtypeStruct((8, HALF), F32)


def faces_kernel(place_ref, list_ref, count_ref, raw_ref, occ_ref, mask_ref, sa_ref, sb_ref, xf_ref, yf_ref):
    even, px, py = place_ref[0], place_ref[1], place_ref[2]
    count = count_ref[0]
    x_at = lax.broadcasted_iota(jnp.int32, (SPAN, PLANE), 0)
    q_at = lax.broadcasted_iota(jnp.int32, (SPAN, PLANE), 1)
    y_at, z_at = q_at // SPAN, q_at % SPAN
    block = (x_at // EDGE) * (2 * LAYERZ) + (y_at // EDGE) * LAYERZ + z_at // EDGE
    active = jnp.zeros((SPAN, PLANE), F32)
    for j in range(NBLK):
        live = jnp.where(j < count, 1.0, 0.0).astype(F32)
        active += jnp.where(block == list_ref[0, j], live, 0.0)
    mask_ref[...] = active * occ_ref[...].astype(F32)

    za = jnp.where(even == 1, SPAN - 1, 0)
    row = lax.broadcasted_iota(jnp.int32, (3 * SPAN, PLANE), 0)
    col = lax.broadcasted_iota(jnp.int32, (3 * SPAN, PLANE), 1)
    kind, at = row // SPAN, row % SPAN
    depth = jnp.where(kind == 0, za, SPAN - 1 - za)
    target = jnp.where(kind == 2, py * SPAN + at, at * SPAN + depth)
    chosen = (col == target).astype(F32)
    for x in range(SPAN):
        left = (chosen * mask_ref[x : x + 1, :]).astype(BF)
        got = jnp.dot(left, raw_ref[x * PLANE : (x + 1) * PLANE, :], preferred_element_type=F32)
        got = got.astype(BF)
        sa_ref[x] = got[0:SPAN]
        sb_ref[x] = got[SPAN : 2 * SPAN]
        yf_ref[x] = got[2 * SPAN :]
    row = lax.broadcasted_iota(jnp.int32, (PLANE, PLANE), 0)
    col = lax.broadcasted_iota(jnp.int32, (PLANE, PLANE), 1)
    left = ((row == col).astype(F32) * mask_ref[pl.ds(px, 1), :]).astype(BF)
    plane = raw_ref[pl.ds(pl.multiple_of(px * PLANE, PLANE), PLANE), :]
    got = jnp.dot(left, plane, preferred_element_type=F32).astype(BF)
    xf_ref[...] = got.reshape(SPAN, SPAN, HALF)


def faces(place, block_list, block_count, raw, occupancy):
    face = jax.ShapeDtypeStruct((SPAN, SPAN, HALF), BF)
    return pl.pallas_call(
        faces_kernel,
        out_shape=(jax.ShapeDtypeStruct((SPAN, PLANE), F32), face, face, face, face),
        in_specs=[SMEM_SPEC] * 3 + [VMEM_SPEC] * 2,
        out_specs=(VMEM_SPEC,) * 5,
        compiler_params=pltpu.CompilerParams(vmem_limit_bytes=12 << 20),
        cost_estimate=COST,
        name="faces",
    )(place, block_list, block_count, raw, occupancy.reshape(SPAN, PLANE))


def edges_kernel(
    place_ref, fa_ref, fb_ref, xf_ref, yf_ref, w_ref, _, zl_ref, zh_ref, xs_ref, ys_ref, es_ref, part_ref, sem
):
    even, px, py = place_ref[0], place_ref[1], place_ref[2]
    copy = pltpu.make_async_copy(
        w_ref.at[pl.ds(place_ref[3], part_ref.shape[0]), pl.ds(pl.multiple_of(place_ref[4], HALF), HALF)],
        part_ref,
        sem,
    )
    copy.start()

    @pl.when(even == 1)
    def _():
        zl_ref[...] = fb_ref[...]
        zh_ref[...] = fa_ref[...]

    @pl.when(even == 0)
    def _():
        zl_ref[...] = fa_ref[...]
        zh_ref[...] = fb_ref[...]

    xs_ref[0:SPAN] = xf_ref[...]
    ys_ref[0:SPAN] = yf_ref[...]
    es_ref[0:SPAN, :] = yf_ref[pl.ds(px, 1)].reshape(SPAN, HALF)
    row = lax.broadcasted_iota(jnp.int32, (2 * SPAN, PLANE), 0)
    col = lax.broadcasted_iota(jnp.int32, (2 * SPAN, PLANE), 1)
    total = None
    for k, ref in enumerate((zl_ref, zh_ref)):
        xs_ref[SPAN + k] = ref[pl.ds(px, 1)].reshape(SPAN, HALF)
        target = jnp.where(
            row < SPAN, row * SPAN + py, jnp.where(row == SPAN + k, px * SPAN + py, -1)
        )
        left = (col == target).astype(F32).astype(BF)
        got = jnp.dot(left, ref[...].reshape(PLANE, HALF), preferred_element_type=F32)
        ys_ref[SPAN + k] = got[0:SPAN].astype(BF)
        total = got[SPAN:] if total is None else total + got[SPAN:]
    es_ref[SPAN:, :] = total.astype(BF)
    copy.wait()


def edges(place, from_a, from_b, xf, yf, weights, mark):
    face = jax.ShapeDtypeStruct((SPAN, SPAN, HALF), BF)
    strip = jax.ShapeDtypeStruct((SPAN + 2, SPAN, HALF), BF)
    corner = jax.ShapeDtypeStruct((2 * SPAN, HALF), BF)
    return pl.pallas_call(
        edges_kernel,
        out_shape=(
            face, face, strip, strip, corner,
            jax.ShapeDtypeStruct((TAPS, HALF, HALF), BF),
        ),
        in_specs=[SMEM_SPEC] + [VMEM_SPEC] * 4 + [HBM_SPEC, ANY_SPEC],
        out_specs=(VMEM_SPEC,) * 5 + (HBM_SPEC,),
        scratch_shapes=[pltpu.SemaphoreType.DMA],
        compiler_params=pltpu.CompilerParams(vmem_limit_bytes=8 << 20),
        cost_estimate=COST,
        name="edges",
    )(place, from_a, from_b, xf, yf, weights, mark)

def keep_column(mask_ref, x):
    return jnp.broadcast_to(mask_ref[x : x + 1, :], (8, PLANE)).T[:, 0:1]


def unpack(place_ref, flat_ref, gp_ref, zp_ref):
    cx, cy = place_ref[6], place_ref[7]
    near_x, far_x = (SPAN + 1) * (1 - cx), (SPAN + 1) * cx
    near_y, far_y = (SPAN + 1) * (1 - cy), (SPAN + 1) * cy
    n = (SPAN + 2) * SPAN
    zero = jnp.zeros((SPAN, HALF), BF)

    def rows(first, count=SPAN):
        return flat_ref[first : first + count, :]

    for x in range(SPAN + 2):
        gp_ref[far_x, x] = zero
        gp_ref[x, far_y] = zero
    for y in range(SPAN):
        gp_ref[near_x, y + 1] = rows(y * SPAN)
        gp_ref[y + 1, near_y] = rows(n + y * SPAN)
    gp_ref[near_x, far_y] = zero
    gp_ref[near_x, near_y] = rows(2 * n + 2 * PLANE)
    place = lax.broadcasted_iota(jnp.int32, (SPAN, SPAN, HALF), 1)
    single = lax.broadcasted_iota(jnp.int32, (SPAN, HALF), 0)
    for side in range(2):
        face = rows(2 * n + side * PLANE, PLANE).astype(F32).reshape(SPAN, SPAN, HALF)
        strip = rows(n + (SPAN + side) * SPAN).astype(F32)
        x_row = rows((SPAN + side) * SPAN).astype(F32)
        corner = flat_ref[2 * n + 2 * PLANE + SPAN :, :].astype(F32)[side : side + 1, :]
        low, high = (jnp.where(cy == want, strip, 0.0).reshape(SPAN, 1, HALF) for want in (1, 0))
        c_low, c_high = (jnp.where(cy == want, corner, 0.0) for want in (1, 0))
        moved = [
            jnp.where(place == SPAN - 1, high, jnp.roll(face, -1, 1)),
            face,
            jnp.where(place == 0, low, jnp.roll(face, 1, 1)),
        ]
        moved_row = [
            jnp.where(single == SPAN - 1, c_high, jnp.roll(x_row, -1, 0)),
            x_row,
            jnp.where(single == 0, c_low, jnp.roll(x_row, 1, 0)),
        ]
        for b in range(3):
            zp_ref[side, b, 1 : 1 + SPAN] = moved[b].astype(BF)
            zp_ref[side, b, far_x] = zero
            zp_ref[side, b, near_x] = moved_row[b].astype(BF)


def assemble(raw_refs, mask_ref, yb_ref, gp_ref):
    each = SPAN // len(raw_refs)
    for x in range(SPAN):
        rows = slice(x % each * PLANE, (x % each + 1) * PLANE)
        block = raw_refs[x // each][rows, :].astype(F32) * keep_column(mask_ref, x)
        gp_ref[x + 1, 1 : 1 + SPAN] = block.astype(BF).reshape(SPAN, SPAN, HALF)
        if yb_ref is not None:
            gp_ref[x + 1, 0] = yb_ref[0, x]
            gp_ref[x + 1, SPAN + 1] = yb_ref[1, x]


def load_features(feat_ref, mask_ref, f_ref, rims):
    cin = feat_ref.shape[1]
    src = lax.broadcasted_iota(jnp.int32, (PLANE, 3 * PLANE), 0)
    col = lax.broadcasted_iota(jnp.int32, (PLANE, 3 * PLANE), 1)
    dst = col % PLANE
    at = dst % SPAN + col // PLANE - 1
    shift = (at >= 0) & (at < SPAN) & (src == dst // SPAN * SPAN + at)
    shift = shift.astype(F32).astype(BF)

    def spread(block, *outs):
        moved = jnp.dot(block, shift, preferred_element_type=F32).astype(BF)
        for ref, cols in outs:
            ref[0:cin, cols] = moved[:, 0:PLANE]
            ref[cin : 2 * cin, cols] = block
            ref[2 * cin :, cols] = moved[:, 2 * PLANE :]

    row = lax.broadcasted_iota(jnp.int32, (4 * SPAN, PLANE), 0)
    pos = lax.broadcasted_iota(jnp.int32, (4 * SPAN, PLANE), 1)
    kind, r = row // SPAN, row % SPAN
    target = jnp.where(kind < 2, kind * (PLANE - SPAN) + r, r * SPAN + (kind - 2) * (SPAN - 1))
    chosen = (pos == target).astype(F32)
    found = []
    whole = slice(0, PLANE)
    for x in range(SPAN):
        cols = slice(x * PLANE, (x + 1) * PLANE)
        plane = feat_ref[cols, :]
        mask = mask_ref[x : x + 1, :]
        outs = [(f_ref, cols)]
        if rims and x in (0, SPAN - 1):
            outs.append((rims[0].at[x % 2], whole))
        spread((plane.T.astype(F32) * mask).astype(BF), *outs)
        if rims:
            left = (chosen * mask).astype(BF)
            found.append(jnp.dot(left, plane, preferred_element_type=F32))
    if rims:
        for side in range(2):
            rim = [v[side * SPAN : (side + 1) * SPAN] for v in found]
            spread(jnp.concatenate(rim, axis=0).astype(BF).T, (rims[1].at[side], whole))
            rim = [v[(side + 2) * SPAN : (side + 3) * SPAN] for v in found]
            rims[2][side] = jnp.concatenate(rim, axis=0).astype(BF).T


def inner_kernel(feat_ref, raw_ref, mask_ref, *refs, pairs, ignored):
    out_ref, mark_ref, *rims, f_ref, gp_ref, hold_ref, sems = refs[ignored:]
    cin = feat_ref.shape[1]
    copies = []

    def leave(source, target):
        copy = pltpu.make_async_copy(source, target, sems.at[len(copies)])
        copy.start()
        copies.append(copy)

    if rims:
        held = rims[3:]
        load_features(feat_ref, mask_ref, f_ref, held)
    else:
        load_features(feat_ref, mask_ref, f_ref, ())
    zero = jnp.zeros((SPAN, HALF), BF)
    for y in range(SPAN + 2):
        gp_ref[0, y] = zero
        gp_ref[SPAN + 1, y] = zero
    for x in range(SPAN):
        block = raw_ref[x * PLANE : (x + 1) * PLANE, :].astype(F32) * keep_column(mask_ref, x)
        gp_ref[x + 1, 1 : 1 + SPAN] = block.astype(BF).reshape(SPAN, SPAN, HALF)
        gp_ref[x + 1, 0] = zero
        gp_ref[x + 1, SPAN + 1] = zero

    def source(shift):
        a, b = SHIFTS[shift]
        block = gp_ref[1 - a : 1 - a + SPAN, 1 - b : 1 - b + SPAN]
        return block.reshape(SPAN * PLANE, HALF)

    mark_ref[...] = jnp.zeros_like(mark_ref)
    for pair in pairs:
        right = jnp.concatenate([source(s) for s in pair], axis=1)
        acc = jnp.dot(f_ref[...], right, preferred_element_type=F32)
        for c in range(3):
            for k, s in enumerate(pair):
                tap = 3 * (s - pairs[0][0]) + c
                hold_ref[tap] = acc[c * cin : (c + 1) * cin, HALF * k : HALF * (k + 1)]
    leave(hold_ref, out_ref)
    if rims:
        for source, target in zip(held, rims[:3]):
            leave(source, target)
    for copy in copies:
        copy.wait()


def weight_grad_inner(features, raw, mask_rows, pairs, with_rims, *ahead):
    cells, cin = features.shape
    taps = 3 * sum(len(pair) for pair in pairs)
    outs = [jax.ShapeDtypeStruct((taps, cin, HALF), F32), MARK]
    held = []
    if with_rims:
        held = [(2, 3 * cin, PLANE), (2, 3 * cin, PLANE), (2, cin, PLANE)]
        outs += [jax.ShapeDtypeStruct(shape, BF) for shape in held]
    return pl.pallas_call(
        functools.partial(inner_kernel, pairs=pairs, ignored=len(ahead)),
        out_shape=tuple(outs),
        in_specs=[VMEM_SPEC] * 3 + [ANY_SPEC] * len(ahead),
        out_specs=(HBM_SPEC, VMEM_SPEC) + (HBM_SPEC,) * len(held),
        scratch_shapes=[pltpu.VMEM(shape, BF) for shape in held]
        + [
            pltpu.VMEM((3 * cin, cells), BF),
            pltpu.VMEM((SPAN + 2, SPAN + 2, SPAN, HALF), BF),
            pltpu.VMEM((taps, cin, HALF), F32),
            pltpu.SemaphoreType.DMA((len(held) + 1,)),
        ],
        compiler_params=pltpu.CompilerParams(vmem_limit_bytes=28 << 20),
        cost_estimate=COST,
        name="weight_inner",
    )(features, raw, mask_rows, *ahead)


def rim_kernel(
    mine_ref, fx_ref, fy_ref, fz_ref, xb_ref, yb_ref, zp_ref, part_a_ref, part_b_ref,
    *refs, scale, pieces, ignored
):
    parts, refs = refs[:pieces], refs[pieces + ignored :]
    keep_ref, send_ref, *flat_refs, acc_ref, sems = refs
    at = 0
    for ref in parts:
        for block in range(ref.shape[0] if len(ref.shape) == 3 else 1):
            value = ref[block] if len(ref.shape) == 3 else ref[...]
            flat_refs[0][at : at + value.shape[0], :] = value
            at += value.shape[0]
    cin = fz_ref.shape[1]
    rows = acc_ref.shape[2]
    zero = jnp.zeros((1, SPAN, HALF), BF)
    more = {}

    def add(shift, c, value):
        more.setdefault(3 * shift + c, []).append(value)

    for side in range(2):
        first = 6 if side == 0 else 0
        right = jnp.concatenate(
            [xb_ref[side, 1 - b : 1 - b + SPAN].reshape(PLANE, HALF) for b in (-1, 0, 1)], axis=1
        )
        got = jnp.dot(fx_ref[side], right, preferred_element_type=F32)
        for b in range(3):
            for c in range(3):
                add(first + b, c, got[c * cin : (c + 1) * cin, b * HALF : (b + 1) * HALF])
        strip = jnp.concatenate([zero, yb_ref[side], zero], axis=0)
        right = jnp.concatenate(
            [strip[1 - a : 1 - a + SPAN].reshape(PLANE, HALF) for a in (-1, 0, 1)], axis=1
        )
        got = jnp.dot(fy_ref[side], right, preferred_element_type=F32)
        for a in range(3):
            for c in range(3):
                shift = 3 * a + (2 if side == 0 else 0)
                add(shift, c, got[c * cin : (c + 1) * cin, a * HALF : (a + 1) * HALF])
        for pair in PAIRS:
            cols = []
            for s in pair:
                a, b = SHIFTS[s]
                cols.append(zp_ref[side, b + 1, 1 - a : 1 - a + SPAN].reshape(PLANE, HALF))
            got = jnp.dot(
                fz_ref[side], jnp.concatenate(cols, axis=1), preferred_element_type=F32
            )
            for k, s in enumerate(pair):
                add(s, 2 if side == 0 else 0, got[:, k * HALF : (k + 1) * HALF])

    for tap in range(27):
        taps_a = part_a_ref.shape[0]
        value = part_a_ref[tap] if tap < taps_a else part_b_ref[tap - taps_a]
        for extra in more.get(tap, []):
            value = value + extra
        value = value * scale
        first = tap * cin
        while first < (tap + 1) * cin:
            block, at = divmod(first, rows)
            count = min(rows - at, (tap + 1) * cin - first)
            piece = value[first - tap * cin : first - tap * cin + count]
            acc_ref[block % 2, block // 2, at : at + count] = piece
            first += count

    mine = mine_ref[0]
    out_send = pltpu.make_async_copy(acc_ref.at[1 - mine], send_ref, sems.at[0])
    out_keep = pltpu.make_async_copy(acc_ref.at[mine], keep_ref, sems.at[1])
    out_send.start()
    out_keep.start()
    out_send.wait()
    out_keep.wait()


def weight_grad_rim(mine, fx, fy, fz, borders, inner_a, inner_b, scale, total, pieces, *ahead):
    cin = fz.shape[1]
    rows = 27 * cin // total
    outs = [jax.ShapeDtypeStruct((total // 2, rows, HALF), F32)] * 2
    if pieces:
        length = sum(v.size for v in pieces) // HALF
        outs.append(jax.ShapeDtypeStruct((length, HALF), BF))
    return pl.pallas_call(
        functools.partial(rim_kernel, scale=scale, pieces=len(pieces), ignored=len(ahead)),
        out_shape=tuple(outs),
        in_specs=[SMEM_SPEC] + [VMEM_SPEC] * (8 + len(pieces)) + [ANY_SPEC] * len(ahead),
        out_specs=(ANY_SPEC, ANY_SPEC) + (VMEM_SPEC,) * (len(outs) - 2),
        scratch_shapes=[
            pltpu.VMEM((2, total // 2, rows, HALF), F32),
            pltpu.SemaphoreType.DMA((2,)),
        ],
        compiler_params=pltpu.CompilerParams(vmem_limit_bytes=24 << 20),
        cost_estimate=COST,
        name="weight_rim",
    )(mine, fx, fy, fz, *borders, inner_a, inner_b, *pieces, *ahead)


def data_kernel(place_ref, mask_ref, *refs, borders, ignored, last):
    around, refs = refs[:borders], refs[borders:]
    *refs, z_ref = refs
    if last:
        *raw_refs, wa_ref, wb_ref, prev_ref = refs[:5]
        out_ref, mark_ref, gp_ref, wt_ref, h_ref = refs[5 + ignored :]
        first_core = place_ref[0] == 1

        def tile_of(tap):
            low = min(tap, TAPS - 1)
            high = max(tap - (27 - TAPS), 0)
            if tap < 27 - TAPS:
                return jnp.where(first_core, wa_ref[low], wb_ref[low])
            if tap >= TAPS:
                return jnp.where(first_core, wb_ref[high], wa_ref[high])
            return jnp.where(first_core, wa_ref[low], wa_ref[high])
    else:
        raw_ref, whole_ref = refs[:2]
        out_ref, mark_ref, gp_ref, wt_ref, h_ref, w_ref, sem = refs[2 + ignored :]
        raw_refs, prev_ref = [raw_ref], None
        copy = pltpu.make_async_copy(whole_ref.at[:, pl.ds(pl.multiple_of(place_ref[5], HALF), HALF)], w_ref, sem)
        copy.start()

        def tile_of(tap):
            return w_ref[tap]

    mark_ref[...] = jnp.zeros_like(mark_ref)
    if borders == 1:
        zp_ref = z_ref
        unpack(place_ref, around[0], gp_ref, zp_ref)
        assemble(raw_refs, mask_ref, None, gp_ref)
    else:
        xb_ref, yb_ref, zp_ref = around
        gp_ref[0] = xb_ref[0]
        gp_ref[SPAN + 1] = xb_ref[1]
        assemble(raw_refs, mask_ref, yb_ref, gp_ref)
    if not last:
        copy.wait()
    for s in range(9):
        for c in range(3):
            tile = tile_of(3 * s + c).astype(F32).T.astype(BF)
            wt_ref[s * HALF : (s + 1) * HALF, c * HALF : (c + 1) * HALF] = tile

    for side, c in ((0, 2), (1, 0)):
        cols = []
        for s in range(9):
            a, b = SHIFTS[s]
            cols.append(zp_ref[side, b + 1, 1 - a : 1 - a + SPAN].reshape(PLANE, HALF))
        h_ref[side] = jnp.dot(
            jnp.concatenate(cols, axis=1),
            wt_ref[:, c * HALF : (c + 1) * HALF],
            preferred_element_type=F32,
        ).reshape(SPAN, SPAN, HALF)

    zpos = lax.broadcasted_iota(jnp.int32, (SPAN, SPAN, HALF), 1)

    def plane(x, _):
        cols = []
        for s in range(9):
            a, b = SHIFTS[s]
            block = gp_ref[pl.ds(x + 1 - a, 1), 1 - b : 1 - b + SPAN]
            cols.append(block.reshape(PLANE, HALF))
        prod = jnp.dot(jnp.concatenate(cols, axis=1), wt_ref[...], preferred_element_type=F32)
        down = pltpu.roll(prod[:, 0:HALF], PLANE - 1, 0).reshape(SPAN, SPAN, HALF)
        mid = prod[:, HALF : 2 * HALF].reshape(SPAN, SPAN, HALF)
        up = pltpu.roll(prod[:, 2 * HALF :], 1, 0).reshape(SPAN, SPAN, HALF)
        low = h_ref[0, pl.ds(x, 1)].reshape(SPAN, 1, HALF)
        high = h_ref[1, pl.ds(x, 1)].reshape(SPAN, 1, HALF)
        full = mid + jnp.where(zpos == 0, low, up) + jnp.where(zpos == SPAN - 1, high, down)
        full = full.reshape(PLANE, HALF)
        rows = pl.ds(pl.multiple_of(x * PLANE, PLANE), PLANE)
        if prev_ref is None:
            out_ref[rows, :] = full
        else:
            keep = jnp.broadcast_to(mask_ref[pl.ds(x, 1), :], (8, PLANE)).T[:, 0:1]
            out_ref[rows, :] = ((full + prev_ref[rows, :]) * keep).astype(BF)
        return 0

    lax.fori_loop(0, SPAN, plane, 0, unroll=4)


def data_grad_local(place, mask_rows, borders, operands, last, *ahead):
    scratch = [
        pltpu.VMEM((SPAN + 2, SPAN + 2, SPAN, HALF), BF),
        pltpu.VMEM((9 * HALF, 3 * HALF), BF),
        pltpu.VMEM((2, SPAN, SPAN, HALF), F32),
    ]
    specs = [VMEM_SPEC] * len(operands)
    if not last:
        specs[-1] = HBM_SPEC
        scratch += [pltpu.VMEM((27, HALF, HALF), BF), pltpu.SemaphoreType.DMA]
    scratch.append(pltpu.VMEM((2, 3, SPAN + 2, SPAN, HALF), BF))
    return pl.pallas_call(
        functools.partial(
            data_kernel, borders=len(borders), ignored=len(ahead), last=last
        ),
        out_shape=(
            jax.ShapeDtypeStruct((SPAN * PLANE, HALF), BF if last else F32),
            MARK,
        ),
        in_specs=[SMEM_SPEC] + [VMEM_SPEC] * (1 + len(borders)) + specs + [ANY_SPEC] * len(ahead),
        out_specs=(VMEM_SPEC, VMEM_SPEC),
        scratch_shapes=scratch,
        compiler_params=pltpu.CompilerParams(vmem_limit_bytes=20 << 20),
        cost_estimate=COST,
        name="data_grad",
    )(place, mask_rows, *borders, *operands, *ahead)


def split_kernel(bits_ref, keep_ref, recv_ref, *outs, bounds, ignored):
    outs = outs[ignored:]
    for k, (low, high, lead) in enumerate(bounds):
        stay_ref, go_ref = outs[2 * k], outs[2 * k + 1]
        shape = keep_ref.shape
        mine = bits_ref[k]
        before = math.prod(shape[:lead])
        for ref, bit in ((stay_ref, mine), (go_ref, 1 - mine)):
            for i in range(before):
                at = []
                for size in reversed(shape[:lead]):
                    i, rest = divmod(i, size)
                    at.insert(0, rest)
                at = tuple(at)
                tail = (slice(None),) * (len(shape) - 3 - lead)
                src = at + (bit,) + tail + (slice(low, high),)
                ref[at] = keep_ref[src] + recv_ref[src]


def split(keep, recv, bits, bounds, *ahead):
    outs = []
    for low, high, lead in bounds:
        shape = keep.shape[:lead] + keep.shape[lead + 1 : -2] + (high - low, HALF)
        outs += [jax.ShapeDtypeStruct(shape, F32)] * 2
    return pl.pallas_call(
        functools.partial(split_kernel, bounds=bounds, ignored=len(ahead)),
        out_shape=tuple(outs),
        in_specs=[SMEM_SPEC, VMEM_SPEC, VMEM_SPEC] + [ANY_SPEC] * len(ahead),
        out_specs=tuple(VMEM_SPEC for _ in outs),
        compiler_params=pltpu.CompilerParams(vmem_limit_bytes=12 << 20),
        cost_estimate=COST,
        name="add_split",
    )(jnp.stack(bits), keep, recv, *ahead)


def swap_bit(block, bit, total):
    return lax.ppermute(block, "space", [(i, i ^ (1 << bit)) for i in range(total)])


def bit_of(index, bit):
    return (index // (1 << bit) % 2).astype(jnp.int32)


def extend(block, dim, stride, coords, side):
    total = lax.axis_size("space")
    length = block.shape[dim]
    first = lax.slice_in_dim(block, 0, 1, axis=dim)
    last = lax.slice_in_dim(block, length - 1, length, axis=dim)
    below = lax.ppermute(
        last, "space", [(i, i + stride) for i in range(total) if coords(i) < side - 1]
    )
    above = lax.ppermute(
        first, "space", [(i + stride, i) for i in range(total) if coords(i) < side - 1]
    )
    return jnp.concatenate([below, block, above], axis=dim)


def turned(face):
    return jnp.stack([face[:, 1 - b : 1 - b + SPAN] for b in (-1, 0, 1)])


def wide_borders(masked, zl, zh, plane_side, depth):
    block = jnp.concatenate([zl[:, :, None], masked, zh[:, :, None]], axis=2)
    block = extend(block, 1, depth, lambda i: i // depth % plane_side, plane_side)
    block = extend(block, 0, depth * plane_side, lambda i: i // (depth * plane_side), plane_side)
    inner = block[:, :, 1 : 1 + SPAN]
    xb = jnp.stack([inner[0], inner[SPAN + 1]])
    yb = jnp.stack([inner[1 : 1 + SPAN, 0], inner[1 : 1 + SPAN, SPAN + 1]])
    zp = jnp.stack([turned(block[:, :, 0]), turned(block[:, :, SPAN + 1])])
    return xb, yb, zp


def pair_borders(cx, cy, xh, yh, eh, zl, zh):
    def both(value, coord, axis):
        zero = jnp.zeros_like(value)
        low = jnp.where(coord == 1, value, zero)
        high = jnp.where(coord == 0, value, zero)
        return jnp.expand_dims(low, axis), jnp.expand_dims(high, axis)

    def around(values, corner, axis):
        low, high = both(corner, cy, axis)
        return jnp.concatenate([low, values, high], axis=axis)

    xb = jnp.concatenate(both(around(xh[:SPAN], eh[:SPAN], 0), cx, 0))
    yb = jnp.concatenate(both(yh[:SPAN], cy, 0))

    def face(z, k):
        rows = around(z, yh[k], 1)
        low, high = both(around(xh[k], eh[k], 0), cx, 0)
        return turned(jnp.concatenate([low, rows, high], axis=0))

    zp = jnp.stack([face(zl, SPAN), face(zh, SPAN + 1)])
    return xb, yb, zp


def body(features, grad_out, weights, occupancy, block_list, block_count):
    total = lax.axis_size("space")
    plane_side = locate_side(total)
    depth = 2 * plane_side
    cells, cin = features.shape
    index = lax.axis_index("space")
    column = lax.axis_index("chan")
    swap = [(0, 1), (1, 0)]
    cx = index // (plane_side * depth)
    cy = index // depth % plane_side
    even = index % 2 == 0

    core = bit_of(index, 0)
    place = jnp.stack(
        [
            (index + 1) % 2,
            jnp.where(cx == 0, SPAN - 1, 0),
            jnp.where(cy == 0, SPAN - 1, 0),
            core * (27 - TAPS),
            (1 - column) * HALF,
            column * HALF,
            cx,
            cy,
        ]
    ).astype(jnp.int32)
    mask_rows, send_a, send_b, xf, yf = faces(
        place, block_list, block_count, grad_out, occupancy
    )

    inside = [i for i in range(total) if i % depth % 2 == 1 and i % depth < depth - 1]
    second = [(i, i + 1) for i in inside] + [(i + 1, i) for i in inside]
    from_a = swap_bit(send_a, 0, total)
    from_b = lax.ppermute(send_b, "space", second)

    half_rows = cells // 2
    other_raw = [
        lax.ppermute(grad_out[k * half_rows : (k + 1) * half_rows], "chan", swap)
        for k in range(2)
    ]
    inner_a, mark, fx, fy, fz = weight_grad_inner(
        features, grad_out, mask_rows, PAIRS[:2], True
    )
    scale = 1.0 / math.sqrt(cells * total)
    if plane_side == 2:
        sx, sy = 2 * depth, depth
        zl, zh, xs, ys, es, part = edges(place, from_a, from_b, xf, yf, weights, mark)
        xh = lax.ppermute(xs, "space", [(i, i ^ sx) for i in range(total)])
        yh = lax.ppermute(ys, "space", [(i, i ^ sy) for i in range(total)])
        eh = lax.ppermute(es, "space", [(i, i ^ sx ^ sy) for i in range(total)])
        inner_b, _ = weight_grad_inner(
            features, grad_out, mask_rows, PAIRS[2:], False, es
        )
        borders = pair_borders(cx, cy, xh, yh, eh, zl, zh)
        keep, send, flat = weight_grad_rim(
            core[None], fx, fy, fz, borders, inner_a, inner_b, scale, total,
            (xh, yh, zl, zh, eh), other_raw[0],
        )
        borders = (flat,)
        other_borders = (lax.ppermute(flat, "chan", swap),)
    else:
        cube = grad_out.reshape(SPAN, SPAN, SPAN, HALF)
        mask = mask_rows.astype(BF).reshape(SPAN, SPAN, SPAN, 1)
        zl = jnp.where(even, from_b, from_a)
        zh = jnp.where(even, from_a, from_b)
        borders = wide_borders(cube * mask, zl, zh, plane_side, depth)
        inner_b, _ = weight_grad_inner(features, grad_out, mask_rows, PAIRS[2:], False)
        keep, send = weight_grad_rim(
            core[None], fx, fy, fz, borders, inner_a, inner_b, scale, total, ()
        )
        other_borders = tuple(lax.ppermute(v, "chan", swap) for v in borders)
        part = lax.dynamic_slice(weights, (place[3], place[4], 0), (TAPS, HALF, HALF))

    part = lax.ppermute(part, "chan", swap)
    part_b = swap_bit(part, 0, total)
    recv = swap_bit(send, 0, total)

    bits = total.bit_length() - 1
    rows = keep.shape[1]
    cut = rows // 2
    keep = keep.reshape((2,) * (bits - 1) + (rows, HALF))
    recv = recv.reshape(keep.shape)
    orders = [list(range(1, bits)), list(range(2, bits)) + [1]]
    have = [list(range(bits - 1, 0, -1)) for _ in orders]
    bounds = [
        (0, cut, have[0].index(orders[0][0])),
        (cut, rows, have[1].index(orders[1][0])),
    ]
    stay1, go1, stay2, go2 = split(
        keep, recv, [bit_of(index, order[0]) for order in orders], bounds
    )
    stays, gos = [stay1, stay2], [go1, go2]
    partial_out = None
    for step in range(bits - 1):
        got = [swap_bit(go, order[step], total) for go, order in zip(gos, orders)]
        ahead = ()
        if step == 0:
            partial_out, mark = data_grad_local(
                place, mask_rows, borders, (grad_out, weights), False, *gos
            )
            ahead = (mark, other_raw[1])
        if step == 1:
            data_out, mark = data_grad_local(
                place, mask_rows, other_borders,
                (*other_raw, part, part_b, partial_out), True, *gos,
            )
            ahead = (mark,)
        if step == bits - 2:
            weight_out = jnp.concatenate([s + g for s, g in zip(stays, got)], axis=0)
            break
        for k, order in enumerate(orders):
            have[k].remove(order[step])
            nxt = order[step + 1]
            stays[k], gos[k] = split(
                stays[k],
                got[k],
                [bit_of(index, nxt)],
                [(0, stays[k].shape[-2], have[k].index(nxt))],
                *ahead,
            )
    return data_out, weight_out

def solution(mesh):
    placed = (
        P("space", None),
        P("space", "chan"),
        P(None, None, "chan"),
        P("space"),
        P("space", None),
        P("space"),
    )
    return jax.shard_map(
        body,
        mesh=mesh,
        in_specs=placed,
        out_specs=(P("space", "chan"), P("space", "chan")),
        check_vma=False,
    )
```

time: 100 us -> 92.2 us (0.922)
  other arithmetic: 11.9 us -> 1.11 us
  local copies, waits for them, and re-layouts: 6.65 us -> 14 us
  Pallas kernels: 46.8 us -> 41.8 us
  waiting for transfers between devices: 11.4 us -> 13 us
  starting transfers between devices: 21.2 us -> 20 us
    unnamed x11 -> x46, local copies, waits for them, and re-layouts: 0.07 us -> 12 us
    pallas_call x9 -> x12, Pallas kernels: 46.8 us -> 41.8 us  [the longest x2 19.4 us: data_grad_local(): pl.pallas_call(functools.partial(data_kernel, borders=len(borders), ignor...]
    ppermute x4 -> x5, waiting for transfers between devices: 0.01 us -> 3.36 us  [the longest x2 1.75 us: body(): lax.ppermute(grad_out[k * half_rows:(k + 1) * half_rows], 'chan', swap)]
    ppermute x9, waiting for transfers between devices: 6.83 us -> 4.15 us  [swap_bit(): lax.ppermute(block, 'space', [(i, i ^ 1 << bit) for i in range(total)])]
    slice x4 -> x1, local copies, waits for them, and re-layouts: 3.62 us -> 1.06 us  [body(): grad_out[k * half_rows:(k + 1) * half_rows]]
    mul x5 -> x0, other arithmetic: 1.88 us -> none  [the longest x1 0.98 us: body(): yf = at(cube, 1, cy) * at(mask, 1, cy)]
    ppermute x1, waiting for transfers between devices: 0.01 us -> 1.88 us  [body(): xh = lax.ppermute(xs, 'space', [(i, i ^ sx) for i in range(total)])]
    another operation x6 -> x3, other arithmetic: 1.72 us -> 0.1 us  [pair_borders(): zp = jnp.stack([face(zl, SPAN), face(zh, SPAN + 1)])]
  transfers between devices with their start and end apart: 16 -> 17, of which waited for: 5 -> 8; matrix products, arithmetic and copies ran while one was open for 18% -> 2% of each run, Pallas kernels for 47% -> 39%
where the time goes in v3:
time: 92.2 us; the launch traced here: 91.7 us
  Pallas kernels  41.8 us (45%)
  starting transfers between devices  20 us (22%)
  local copies, waits for them, and re-layouts  14 us (15%)
  waiting for transfers between devices  13 us (14%)
  between operations  1.76 us (2%)
  other arithmetic  1.11 us (1%)
    pallas_call x2, Pallas kernels, data_grad_local(): pl.pallas_call(functools.partial(data_kernel, borders=len(borders), ignor...  19.4 us
    pallas_call x2, Pallas kernels, weight_grad_inner(): pl.pallas_call(functools.partial(inner_kernel, pairs=pairs, ignored=len(a...  12.9 us
    unnamed x46, local copies, waits for them, and re-layouts  12 us
    ppermute x9, starting transfers between devices, swap_bit(): lax.ppermute(block, 'space', [(i, i ^ 1 << bit) for i in range(total)])  9.74 us
    ppermute x1, starting transfers between devices, body(): eh = lax.ppermute(es, 'space', [(i, i ^ sx ^ sy) for i in range(total)])  4.7 us
    ppermute x9, waiting for transfers between devices, swap_bit(): lax.ppermute(block, 'space', [(i, i ^ 1 << bit) for i in range(total)])  4.15 us
    pallas_call x5, Pallas kernels, split(): pl.pallas_call(functools.partial(split_kernel, bounds=bounds, ignored=len...  3.88 us
    ppermute x1, waiting for transfers between devices, body(): yh = lax.ppermute(ys, 'space', [(i, i ^ sy) for i in range(total)])  3.65 us
  transfers between devices with their start and end apart: 17, of which 8 were waited for; matrix products, arithmetic and copies ran while one was open for 2% of the time, Pallas kernels for 39%

profile of v3, /device:TPU:0, one launch (start us, length us, event | category | flops | bytes accessed | tf_op | source)
XLA Modules:
  0.0 91.7 jit_solution(17734872429882172970)
XLA Ops:
  0.7 0.7 reshape.313.occ_ref
  2.1 0.1 stack.81.place_ref
  2.2 1.2 %copy-done = bf16[4096,128]{1,0:T(8,128)(2,1)S(1)} copy-done((bf16[4096,128]{1,0:T(8,128)(2,1)S(1)}, bf16[4096,128]{1,0:T(8,128)(2,1)}, u32[]{:S(2)}) %copy-start) | copy-done | bytes 1048600
  3.4 0.7 copy-done.22
  4.1 0.9 faces.1
  4.9 0.5 collective-permute-start
  5.5 0.7 collective-permute-start.1
  6.1 0.0 copy-start.2
  6.1 1.6 %copy-done.2 = bf16[4096,256]{1,0:T(8,128)(2,1)S(1)} copy-done((bf16[4096,256]{1,0:T(8,128)(2,1)S(1)}, bf16[4096,256]{1,0:T(8,128)(2,1)}, u32[]{:S(2)}) %copy-start.2) | copy-done | bytes 2097176
  7.7 5.6 %weight_inner.2 = (f32[12,256,128]{2,1,0:T(8,128)S(1)}, f32[8,128]{1,0:T(8,128)S(1)}, bf16[2,768,256]{2,1,0:T(8,128)(2,1)S(1)}, bf16[2,768,256]{2,1,0:T(8,128)(2,1)S(1)}, bf16[2,256,256]{2,1,0:T(8,128)(2,1)S(1)}) custom-call(bf16[4096,256]{1,0:T(8,128)(2,1)S(1)} %copy-done.2, bf16[4096,128]{1,0:T(8,128)(2,1)S(1)} %copy-done.1, ...), custom_call_target="tpu_custom_call" | custom-call | flops 1 | bytes 1 | tf_op jit(solution)/shard_map/weight_inner/pallas_call | solution.py:301
  13.4 0.0 copy-start.12
  13.4 0.0 collective-permute-done.fa_ref
  13.4 0.0 collective-permute-done.1.fb_ref
  13.4 0.0 copy-start.3
  13.4 1.3 %edges.1 = (bf16[16,16,128]{2,1,0:T(8,128)(2,1)S(1)}, bf16[16,16,128]{2,1,0:T(8,128)(2,1)S(1)}, bf16[18,16,128]{2,1,0:T(8,128)(2,1)S(1)}, bf16[18,16,128]{2,1,0:...) custom-call(s32[8]{0:T(128)S(1)} %stack.81.place_ref, ...), custom_call_target="tpu_custom_call" | custom-call | flops 1 | bytes 1 | tf_op jit(solution)/shard_map/edges/pallas_call | solution.py:133
  14.8 4.7 %collective-permute-start.2 = (bf16[32,128]{1,0:T(8,128)(2,1)S(1)}, bf16[32,128]{1,0:T(8,128)(2,1)S(1)}, u32[]{:S(2)}, u32[]{:S(2)}) collective-permute-start(bf16[32,128]{1,0:T(8,128)(2,1)S(1)} %get-tuple-element.47.refs_0_), channel_id=1, source_target_pairs={{0,24},{2,26},{4,28},{6,30},{8,16},{10,18},{12,20},{14,22},{16,8},... | collective-permute-start | bytes 24584 | tf_op jit(solution)/shard_map/ppermute | solution.py:665
  19.5 1.1 %fusion.4 = (bf16[2048,128]{1,0:T(8,128)(2,1)}, bf16[2048,128]{1,0:T(8,128)(2,1)}) fusion(bf16[4096,128]{1,0:T(8,128)(2,1)S(1)} %copy-done.1), kind=kLoop, calls=%fused_computation.41 | loop fusion | bytes 2097152 | tf_op jit(solution)/shard_map/slice | solution.py:653
  20.6 1.6 %collective-permute-start.5 = (bf16[2048,128]{1,0:T(8,128)(2,1)}, bf16[2048,128]{1,0:T(8,128)(2,1)}, u32[]{:S(2)}, u32[]{:S(2)}) collective-permute-start(bf16[2048,128]{1,0:T(8,128)(2,1)} %get-tuple-element.75), channel_id=1, source_target_pairs={{0,1},{1,0},{2,3},{3,2},{4,5},{5,4},{6,7},{7,6},{8,9},{9,8},{10,11... | collective-permute-start | bytes 1572872 | tf_op jit(solution)/shard_map/ppermute | solution.py:653
  22.2 7.3 %weight_inner.3 = (f32[15,256,128]{2,1,0:T(8,128)S(1)}, f32[8,128]{1,0:T(8,128)}) custom-call(bf16[4096,256]{1,0:T(8,128)(2,1)S(1)} %copy-done.3, bf16[4096,128]{1,0:T(8,128)(2,1)S(1)} %copy-done.1, f32[16,256]{1,0:T(8,128)S(1)} %get-tuple-element.38.mask_ref, bf16[32,128]{1,0:T(8,128)(2,1)S(1)} %get-tuple-element.47.refs_0_), custom_call_target="tpu_custom_call" | custom-call | flops 1 | bytes 1 | tf_op jit(solution)/shard_map/weight_inner/pallas_call | solution.py:301
  29.5 0.1 collective-permute-start.3
  29.5 0.8 collective-permute-start.4
  30.3 0.0 collective-permute-done.2.refs_4_
  30.3 3.6 %collective-permute-done.4.refs_1_ = bf16[18,16,128]{2,1,0:T(8,128)(2,1)S(1)} collective-permute-done((bf16[18,16,128]{2,1,0:T(8,128)(2,1)S(1)}, bf16[18,16,128]{2,1,0:T(8,128)(2,1)S(1)}, u32[]{:S(2)}, u32[]{:S(2)}) %collective-permute-start.4) | collective-permute-done | bytes 73760 | tf_op jit(solution)/shard_map/ppermute | solution.py:664
  34.0 1.9 %collective-permute-done.3.refs_0_ = bf16[18,16,128]{2,1,0:T(8,128)(2,1)S(1)} collective-permute-done((bf16[18,16,128]{2,1,0:T(8,128)(2,1)S(1)}, bf16[18,16,128]{2,1,0:T(8,128)(2,1)S(1)}, u32[]{:S(2)}, u32[]{:S(2)}) %collective-permute-start.3) | collective-permute-done | bytes 73760 | tf_op jit(solution)/shard_map/ppermute | solution.py:663
  35.9 0.1 pad_maximum_fusion.4
  36.0 0.0 copy-start.13
  36.2 0.1 pad_maximum_fusion.5
  36.4 0.0 collective-permute-done.5.refs_5_.refs_1_
  36.4 1.0 %copy-done.11 = f32[12,256,128]{2,1,0:T(8,128)S(1)} copy-done((f32[12,256,128]{2,1,0:T(8,128)S(1)}, f32[12,256,128]{2,1,0:T(8,128)}, u32[]{:S(2)}) %copy-start.11) | copy-done | bytes 1572888
  37.4 0.2 copy-done.13
  37.6 0.2 copy-done.15
  37.9 0.1 copy-done.21
  37.9 3.4 %weight_rim.1 = (f32[8,432,128]{2,1,0:T(8,128)S(1)}, f32[8,432,128]{2,1,0:T(8,128)}, bf16[1120,128]{1,0:T(8,128)(2,1)}) custom-call(s32[1]{0:T(128)} %bitcast.8.mine_ref, bf16[2,768,256]{2,1,0:T(8,128)(2,1)S(1)} %copy-done.13, bf16[2,768,256]{2,1,0:T(8,128)(2,1)S(1)} %copy-done.15, bf16[2,256,256]{2,1,0:T(8,128)(2,1)S(1)} %copy-done.21, ...), custom_call_target="tpu_custom_call" | custom-call | flops 1 | bytes 1 | tf_op jit(solution)/shard_map/weight_rim/pallas_call | solution.py:398
  41.3 1.2 %copy-done.6 = f32[8,432,128]{2,1,0:T(8,128)} copy-done((f32[8,432,128]{2,1,0:T(8,128)}, f32[8,432,128]{2,1,0:T(8,128)S(1)}, u32[]{:S(2)}) %copy-start.6) | copy-done | bytes 1769496
  42.5 0.4 collective-permute-start.10
  42.9 0.5 collective-permute-start.8
  43.4 1.5 %collective-permute-start.7 = (bf16[2048,128]{1,0:T(8,128)(2,1)}, bf16[2048,128]{1,0:T(8,128)(2,1)S(1)}, u32[]{:S(2)}, u32[]{:S(2)}) collective-permute-start(bf16[2048,128]{1,0:T(8,128)(2,1)} %get-tuple-element.74), channel_id=1, source_target_pairs={{0,1},{1,0},{2,3},{3,2},{4,5},{5,4},{6,7},{7,6},{8,9},{9,8},{10,11... | collective-permute-start | bytes 1572872 | tf_op jit(solution)/shard_map/ppermute | solution.py:653
  45.0 0.1 pad_add_fusion.bits_ref
  45.0 1.4 %collective-permute-done.10 = f32[8,432,128]{2,1,0:T(8,128)S(1)} collective-permute-done((f32[8,432,128]{2,1,0:T(8,128)}, f32[8,432,128]{2,1,0:T(8,128)S(1)}, u32[]{:S(2)}, u32[]{:S(2)}) %collective-permute-start.10) | collective-permute-done | bytes 1769504 | tf_op jit(solution)/shard_map/ppermute | solution.py:558
  46.5 1.2 %copy-done.8 = f32[8,432,128]{2,1,0:T(8,128)} copy-done((f32[8,432,128]{2,1,0:T(8,128)}, f32[8,432,128]{2,1,0:T(8,128)S(1)}, u32[]{:S(2)}) %copy-start.8) | copy-done | bytes 1769496
  47.7 1.5 %copy-done.7 = f32[8,432,128]{2,1,0:T(8,128)S(1)} copy-done((f32[8,432,128]{2,1,0:T(8,128)S(1)}, f32[8,432,128]{2,1,0:T(8,128)}, u32[]{:S(2)}) %copy-start.7) | copy-done | bytes 1769496
  49.2 1.5 %copy-done.9 = f32[8,432,128]{2,1,0:T(8,128)S(1)} copy-done((f32[8,432,128]{2,1,0:T(8,128)S(1)}, f32[8,432,128]{2,1,0:T(8,128)}, u32[]{:S(2)}) %copy-start.9) | copy-done | bytes 1769496
  50.7 1.7 %add_split.5 = (f32[2,2,216,128]{3,2,1,0:T(8,128)S(1)}, f32[2,2,216,128]{3,2,1,0:T(8,128)}, f32[2,2,216,128]{3,2,1,0:T(8,128)S(1)}, f32[2,2,216,128]{3,2,1,0:T(8,128)}) custom-call(s32[2]{0:T(128)S(1)} %pad_add_fusion.bits_ref, f32[2,2,2,432,128]{4,3,2,1,0:T(8,128)S(1)} %bitcast.55, f32[2,2,2,432,128]{4,3,2,1,0:T(8,128)S(1)} %bitcast.56), custom_call_target="tpu_custom_call" | custom-call | flops 1 | bytes 1 | tf_op jit(solution)/shard_map/add_split/pallas_call | solution.py:546
  52.4 0.8 copy-done.16
  53.2 0.8 copy-done.18
  53.9 2.2 %collective-permute-start.11 = (f32[2,2,216,128]{3,2,1,0:T(8,128)}, f32[2,2,216,128]{3,2,1,0:T(8,128)}, u32[]{:S(2)}, u32[]{:S(2)}) collective-permute-start(f32[2,2,216,128]{3,2,1,0:T(8,128)} %get-tuple-element.58.refs_3_), channel_id=1, source_target_pairs={{0,4},{2,6},{4,0},{6,2},{8,12},{10,14},{12,8},{14,10},{16,20},{18,... | collective-permute-start | bytes 1327112 | tf_op jit(solution)/shard_map/ppermute | solution.py:558
  56.2 0.0 collective-permute-start.12
  56.2 0.5 collective-permute-done.8.refs_3_
  56.6 0.0 collective-permute-start.9
  56.6 0.5 collective-permute-start.6
  57.1 8.9 %data_grad.2 = (f32[4096,128]{1,0:T(8,128)S(1)}, f32[8,128]{1,0:T(8,128)S(1)}) custom-call(s32[8]{0:T(128)S(1)} %stack.81.place_ref, f32[16,256]{1,0:T(8,128)S(1)} %get-tuple-element.38.mask_ref, bf16[1120,128]{1,0:T(8,128)(2,1)} %get-tuple-element.54.refs_0_, bf16[4096,128]{1,0:T(8,128)(2,1)S(1)} %copy-done.1, bf16[27,256,128]{2,1,0:T(8,128)(2,1)S(1)} %copy-done.5, ...), custom_call_target="tpu_custom_call" | custom-call | flops 1 | bytes 1 | tf_op jit(solution)/shard_map/data_grad/pallas_call | solution.py:505
  66.0 1.7 %collective-permute-done.7.outs_1_.refs_2_ = bf16[2048,128]{1,0:T(8,128)(2,1)S(1)} collective-permute-done((bf16[2048,128]{1,0:T(8,128)(2,1)}, bf16[2048,128]{1,0:T(8,128)(2,1)S(1)}, u32[]{:S(2)}, u32[]{:S(2)}) %collective-permute-start.7) | collective-permute-done | bytes 524320 | tf_op jit(solution)/shard_map/ppermute | solution.py:653
  67.8 1.1 %add_split.6 = (f32[2,216,128]{2,1,0:T(8,128)S(1)}, f32[2,216,128]{2,1,0:T(8,128)S(1)}) custom-call(s32[1]{0:T(128)} %bitcast.7.bits_ref, f32[2,2,216,128]{3,2,1,0:T(8,128)S(1)} %copy-done.19, f32[2,2,216,128]{3,2,1,0:T(8,128)} %collective-permute-done.11.recv_ref, f32[8,128]{1,0:T(8,128)S(1)} %get-tuple-element.62.outs_0_, ...), custom_call_target="tpu_custom_call" | custom-call | flops 1 | bytes 1 | tf_op jit(solution)/shard_map/add_split/pallas_call | solution.py:546
  68.8 0.1 collective-permute-start.13
  68.9 0.0 collective-permute-done.12.recv_ref
  68.9 1.1 %add_split.7 = (f32[2,216,128]{2,1,0:T(8,128)S(1)}, f32[2,216,128]{2,1,0:T(8,128)S(1)}) custom-call(s32[1]{0:T(128)} %bitcast.33.bits_ref, f32[2,2,216,128]{3,2,1,0:T(8,128)S(1)} %copy-done.17, f32[2,2,216,128]{3,2,1,0:T(8,128)} %collective-permute-done.12.recv_ref, f32[8,128]{1,0:T(8,128)S(1)} %get-tuple-element.62.outs_0_, ...), custom_call_target="tpu_custom_call" | custom-call | flops 1 | bytes 1 | tf_op jit(solution)/shard_map/add_split/pallas_call | solution.py:546
  70.0 2.0 %collective-permute-start.15 = (f32[2,216,128]{2,1,0:T(8,128)S(1)}, f32[2,216,128]{2,1,0:T(8,128)S(1)}, u32[]{:S(2)}, u32[]{:S(2)}) collective-permute-start(f32[2,216,128]{2,1,0:T(8,128)S(1)} %get-tuple-element.65.refs_7_), channel_id=1, source_target_pairs={{0,16},{2,18},{4,20},{6,22},{8,24},{10,26},{12,28},{14,30},{16,0},... | collective-permute-start | bytes 663560 | tf_op jit(solution)/shard_map/ppermute | solution.py:558
  72.0 1.1 %collective-permute-done.6.refs_0_ = bf16[1120,128]{1,0:T(8,128)(2,1)} collective-permute-done((bf16[1120,128]{1,0:T(8,128)(2,1)}, bf16[1120,128]{1,0:T(8,128)(2,1)}, u32[]{:S(2)}, u32[]{:S(2)}) %collective-permute-start.6) | collective-permute-done | bytes 286752 | tf_op jit(solution)/shard_map/ppermute | solution.py:675
  73.2 10.6 %data_grad.3 = (bf16[4096,128]{1,0:T(8,128)(2,1)}, f32[8,128]{1,0:T(8,128)S(1)}) custom-call(s32[8]{0:T(128)S(1)} %stack.81.place_ref, f32[16,256]{1,0:T(8,128)S(1)} %get-tuple-element.38.mask_ref, bf16[1120,128]{1,0:T(8,128)(2,1)} %collective-permute-done.6.refs_0_, bf16[2048,128]{1,0:T(8,128)(2,1)} %collective-permute-done.5.refs_5_.refs_1_, ...), custom_call_target="tpu_custom_call" | custom-call | flops 1 | bytes 1 | tf_op jit(solution)/shard_map/data_grad/pallas_call | solution.py:505
  83.8 1.4 %collective-permute-start.14 = (f32[216,128]{1,0:T(8,128)S(1)}, f32[216,128]{1,0:T(8,128)S(1)}, u32[]{:S(2)}, u32[]{:S(2)}) collective-permute-start(f32[216,128]{1,0:T(8,128)S(1)} %get-tuple-element.70), channel_id=1, source_target_pairs={{0,16},{2,18},{4,20},{6,22},{8,24},{10,26},{12,28},{14,30},{16,0},... | collective-permute-start | bytes 331784 | tf_op jit(solution)/shard_map/ppermute | solution.py:558
  85.2 3.1 %collective-permute-start.16 = (f32[216,128]{1,0:T(8,128)S(1)}, f32[216,128]{1,0:T(8,128)S(1)}, u32[]{:S(2)}, u32[]{:S(2)}) collective-permute-start(f32[216,128]{1,0:T(8,128)S(1)} %get-tuple-element.73), channel_id=1, source_target_pairs={{0,4},{2,6},{4,0},{6,2},{8,12},{10,14},{12,8},{14,10},{16,20},{18,... | collective-permute-start | bytes 331784 | tf_op jit(solution)/shard_map/ppermute | solution.py:558
  88.3 2.5 %collective-permute-done.14 = f32[216,128]{1,0:T(8,128)S(1)} collective-permute-done((f32[216,128]{1,0:T(8,128)S(1)}, f32[216,128]{1,0:T(8,128)S(1)}, u32[]{:S(2)}, u32[]{:S(2)}) %collective-permute-start.14) | collective-permute-done | bytes 110624 | tf_op jit(solution)/shard_map/ppermute | solution.py:558
  90.7 0.3 collective-permute-done.16
  91.0 0.7 pad_maximum_fusion.1
  (56 shorter events, 0.5 us)
Async XLA Ops:
  2.2 1.2 %copy-start = (bf16[4096,128]{1,0:T(8,128)(2,1)S(1)}, bf16[4096,128]{1,0:T(8,128)(2,1)}, u32[]{:S(2)}) copy-start(bf16[4096,128]{1,0:T(8,128)(2,1)} %refs_1_.1) | copy-start | bytes 3145732
  3.4 0.7 copy-start.22
  4.1 2.1 %copy-start.1 = (bf16[4096,128]{1,0:T(8,128)(2,1)S(1)}, bf16[4096,128]{1,0:T(8,128)(2,1)}, u32[]{:S(2)}) copy-start(bf16[4096,128]{1,0:T(8,128)(2,1)} %refs_1_.1) | copy-start | bytes 3145732
  4.9 8.5 %collective-permute-start = (bf16[16,16,128]{2,1,0:T(8,128)(2,1)S(1)}, bf16[16,16,128]{2,1,0:T(8,128)(2,1)S(1)}, u32[]{:S(2)}, u32[]{:S(2)}) collective-permute-start(bf16[16,16,128]{2,1,0:T(8,128)(2,1)S(1)} %get-tuple-element.42), channel_id=1, source_target_pairs={{0,2},{2,0},{4,6},{6,4},{8,10},{10,8},{12,14},{14,12},{16,18},{18,... | collective-permute-start | bytes 196616 | tf_op jit(solution)/shard_map/ppermute | solution.py:558
  5.5 7.9 %collective-permute-start.1 = (bf16[16,16,128]{2,1,0:T(8,128)(2,1)S(1)}, bf16[16,16,128]{2,1,0:T(8,128)(2,1)S(1)}, u32[]{:S(2)}, u32[]{:S(2)}) collective-permute-start(bf16[16,16,128]{2,1,0:T(8,128)(2,1)S(1)} %get-tuple-element.43), channel_id=1, source_target_pairs={{2,4},{10,12},{18,20},{26,28},{4,2},{12,10},{20,18},{28,26},{3,5},... | collective-permute-start | bytes 196616 | tf_op jit(solution)/shard_map/ppermute | solution.py:649
  6.1 1.6 %copy-start.2 = (bf16[4096,256]{1,0:T(8,128)(2,1)S(1)}, bf16[4096,256]{1,0:T(8,128)(2,1)}, u32[]{:S(2)}) copy-start(bf16[4096,256]{1,0:T(8,128)(2,1)} %feat_ref.3) | copy-start | bytes 6291460
  7.7 5.7 %copy-start.4 = (bf16[27,256,128]{2,1,0:T(8,128)(2,1)S(1)}, bf16[27,256,128]{2,1,0:T(8,128)(2,1)}, u32[]{:S(2)}) copy-start(bf16[27,256,128]{2,1,0:T(8,128)(2,1)} %refs_2_.1) | copy-start | bytes 5308420
  13.4 7.2 %copy-start.10 = (f32[12,256,128]{2,1,0:T(8,128)}, f32[12,256,128]{2,1,0:T(8,128)S(1)}, u32[]{:S(2)}) copy-start(f32[12,256,128]{2,1,0:T(8,128)S(1)} %get-tuple-element.52.part_a_ref) | copy-start | bytes 4718596
  13.4 7.2 %copy-start.12 = (bf16[2,768,256]{2,1,0:T(8,128)(2,1)}, bf16[2,768,256]{2,1,0:T(8,128)(2,1)S(1)}, u32[]{:S(2)}) copy-start(bf16[2,768,256]{2,1,0:T(8,128)(2,1)S(1)} %get-tuple-element.39.fx_ref) | copy-start | bytes 2359300
  13.4 7.2 %copy-start.14 = (bf16[2,768,256]{2,1,0:T(8,128)(2,1)}, bf16[2,768,256]{2,1,0:T(8,128)(2,1)S(1)}, u32[]{:S(2)}) copy-start(bf16[2,768,256]{2,1,0:T(8,128)(2,1)S(1)} %get-tuple-element.40.fy_ref) | copy-start | bytes 2359300
  13.4 7.2 %copy-start.20 = (bf16[2,256,256]{2,1,0:T(8,128)(2,1)}, bf16[2,256,256]{2,1,0:T(8,128)(2,1)S(1)}, u32[]{:S(2)}) copy-start(bf16[2,256,256]{2,1,0:T(8,128)(2,1)S(1)} %get-tuple-element.41.fz_ref) | copy-start | bytes 786436
  13.4 8.7 %copy-start.3 = (bf16[4096,256]{1,0:T(8,128)(2,1)S(1)}, bf16[4096,256]{1,0:T(8,128)(2,1)}, u32[]{:S(2)}) copy-start(bf16[4096,256]{1,0:T(8,128)(2,1)} %feat_ref.3) | copy-start | bytes 6291460
  14.8 15.5 %collective-permute-start.2 = (bf16[32,128]{1,0:T(8,128)(2,1)S(1)}, bf16[32,128]{1,0:T(8,128)(2,1)S(1)}, u32[]{:S(2)}, u32[]{:S(2)}) collective-permute-start(bf16[32,128]{1,0:T(8,128)(2,1)S(1)} %get-tuple-element.47.refs_0_), channel_id=1, source_target_pairs={{0,24},{2,26},{4,28},{6,30},{8,16},{10,18},{12,20},{14,22},{16,8},... | collective-permute-start | bytes 24584 | tf_op jit(solution)/shard_map/ppermute | solution.py:665
  20.6 15.9 %collective-permute-start.5 = (bf16[2048,128]{1,0:T(8,128)(2,1)}, bf16[2048,128]{1,0:T(8,128)(2,1)}, u32[]{:S(2)}, u32[]{:S(2)}) collective-permute-start(bf16[2048,128]{1,0:T(8,128)(2,1)} %get-tuple-element.75), channel_id=1, source_target_pairs={{0,1},{1,0},{2,3},{3,2},{4,5},{5,4},{6,7},{7,6},{8,9},{9,8},{10,11... | collective-permute-start | bytes 1572872 | tf_op jit(solution)/shard_map/ppermute | solution.py:653
  29.5 6.4 %collective-permute-start.3 = (bf16[18,16,128]{2,1,0:T(8,128)(2,1)S(1)}, bf16[18,16,128]{2,1,0:T(8,128)(2,1)S(1)}, u32[]{:S(2)}, u32[]{:S(2)}) collective-permute-start(bf16[18,16,128]{2,1,0:T(8,128)(2,1)S(1)} %get-tuple-element.48), channel_id=1, source_target_pairs={{0,16},{2,18},{4,20},{6,22},{8,24},{10,26},{12,28},{14,30},{16,0},... | collective-permute-start | bytes 221192 | tf_op jit(solution)/shard_map/ppermute | solution.py:663
  29.5 4.4 %collective-permute-start.4 = (bf16[18,16,128]{2,1,0:T(8,128)(2,1)S(1)}, bf16[18,16,128]{2,1,0:T(8,128)(2,1)S(1)}, u32[]{:S(2)}, u32[]{:S(2)}) collective-permute-start(bf16[18,16,128]{2,1,0:T(8,128)(2,1)S(1)} %get-tuple-element.49), channel_id=1, source_target_pairs={{0,8},{2,10},{4,12},{6,14},{8,0},{10,2},{12,4},{14,6},{16,24},{18,... | collective-permute-start | bytes 221192 | tf_op jit(solution)/shard_map/ppermute | solution.py:664
  36.0 1.4 %copy-start.11 = (f32[12,256,128]{2,1,0:T(8,128)S(1)}, f32[12,256,128]{2,1,0:T(8,128)}, u32[]{:S(2)}) copy-start(f32[12,256,128]{2,1,0:T(8,128)} %copy-done.10) | copy-start | bytes 4718596
  36.0 1.6 %copy-start.13 = (bf16[2,768,256]{2,1,0:T(8,128)(2,1)S(1)}, bf16[2,768,256]{2,1,0:T(8,128)(2,1)}, u32[]{:S(2)}) copy-start(bf16[2,768,256]{2,1,0:T(8,128)(2,1)} %copy-done.12) | copy-start | bytes 2359300
  36.0 1.8 %copy-start.15 = (bf16[2,768,256]{2,1,0:T(8,128)(2,1)S(1)}, bf16[2,768,256]{2,1,0:T(8,128)(2,1)}, u32[]{:S(2)}) copy-start(bf16[2,768,256]{2,1,0:T(8,128)(2,1)} %copy-done.14) | copy-start | bytes 2359300
  36.1 1.9 %copy-start.21 = (bf16[2,256,256]{2,1,0:T(8,128)(2,1)S(1)}, bf16[2,256,256]{2,1,0:T(8,128)(2,1)}, u32[]{:S(2)}) copy-start(bf16[2,256,256]{2,1,0:T(8,128)(2,1)} %copy-done.20) | copy-start | bytes 786436
  41.3 1.2 %copy-start.6 = (f32[8,432,128]{2,1,0:T(8,128)}, f32[8,432,128]{2,1,0:T(8,128)S(1)}, u32[]{:S(2)}) copy-start(f32[8,432,128]{2,1,0:T(8,128)S(1)} %get-tuple-element.56) | copy-start | bytes 5308420
  42.5 3.9 %collective-permute-start.10 = (f32[8,432,128]{2,1,0:T(8,128)}, f32[8,432,128]{2,1,0:T(8,128)S(1)}, u32[]{:S(2)}, u32[]{:S(2)}) collective-permute-start(f32[8,432,128]{2,1,0:T(8,128)} %get-tuple-element.57), channel_id=1, source_target_pairs={{0,2},{2,0},{4,6},{6,4},{8,10},{10,8},{12,14},{14,12},{16,18},{18,... | collective-permute-start | bytes 5308424 | tf_op jit(solution)/shard_map/ppermute | solution.py:558
  42.9 13.7 %collective-permute-start.8 = (bf16[14,128,128]{2,1,0:T(8,128)(2,1)}, bf16[14,128,128]{2,1,0:T(8,128)(2,1)}, u32[]{:S(2)}, u32[]{:S(2)}) collective-permute-start(bf16[14,128,128]{2,1,0:T(8,128)(2,1)} %get-tuple-element.55), channel_id=1, source_target_pairs={{0,1},{1,0},{2,3},{3,2},{4,5},{5,4},{6,7},{7,6},{8,9},{9,8},{10,11... | collective-permute-start | bytes 1376264 | tf_op jit(solution)/shard_map/ppermute | solution.py:689
  43.4 24.3 %collective-permute-start.7 = (bf16[2048,128]{1,0:T(8,128)(2,1)}, bf16[2048,128]{1,0:T(8,128)(2,1)S(1)}, u32[]{:S(2)}, u32[]{:S(2)}) collective-permute-start(bf16[2048,128]{1,0:T(8,128)(2,1)} %get-tuple-element.74), channel_id=1, source_target_pairs={{0,1},{1,0},{2,3},{3,2},{4,5},{5,4},{6,7},{7,6},{8,9},{9,8},{10,11... | collective-permute-start | bytes 1572872 | tf_op jit(solution)/shard_map/ppermute | solution.py:653
  46.5 1.2 %copy-start.8 = (f32[8,432,128]{2,1,0:T(8,128)}, f32[8,432,128]{2,1,0:T(8,128)S(1)}, u32[]{:S(2)}) copy-start(f32[8,432,128]{2,1,0:T(8,128)S(1)} %collective-permute-done.10) | copy-start | bytes 5308420
  47.7 1.5 %copy-start.7 = (f32[8,432,128]{2,1,0:T(8,128)S(1)}, f32[8,432,128]{2,1,0:T(8,128)}, u32[]{:S(2)}) copy-start(f32[8,432,128]{2,1,0:T(8,128)} %copy-done.6) | copy-start | bytes 5308420
  49.2 1.5 %copy-start.9 = (f32[8,432,128]{2,1,0:T(8,128)S(1)}, f32[8,432,128]{2,1,0:T(8,128)}, u32[]{:S(2)}) copy-start(f32[8,432,128]{2,1,0:T(8,128)} %copy-done.8) | copy-start | bytes 5308420
  50.7 6.5 %copy-start.5 = (bf16[27,256,128]{2,1,0:T(8,128)(2,1)S(1)}, bf16[27,256,128]{2,1,0:T(8,128)(2,1)}, u32[]{:S(2)}) copy-start(bf16[27,256,128]{2,1,0:T(8,128)(2,1)} %refs_2_.1) | copy-start | bytes 5308420
  52.4 0.8 copy-start.16
  53.2 0.8 copy-start.18
  53.9 13.8 %collective-permute-start.11 = (f32[2,2,216,128]{3,2,1,0:T(8,128)}, f32[2,2,216,128]{3,2,1,0:T(8,128)}, u32[]{:S(2)}, u32[]{:S(2)}) collective-permute-start(f32[2,2,216,128]{3,2,1,0:T(8,128)} %get-tuple-element.58.refs_3_), channel_id=1, source_target_pairs={{0,4},{2,6},{4,0},{6,2},{8,12},{10,14},{12,8},{14,10},{16,20},{18,... | collective-permute-start | bytes 1327112 | tf_op jit(solution)/shard_map/ppermute | solution.py:558
  56.2 12.8 %collective-permute-start.12 = (f32[2,2,216,128]{3,2,1,0:T(8,128)}, f32[2,2,216,128]{3,2,1,0:T(8,128)}, u32[]{:S(2)}, u32[]{:S(2)}) collective-permute-start(f32[2,2,216,128]{3,2,1,0:T(8,128)} %get-tuple-element.59.refs_4_), channel_id=1, source_target_pairs={{0,8},{2,10},{4,12},{6,14},{8,0},{10,2},{12,4},{14,6},{16,24},{18,... | collective-permute-start | bytes 1327112 | tf_op jit(solution)/shard_map/ppermute | solution.py:558
  56.6 16.5 %collective-permute-start.9 = (bf16[14,128,128]{2,1,0:T(8,128)(2,1)}, bf16[14,128,128]{2,1,0:T(8,128)(2,1)}, u32[]{:S(2)}, u32[]{:S(2)}) collective-permute-start(bf16[14,128,128]{2,1,0:T(8,128)(2,1)} %collective-permute-done.8.refs_3_), channel_id=1, source_target_pairs={{0,2},{2,0},{4,6},{6,4},{8,10},{10,8},{12,14},{14,12},{16,18},{18,... | collective-permute-start | bytes 1376264 | tf_op jit(solution)/shard_map/ppermute | solution.py:558
  56.6 16.5 %collective-permute-start.6 = (bf16[1120,128]{1,0:T(8,128)(2,1)}, bf16[1120,128]{1,0:T(8,128)(2,1)}, u32[]{:S(2)}, u32[]{:S(2)}) collective-permute-start(bf16[1120,128]{1,0:T(8,128)(2,1)} %get-tuple-element.54.refs_0_), channel_id=1, source_target_pairs={{0,1},{1,0},{2,3},{3,2},{4,5},{5,4},{6,7},{7,6},{8,9},{9,8},{10,11... | collective-permute-start | bytes 860168 | tf_op jit(solution)/shard_map/ppermute | solution.py:675
  57.1 10.6 %copy-start.19 = (f32[2,2,216,128]{3,2,1,0:T(8,128)S(1)}, f32[2,2,216,128]{3,2,1,0:T(8,128)}, u32[]{:S(2)}) copy-start(f32[2,2,216,128]{3,2,1,0:T(8,128)} %copy-done.18) | copy-start | bytes 1327108
  57.1 11.8 %copy-start.17 = (f32[2,2,216,128]{3,2,1,0:T(8,128)S(1)}, f32[2,2,216,128]{3,2,1,0:T(8,128)}, u32[]{:S(2)}) copy-start(f32[2,2,216,128]{3,2,1,0:T(8,128)} %copy-done.16) | copy-start | bytes 1327108
  68.8 14.9 %collective-permute-start.13 = (f32[2,216,128]{2,1,0:T(8,128)S(1)}, f32[2,216,128]{2,1,0:T(8,128)S(1)}, u32[]{:S(2)}, u32[]{:S(2)}) collective-permute-start(f32[2,216,128]{2,1,0:T(8,128)S(1)} %get-tuple-element.63.refs_6_), channel_id=1, source_target_pairs={{0,8},{2,10},{4,12},{6,14},{8,0},{10,2},{12,4},{14,6},{16,24},{18,... | collective-permute-start | bytes 663560 | tf_op jit(solution)/shard_map/ppermute | solution.py:558
  70.0 15.2 %collective-permute-start.15 = (f32[2,216,128]{2,1,0:T(8,128)S(1)}, f32[2,216,128]{2,1,0:T(8,128)S(1)}, u32[]{:S(2)}, u32[]{:S(2)}) collective-permute-start(f32[2,216,128]{2,1,0:T(8,128)S(1)} %get-tuple-element.65.refs_7_), channel_id=1, source_target_pairs={{0,16},{2,18},{4,20},{6,22},{8,24},{10,26},{12,28},{14,30},{16,0},... | collective-permute-start | bytes 663560 | tf_op jit(solution)/shard_map/ppermute | solution.py:558
  83.8 7.0 %collective-permute-start.14 = (f32[216,128]{1,0:T(8,128)S(1)}, f32[216,128]{1,0:T(8,128)S(1)}, u32[]{:S(2)}, u32[]{:S(2)}) collective-permute-start(f32[216,128]{1,0:T(8,128)S(1)} %get-tuple-element.70), channel_id=1, source_target_pairs={{0,16},{2,18},{4,20},{6,22},{8,24},{10,26},{12,28},{14,30},{16,0},... | collective-permute-start | bytes 331784 | tf_op jit(solution)/shard_map/ppermute | solution.py:558
  85.2 5.8 %collective-permute-start.16 = (f32[216,128]{1,0:T(8,128)S(1)}, f32[216,128]{1,0:T(8,128)S(1)}, u32[]{:S(2)}, u32[]{:S(2)}) collective-permute-start(f32[216,128]{1,0:T(8,128)S(1)} %get-tuple-element.73), channel_id=1, source_target_pairs={{0,4},{2,6},{4,0},{6,2},{8,12},{10,14},{12,8},{14,10},{16,20},{18,... | collective-permute-start | bytes 331784 | tf_op jit(solution)/shard_map/ppermute | solution.py:558

commit v4 on v3

--- a/solution.py
+++ b/solution.py
@@ -311,7 +311,9 @@
             pltpu.SemaphoreType.DMA((len(held) + 1,)),
         ],
         compiler_params=pltpu.CompilerParams(vmem_limit_bytes=28 << 20),
-        cost_estimate=COST,
+        cost_estimate=pl.CostEstimate(
+            flops=0 if with_rims else 1 << 31, bytes_accessed=1, transcendentals=0
+        ),
         name="weight_inner",
     )(features, raw, mask_rows, *ahead)
 
@@ -329,7 +331,8 @@
             flat_refs[0][at : at + value.shape[0], :] = value
             at += value.shape[0]
     cin = fz_ref.shape[1]
-    rows = acc_ref.shape[2]
+    rows = acc_ref.shape[-2]
+    bits = len(acc_ref.shape) - 2
     zero = jnp.zeros((1, SPAN, HALF), BF)
     more = {}
 
@@ -376,7 +379,8 @@
             block, at = divmod(first, rows)
             count = min(rows - at, (tap + 1) * cin - first)
             piece = value[first - tap * cin : first - tap * cin + count]
-            acc_ref[block % 2, block // 2, at : at + count] = piece
+            spot = (block % 2,) + tuple(block // 2 ** (bits - 1 - k) % 2 for k in range(bits - 1))
+            acc_ref[spot + (slice(at, at + count),)] = piece
             first += count
 
     mine = mine_ref[0]
@@ -391,7 +395,8 @@
 def weight_grad_rim(mine, fx, fy, fz, borders, inner_a, inner_b, scale, total, pieces, *ahead):
     cin = fz.shape[1]
     rows = 27 * cin // total
-    outs = [jax.ShapeDtypeStruct((total // 2, rows, HALF), F32)] * 2
+    by_bit = (2,) * (total.bit_length() - 2)
+    outs = [jax.ShapeDtypeStruct(by_bit + (rows, HALF), F32)] * 2
     if pieces:
         length = sum(v.size for v in pieces) // HALF
         outs.append(jax.ShapeDtypeStruct((length, HALF), BF))
@@ -401,7 +406,7 @@
         in_specs=[SMEM_SPEC] + [VMEM_SPEC] * (8 + len(pieces)) + [ANY_SPEC] * len(ahead),
         out_specs=(ANY_SPEC, ANY_SPEC) + (VMEM_SPEC,) * (len(outs) - 2),
         scratch_shapes=[
-            pltpu.VMEM((2, total // 2, rows, HALF), F32),
+            pltpu.VMEM((2,) + by_bit + (rows, HALF), F32),
             pltpu.SemaphoreType.DMA((2,)),
         ],
         compiler_params=pltpu.CompilerParams(vmem_limit_bytes=24 << 20),
@@ -664,7 +669,7 @@
         yh = lax.ppermute(ys, "space", [(i, i ^ sy) for i in range(total)])
         eh = lax.ppermute(es, "space", [(i, i ^ sx ^ sy) for i in range(total)])
         inner_b, _ = weight_grad_inner(
-            features, grad_out, mask_rows, PAIRS[2:], False, es
+            features, grad_out, mask_rows, PAIRS[2:], False, xs, ys, es
         )
         borders = pair_borders(cx, cy, xh, yh, eh, zl, zh)
         keep, send, flat = weight_grad_rim(
@@ -691,10 +696,8 @@
     recv = swap_bit(send, 0, total)
 
     bits = total.bit_length() - 1
-    rows = keep.shape[1]
+    rows = keep.shape[-2]
     cut = rows // 2
-    keep = keep.reshape((2,) * (bits - 1) + (rows, HALF))
-    recv = recv.reshape(keep.shape)
     orders = [list(range(1, bits)), list(range(2, bits)) + [1]]
     have = [list(range(bits - 1, 0, -1)) for _ in orders]
     bounds = [

time: 92.2 us -> 91.2 us (0.989)
  local copies, waits for them, and re-layouts: 14 us -> 9.74 us
  Pallas kernels: 41.8 us -> 43.6 us
  starting transfers between devices: 20 us -> 21.3 us
    unnamed x46 -> x32, local copies, waits for them, and re-layouts: 12 us -> 7.76 us
    ppermute x1, starting transfers between devices: 4.7 us -> 1.35 us  [body(): eh = lax.ppermute(es, 'space', [(i, i ^ sx ^ sy) for i in range(total)])]
    ppermute x1, starting transfers between devices: 0.07 us -> 2.66 us  [body(): xh = lax.ppermute(xs, 'space', [(i, i ^ sx) for i in range(total)])]
    ppermute x1, waiting for transfers between devices: 1.88 us -> 0.01 us  [body(): xh = lax.ppermute(xs, 'space', [(i, i ^ sx) for i in range(total)])]
    ppermute x1, waiting for transfers between devices: 0.46 us -> 1.55 us  [body(): part = lax.ppermute(part, 'chan', swap)]
    ppermute x9, waiting for transfers between devices: 4.15 us -> 5.21 us  [swap_bit(): lax.ppermute(block, 'space', [(i, i ^ 1 << bit) for i in range(total)])]
    pallas_call x5, Pallas kernels: 3.88 us -> 4.84 us  [split(): pl.pallas_call(functools.partial(split_kernel, bounds=bounds, ignored=len...]
  transfers between devices with their start and end apart: 17 -> 17, of which waited for: 8 -> 6; matrix products, arithmetic and copies ran while one was open for 2% -> 2% of each run, Pallas kernels for 39% -> 43%
where the time goes in v4:
time: 91.2 us; the launch traced here: 90.7 us
  Pallas kernels  43.6 us (48%)
  starting transfers between devices  21.3 us (23%)
  waiting for transfers between devices  13.3 us (15%)
  local copies, waits for them, and re-layouts  9.74 us (11%)
  between operations  1.67 us (2%)
  other arithmetic  1.12 us (1%)
    pallas_call x2, Pallas kernels, data_grad_local(): pl.pallas_call(functools.partial(data_kernel, borders=len(borders), ignor...  19.3 us
    pallas_call x2, Pallas kernels, weight_grad_inner(): pl.pallas_call(functools.partial(inner_kernel, pairs=pairs, ignored=len(a...  12.9 us
    ppermute x9, starting transfers between devices, swap_bit(): lax.ppermute(block, 'space', [(i, i ^ 1 << bit) for i in range(total)])  10.7 us
    unnamed x32, local copies, waits for them, and re-layouts  7.76 us
    ppermute x9, waiting for transfers between devices, swap_bit(): lax.ppermute(block, 'space', [(i, i ^ 1 << bit) for i in range(total)])  5.21 us
    pallas_call x5, Pallas kernels, split(): pl.pallas_call(functools.partial(split_kernel, bounds=bounds, ignored=len...  4.84 us
    ppermute x1, waiting for transfers between devices, body(): yh = lax.ppermute(ys, 'space', [(i, i ^ sy) for i in range(total)])  4.5 us
    ppermute x2, starting transfers between devices, body(): lax.ppermute(grad_out[k * half_rows:(k + 1) * half_rows], 'chan', swap)  4 us
  transfers between devices with their start and end apart: 17, of which 6 were waited for; matrix products, arithmetic and copies ran while one was open for 2% of the time, Pallas kernels for 43%

profile of v4, /device:TPU:0, one launch (start us, length us, event | category | flops | bytes accessed | tf_op | source)
XLA Modules:
  0.0 90.7 jit_solution(3469599911929533348)
XLA Ops:
  0.7 0.7 reshape.307.occ_ref
  2.1 0.1 stack.81.place_ref
  2.2 1.2 %copy-done = bf16[4096,128]{1,0:T(8,128)(2,1)S(1)} copy-done((bf16[4096,128]{1,0:T(8,128)(2,1)S(1)}, bf16[4096,128]{1,0:T(8,128)(2,1)}, u32[]{:S(2)}) %copy-start) | copy-done | bytes 1048600
  3.4 0.7 copy-done.15
  4.1 1.5 %faces.1 = (f32[16,256]{1,0:T(8,128)S(1)}, bf16[16,16,128]{2,1,0:T(8,128)(2,1)}, bf16[16,16,128]{2,1,0:T(8,128)(2,1)}, bf16[16,16,128]{2,1,0:T(8,128)(2,1)S(1)}, bf16[16,16,128]{2,1,0:T(8,128)(2,1)S(1)}) custom-call(s32[8]{0:T(128)S(1)} %stack.81.place_ref, s32[1,8]{1,0:T(1,128)S(1)} %copy-done.15, s32[1]{0:T(128)S(6)} %copy.12.count_ref, ...), custom_call_target="tpu_custom_call" | custom-call | flops 1 | bytes 1 | tf_op jit(solution)/shard_map/faces/pallas_call | solution.py:78
  5.6 0.5 collective-permute-start
  6.0 1.3 %collective-permute-start.1 = (bf16[16,16,128]{2,1,0:T(8,128)(2,1)}, bf16[16,16,128]{2,1,0:T(8,128)(2,1)}, u32[]{:S(2)}, u32[]{:S(2)}) collective-permute-start(bf16[16,16,128]{2,1,0:T(8,128)(2,1)} %get-tuple-element.43), channel_id=1, source_target_pairs={{2,4},{10,12},{18,20},{26,28},{4,2},{12,10},{20,18},{28,26},{3,5},... | collective-permute-start | bytes 196616 | tf_op jit(solution)/shard_map/ppermute | solution.py:654
  7.3 0.0 copy-done.12
  7.3 0.0 copy-done.1
  7.3 1.0 %fusion.4 = (bf16[2048,128]{1,0:T(8,128)(2,1)}, bf16[2048,128]{1,0:T(8,128)(2,1)}) fusion(bf16[4096,128]{1,0:T(8,128)(2,1)S(1)} %copy-done.1), kind=kLoop, calls=%fused_computation.41 | loop fusion | bytes 2097152 | tf_op jit(solution)/shard_map/slice | solution.py:658
  8.3 2.5 %collective-permute-start.5 = (bf16[2048,128]{1,0:T(8,128)(2,1)}, bf16[2048,128]{1,0:T(8,128)(2,1)S(1)}, u32[]{:S(2)}, u32[]{:S(2)}) collective-permute-start(bf16[2048,128]{1,0:T(8,128)(2,1)} %get-tuple-element.75), channel_id=1, source_target_pairs={{0,1},{1,0},{2,3},{3,2},{4,5},{5,4},{6,7},{7,6},{8,9},{9,8},{10,11... | collective-permute-start | bytes 1572872 | tf_op jit(solution)/shard_map/ppermute | solution.py:658
  10.9 1.6 %copy-done.3 = bf16[4096,256]{1,0:T(8,128)(2,1)S(1)} copy-done((bf16[4096,256]{1,0:T(8,128)(2,1)S(1)}, bf16[4096,256]{1,0:T(8,128)(2,1)}, u32[]{:S(2)}) %copy-start.3) | copy-done | bytes 2097176
  12.4 5.6 %weight_inner.2 = (f32[12,256,128]{2,1,0:T(8,128)S(1)}, f32[8,128]{1,0:T(8,128)S(1)}, bf16[2,768,256]{2,1,0:T(8,128)(2,1)S(1)}, bf16[2,768,256]{2,1,0:T(8,128)(2,1)S(1)}, bf16[2,256,256]{2,1,0:T(8,128)(2,1)S(1)}) custom-call(bf16[4096,256]{1,0:T(8,128)(2,1)S(1)} %copy-done.3, bf16[4096,128]{1,0:T(8,128)(2,1)S(1)} %copy-done.1, ...), custom_call_target="tpu_custom_call" | custom-call | bytes 1 | tf_op jit(solution)/shard_map/weight_inner/pallas_call | solution.py:301
  18.1 0.0 collective-permute-done.fa_ref
  18.1 0.0 collective-permute-done.1.fb_ref
  18.1 0.0 copy-done.2
  18.1 0.0 copy-done.13
  18.1 1.6 %edges.1 = (bf16[16,16,128]{2,1,0:T(8,128)(2,1)S(1)}, bf16[16,16,128]{2,1,0:T(8,128)(2,1)S(1)}, bf16[18,16,128]{2,1,0:T(8,128)(2,1)S(1)}, bf16[18,16,128]{2,1,0:...) custom-call(s32[8]{0:T(128)S(1)} %copy-done.13, ...), custom_call_target="tpu_custom_call" | custom-call | flops 1 | bytes 1 | tf_op jit(solution)/shard_map/edges/pallas_call | solution.py:133
  19.8 2.7 %collective-permute-start.3 = (bf16[18,16,128]{2,1,0:T(8,128)(2,1)S(1)}, bf16[18,16,128]{2,1,0:T(8,128)(2,1)S(1)}, u32[]{:S(2)}, u32[]{:S(2)}) collective-permute-start(bf16[18,16,128]{2,1,0:T(8,128)(2,1)S(1)} %get-tuple-element.48.refs_0_), channel_id=1, source_target_pairs={{0,16},{2,18},{4,20},{6,22},{8,24},{10,26},{12,28},{14,30},{16,0},... | collective-permute-start | bytes 221192 | tf_op jit(solution)/shard_map/ppermute | solution.py:668
  22.4 1.3 %collective-permute-start.2 = (bf16[32,128]{1,0:T(8,128)(2,1)S(1)}, bf16[32,128]{1,0:T(8,128)(2,1)S(1)}, u32[]{:S(2)}, u32[]{:S(2)}) collective-permute-start(bf16[32,128]{1,0:T(8,128)(2,1)S(1)} %get-tuple-element.47.refs_2_), channel_id=1, source_target_pairs={{0,24},{2,26},{4,28},{6,30},{8,16},{10,18},{12,20},{14,22},{16,8},... | collective-permute-start | bytes 24584 | tf_op jit(solution)/shard_map/ppermute | solution.py:670
  23.8 7.3 %weight_inner.3 = (f32[15,256,128]{2,1,0:T(8,128)S(1)}, f32[8,128]{1,0:T(8,128)}) custom-call(bf16[4096,256]{1,0:T(8,128)(2,1)S(1)} %copy-done.3, bf16[4096,128]{1,0:T(8,128)(2,1)S(1)} %copy-done.1, f32[16,256]{1,0:T(8,128)S(1)} %get-tuple-element.38.mask_ref, bf16[18,16,128]{2,1,0:T(8,128)(2,1)S(1)} %get-tuple-element.48.refs_0_, ...), custom_call_target="tpu_custom_call" | custom-call | flops 2147483648 | bytes 1 | tf_op jit(solution)/shard_map/weight_inner/pallas_call | solution.py:301
  31.1 0.3 collective-permute-start.4
  31.4 0.0 collective-permute-done.2.refs_4_
  31.4 4.5 %collective-permute-done.4.refs_1_ = bf16[18,16,128]{2,1,0:T(8,128)(2,1)S(1)} collective-permute-done((bf16[18,16,128]{2,1,0:T(8,128)(2,1)S(1)}, bf16[18,16,128]{2,1,0:T(8,128)(2,1)S(1)}, u32[]{:S(2)}, u32[]{:S(2)}) %collective-permute-start.4) | collective-permute-done | bytes 73760 | tf_op jit(solution)/shard_map/ppermute | solution.py:669
  35.9 0.0 collective-permute-done.3.refs_0_
  36.0 0.1 pad_maximum_fusion.4
  36.2 0.1 pad_maximum_fusion.5
  36.4 0.0 collective-permute-done.5.refs_5_.refs_1_
  36.5 0.0 copy-start.4
  36.5 3.4 %weight_rim.1 = (f32[2,2,2,432,128]{4,3,2,1,0:T(8,128)S(1)}, f32[2,2,2,432,128]{4,3,2,1,0:T(8,128)}, bf16[1120,128]{1,0:T(8,128)(2,1)}) custom-call(s32[1]{0:T(128)} %bitcast.8.mine_ref, bf16[2,768,256]{2,1,0:T(8,128)(2,1)S(1)} %get-tuple-element.39.fx_ref, bf16[2,768,256]{2,1,0:T(8,128)(2,1)S(1)} %get-tuple-element.40.fy_ref, ...), custom_call_target="tpu_custom_call" | custom-call | flops 1 | bytes 1 | tf_op jit(solution)/shard_map/weight_rim/pallas_call | solution.py:403
  39.9 0.0 copy-done.4
  39.9 1.2 %copy-done.6 = f32[2,2,2,432,128]{4,3,2,1,0:T(8,128)} copy-done((f32[2,2,2,432,128]{4,3,2,1,0:T(8,128)}, f32[2,2,2,432,128]{4,3,2,1,0:T(8,128)S(1)}, u32[]{:S(2)}) %copy-start.6) | copy-done | bytes 1769496
  41.2 0.2 collective-permute-start.10
  41.4 0.5 collective-permute-start.8
  41.9 1.5 %collective-permute-start.7 = (bf16[2048,128]{1,0:T(8,128)(2,1)}, bf16[2048,128]{1,0:T(8,128)(2,1)S(1)}, u32[]{:S(2)}, u32[]{:S(2)}) collective-permute-start(bf16[2048,128]{1,0:T(8,128)(2,1)} %get-tuple-element.74), channel_id=1, source_target_pairs={{0,1},{1,0},{2,3},{3,2},{4,5},{5,4},{6,7},{7,6},{8,9},{9,8},{10,11... | collective-permute-start | bytes 1572872 | tf_op jit(solution)/shard_map/ppermute | solution.py:658
  43.4 0.1 pad_add_fusion.bits_ref
  43.5 1.7 %collective-permute-done.10.recv_ref = f32[2,2,2,432,128]{4,3,2,1,0:T(8,128)} collective-permute-done((f32[2,2,2,432,128]{4,3,2,1,0:T(8,128)}, f32[2,2,2,432,128]{4,3,2,1,0:T(8,128)}, u32[]{:S(2)}, u32[]{:S(2)}) %collective-permute-start.10) | collective-permute-done | bytes 1769504 | tf_op jit(solution)/shard_map/ppermute | solution.py:563
  45.2 1.5 %copy-done.7 = f32[2,2,2,432,128]{4,3,2,1,0:T(8,128)S(1)} copy-done((f32[2,2,2,432,128]{4,3,2,1,0:T(8,128)S(1)}, f32[2,2,2,432,128]{4,3,2,1,0:T(8,128)}, u32[]{:S(2)}) %copy-start.7) | copy-done | bytes 1769496
  46.7 2.6 %add_split.5 = (f32[2,2,216,128]{3,2,1,0:T(8,128)S(1)}, f32[2,2,216,128]{3,2,1,0:T(8,128)}, f32[2,2,216,128]{3,2,1,0:T(8,128)S(1)}, f32[2,2,216,128]{3,2,1,0:T(8,128)}) custom-call(s32[2]{0:T(128)S(1)} %pad_add_fusion.bits_ref, f32[2,2,2,432,128]{4,3,2,1,0:T(8,128)S(1)} %copy-done.7, f32[2,2,2,432,128]{4,3,2,1,0:T(8,128)} %collective-permute-done.10.recv_ref), custom_call_target="tpu_custom_call" | custom-call | flops 1 | bytes 1 | tf_op jit(solution)/shard_map/add_split/pallas_call | solution.py:551
  49.3 0.8 copy-done.8
  50.1 0.8 copy-done.10
  50.9 2.4 %collective-permute-start.11 = (f32[2,2,216,128]{3,2,1,0:T(8,128)}, f32[2,2,216,128]{3,2,1,0:T(8,128)}, u32[]{:S(2)}, u32[]{:S(2)}) collective-permute-start(f32[2,2,216,128]{3,2,1,0:T(8,128)} %get-tuple-element.58.refs_3_), channel_id=1, source_target_pairs={{0,4},{2,6},{4,0},{6,2},{8,12},{10,14},{12,8},{14,10},{16,20},{18,... | collective-permute-start | bytes 1327112 | tf_op jit(solution)/shard_map/ppermute | solution.py:563
  53.2 0.2 collective-permute-start.12
  53.5 1.6 %collective-permute-done.8.refs_3_ = bf16[14,128,128]{2,1,0:T(8,128)(2,1)} collective-permute-done((bf16[14,128,128]{2,1,0:T(8,128)(2,1)}, bf16[14,128,128]{2,1,0:T(8,128)(2,1)}, u32[]{:S(2)}, u32[]{:S(2)}) %collective-permute-start.8) | collective-permute-done | bytes 458784 | tf_op jit(solution)/shard_map/ppermute | solution.py:694
  55.0 0.0 collective-permute-start.9
  55.0 0.6 collective-permute-start.6
  55.6 8.9 %data_grad.2 = (f32[4096,128]{1,0:T(8,128)S(1)}, f32[8,128]{1,0:T(8,128)S(1)}) custom-call(s32[8]{0:T(128)S(1)} %copy-done.14, f32[16,256]{1,0:T(8,128)S(1)} %get-tuple-element.38.mask_ref, bf16[1120,128]{1,0:T(8,128)(2,1)} %get-tuple-element.54.refs_0_, bf16[4096,128]{1,0:T(8,128)(2,1)S(1)} %copy-done.1, bf16[27,256,128]{2,1,0:T(8,128)(2,1)S(1)} %copy-done.2, ...), custom_call_target="tpu_custom_call" | custom-call | flops 1 | bytes 1 | tf_op jit(solution)/shard_map/data_grad/pallas_call | solution.py:510
  64.5 1.7 %collective-permute-done.7.outs_1_.refs_2_ = bf16[2048,128]{1,0:T(8,128)(2,1)S(1)} collective-permute-done((bf16[2048,128]{1,0:T(8,128)(2,1)}, bf16[2048,128]{1,0:T(8,128)(2,1)S(1)}, u32[]{:S(2)}, u32[]{:S(2)}) %collective-permute-start.7) | collective-permute-done | bytes 524320 | tf_op jit(solution)/shard_map/ppermute | solution.py:658
  66.2 0.0 collective-permute-done.11.recv_ref
  66.2 1.1 %add_split.6 = (f32[2,216,128]{2,1,0:T(8,128)S(1)}, f32[2,216,128]{2,1,0:T(8,128)S(1)}) custom-call(s32[1]{0:T(128)} %bitcast.7.bits_ref, f32[2,2,216,128]{3,2,1,0:T(8,128)S(1)} %copy-done.11, f32[2,2,216,128]{3,2,1,0:T(8,128)} %collective-permute-done.11.recv_ref, f32[8,128]{1,0:T(8,128)S(1)} %get-tuple-element.62.outs_0_, ...), custom_call_target="tpu_custom_call" | custom-call | flops 1 | bytes 1 | tf_op jit(solution)/shard_map/add_split/pallas_call | solution.py:551
  67.2 0.3 collective-permute-start.13
  67.6 0.0 collective-permute-done.12.recv_ref
  67.6 1.1 %add_split.7 = (f32[2,216,128]{2,1,0:T(8,128)S(1)}, f32[2,216,128]{2,1,0:T(8,128)S(1)}) custom-call(s32[1]{0:T(128)} %bitcast.31.bits_ref, f32[2,2,216,128]{3,2,1,0:T(8,128)S(1)} %copy-done.9, f32[2,2,216,128]{3,2,1,0:T(8,128)} %collective-permute-done.12.recv_ref, f32[8,128]{1,0:T(8,128)S(1)} %get-tuple-element.62.outs_0_, ...), custom_call_target="tpu_custom_call" | custom-call | flops 1 | bytes 1 | tf_op jit(solution)/shard_map/add_split/pallas_call | solution.py:551
  68.6 2.8 %collective-permute-start.15 = (f32[2,216,128]{2,1,0:T(8,128)S(1)}, f32[2,216,128]{2,1,0:T(8,128)S(1)}, u32[]{:S(2)}, u32[]{:S(2)}) collective-permute-start(f32[2,216,128]{2,1,0:T(8,128)S(1)} %get-tuple-element.65.refs_7_), channel_id=1, source_target_pairs={{0,16},{2,18},{4,20},{6,22},{8,24},{10,26},{12,28},{14,30},{16,0},... | collective-permute-start | bytes 663560 | tf_op jit(solution)/shard_map/ppermute | solution.py:563
  71.5 0.3 collective-permute-done.6.refs_0_
  71.8 0.0 collective-permute-done.9.refs_4_
  71.8 10.4 %data_grad.3 = (bf16[4096,128]{1,0:T(8,128)(2,1)}, f32[8,128]{1,0:T(8,128)S(1)}) custom-call(s32[8]{0:T(128)S(1)} %copy-done.14, f32[16,256]{1,0:T(8,128)S(1)} %get-tuple-element.38.mask_ref, bf16[1120,128]{1,0:T(8,128)(2,1)} %collective-permute-done.6.refs_0_, bf16[2048,128]{1,0:T(8,128)(2,1)S(1)} %copy-done.5, ...), custom_call_target="tpu_custom_call" | custom-call | flops 1 | bytes 1 | tf_op jit(solution)/shard_map/data_grad/pallas_call | solution.py:510
  82.2 0.0 collective-permute-done.13.recv_ref
  82.2 1.8 %collective-permute-start.14 = (f32[216,128]{1,0:T(8,128)S(1)}, f32[216,128]{1,0:T(8,128)S(1)}, u32[]{:S(2)}, u32[]{:S(2)}) collective-permute-start(f32[216,128]{1,0:T(8,128)S(1)} %get-tuple-element.70), channel_id=1, source_target_pairs={{0,16},{2,18},{4,20},{6,22},{8,24},{10,26},{12,28},{14,30},{16,0},... | collective-permute-start | bytes 331784 | tf_op jit(solution)/shard_map/ppermute | solution.py:563
  84.0 0.0 collective-permute-done.15.recv_ref
  84.0 2.4 %collective-permute-start.16 = (f32[216,128]{1,0:T(8,128)S(1)}, f32[216,128]{1,0:T(8,128)S(1)}, u32[]{:S(2)}, u32[]{:S(2)}) collective-permute-start(f32[216,128]{1,0:T(8,128)S(1)} %get-tuple-element.73), channel_id=1, source_target_pairs={{0,4},{2,6},{4,0},{6,2},{8,12},{10,14},{12,8},{14,10},{16,20},{18,... | collective-permute-start | bytes 331784 | tf_op jit(solution)/shard_map/ppermute | solution.py:563
  86.5 3.5 %collective-permute-done.14 = f32[216,128]{1,0:T(8,128)S(1)} collective-permute-done((f32[216,128]{1,0:T(8,128)S(1)}, f32[216,128]{1,0:T(8,128)S(1)}, u32[]{:S(2)}, u32[]{:S(2)}) %collective-permute-start.14) | collective-permute-done | bytes 110624 | tf_op jit(solution)/shard_map/ppermute | solution.py:563
  89.9 0.0 collective-permute-done.16
  90.0 0.7 pad_maximum_fusion.1
  (42 shorter events, 0.4 us)
Async XLA Ops:
  2.2 1.2 %copy-start = (bf16[4096,128]{1,0:T(8,128)(2,1)S(1)}, bf16[4096,128]{1,0:T(8,128)(2,1)}, u32[]{:S(2)}) copy-start(bf16[4096,128]{1,0:T(8,128)(2,1)} %refs_1_.1) | copy-start | bytes 3145732
  3.4 0.7 copy-start.15
  4.1 3.2 %copy-start.12 = (s32[8]{0:T(128)}, s32[8]{0:T(128)S(1)}, u32[]{:S(2)}) copy-start(s32[8]{0:T(128)S(1)} %stack.81.place_ref) | copy-start | bytes 100
  4.1 3.2 %copy-start.1 = (bf16[4096,128]{1,0:T(8,128)(2,1)S(1)}, bf16[4096,128]{1,0:T(8,128)(2,1)}, u32[]{:S(2)}) copy-start(bf16[4096,128]{1,0:T(8,128)(2,1)} %refs_1_.1) | copy-start | bytes 3145732
  5.6 12.5 %collective-permute-start = (bf16[16,16,128]{2,1,0:T(8,128)(2,1)}, bf16[16,16,128]{2,1,0:T(8,128)(2,1)S(1)}, u32[]{:S(2)}, u32[]{:S(2)}) collective-permute-start(bf16[16,16,128]{2,1,0:T(8,128)(2,1)} %get-tuple-element.42), channel_id=1, source_target_pairs={{0,2},{2,0},{4,6},{6,4},{8,10},{10,8},{12,14},{14,12},{16,18},{18,... | collective-permute-start | bytes 196616 | tf_op jit(solution)/shard_map/ppermute | solution.py:563
  6.0 12.1 %collective-permute-start.1 = (bf16[16,16,128]{2,1,0:T(8,128)(2,1)}, bf16[16,16,128]{2,1,0:T(8,128)(2,1)}, u32[]{:S(2)}, u32[]{:S(2)}) collective-permute-start(bf16[16,16,128]{2,1,0:T(8,128)(2,1)} %get-tuple-element.43), channel_id=1, source_target_pairs={{2,4},{10,12},{18,20},{26,28},{4,2},{12,10},{20,18},{28,26},{3,5},... | collective-permute-start | bytes 196616 | tf_op jit(solution)/shard_map/ppermute | solution.py:654
  8.3 9.8 %copy-start.2 = (bf16[27,256,128]{2,1,0:T(8,128)(2,1)S(1)}, bf16[27,256,128]{2,1,0:T(8,128)(2,1)}, u32[]{:S(2)}) copy-start(bf16[27,256,128]{2,1,0:T(8,128)(2,1)} %refs_2_.1) | copy-start | bytes 5308420
  8.3 28.1 %collective-permute-start.5 = (bf16[2048,128]{1,0:T(8,128)(2,1)}, bf16[2048,128]{1,0:T(8,128)(2,1)S(1)}, u32[]{:S(2)}, u32[]{:S(2)}) collective-permute-start(bf16[2048,128]{1,0:T(8,128)(2,1)} %get-tuple-element.75), channel_id=1, source_target_pairs={{0,1},{1,0},{2,3},{3,2},{4,5},{5,4},{6,7},{7,6},{8,9},{9,8},{10,11... | collective-permute-start | bytes 1572872 | tf_op jit(solution)/shard_map/ppermute | solution.py:658
  10.9 1.6 %copy-start.3 = (bf16[4096,256]{1,0:T(8,128)(2,1)S(1)}, bf16[4096,256]{1,0:T(8,128)(2,1)}, u32[]{:S(2)}) copy-start(bf16[4096,256]{1,0:T(8,128)(2,1)} %feat_ref.3) | copy-start | bytes 6291460
  12.4 5.7 %copy-start.13 = (s32[8]{0:T(128)S(1)}, s32[8]{0:T(128)}, u32[]{:S(2)}) copy-start(s32[8]{0:T(128)} %copy-done.12) | copy-start | bytes 100
  19.8 16.2 %collective-permute-start.3 = (bf16[18,16,128]{2,1,0:T(8,128)(2,1)S(1)}, bf16[18,16,128]{2,1,0:T(8,128)(2,1)S(1)}, u32[]{:S(2)}, u32[]{:S(2)}) collective-permute-start(bf16[18,16,128]{2,1,0:T(8,128)(2,1)S(1)} %get-tuple-element.48.refs_0_), channel_id=1, source_target_pairs={{0,16},{2,18},{4,20},{6,22},{8,24},{10,26},{12,28},{14,30},{16,0},... | collective-permute-start | bytes 221192 | tf_op jit(solution)/shard_map/ppermute | solution.py:668
  22.4 9.0 %collective-permute-start.2 = (bf16[32,128]{1,0:T(8,128)(2,1)S(1)}, bf16[32,128]{1,0:T(8,128)(2,1)S(1)}, u32[]{:S(2)}, u32[]{:S(2)}) collective-permute-start(bf16[32,128]{1,0:T(8,128)(2,1)S(1)} %get-tuple-element.47.refs_2_), channel_id=1, source_target_pairs={{0,24},{2,26},{4,28},{6,30},{8,16},{10,18},{12,20},{14,22},{16,8},... | collective-permute-start | bytes 24584 | tf_op jit(solution)/shard_map/ppermute | solution.py:670
  31.1 4.8 %collective-permute-start.4 = (bf16[18,16,128]{2,1,0:T(8,128)(2,1)S(1)}, bf16[18,16,128]{2,1,0:T(8,128)(2,1)S(1)}, u32[]{:S(2)}, u32[]{:S(2)}) collective-permute-start(bf16[18,16,128]{2,1,0:T(8,128)(2,1)S(1)} %get-tuple-element.49.refs_1_), channel_id=1, source_target_pairs={{0,8},{2,10},{4,12},{6,14},{8,0},{10,2},{12,4},{14,6},{16,24},{18,... | collective-permute-start | bytes 221192 | tf_op jit(solution)/shard_map/ppermute | solution.py:669
  36.5 3.4 %copy-start.4 = (bf16[2048,128]{1,0:T(8,128)(2,1)}, bf16[2048,128]{1,0:T(8,128)(2,1)S(1)}, u32[]{:S(2)}) copy-start(bf16[2048,128]{1,0:T(8,128)(2,1)S(1)} %collective-permute-done.5.refs_5_.refs_1_) | copy-start | bytes 1572868
  39.9 1.2 %copy-start.6 = (f32[2,2,2,432,128]{4,3,2,1,0:T(8,128)}, f32[2,2,2,432,128]{4,3,2,1,0:T(8,128)S(1)}, u32[]{:S(2)}) copy-start(f32[2,2,2,432,128]{4,3,2,1,0:T(8,128)S(1)} %get-tuple-element.56.keep_ref) | copy-start | bytes 5308420
  41.2 4.0 %collective-permute-start.10 = (f32[2,2,2,432,128]{4,3,2,1,0:T(8,128)}, f32[2,2,2,432,128]{4,3,2,1,0:T(8,128)}, u32[]{:S(2)}, u32[]{:S(2)}) collective-permute-start(f32[2,2,2,432,128]{4,3,2,1,0:T(8,128)} %get-tuple-element.57), channel_id=1, source_target_pairs={{0,2},{2,0},{4,6},{6,4},{8,10},{10,8},{12,14},{14,12},{16,18},{18,... | collective-permute-start | bytes 5308424 | tf_op jit(solution)/shard_map/ppermute | solution.py:563
  41.4 13.7 %collective-permute-start.8 = (bf16[14,128,128]{2,1,0:T(8,128)(2,1)}, bf16[14,128,128]{2,1,0:T(8,128)(2,1)}, u32[]{:S(2)}, u32[]{:S(2)}) collective-permute-start(bf16[14,128,128]{2,1,0:T(8,128)(2,1)} %get-tuple-element.55), channel_id=1, source_target_pairs={{0,1},{1,0},{2,3},{3,2},{4,5},{5,4},{6,7},{7,6},{8,9},{9,8},{10,11... | collective-permute-start | bytes 1376264 | tf_op jit(solution)/shard_map/ppermute | solution.py:694
  41.9 24.2 %collective-permute-start.7 = (bf16[2048,128]{1,0:T(8,128)(2,1)}, bf16[2048,128]{1,0:T(8,128)(2,1)S(1)}, u32[]{:S(2)}, u32[]{:S(2)}) collective-permute-start(bf16[2048,128]{1,0:T(8,128)(2,1)} %get-tuple-element.74), channel_id=1, source_target_pairs={{0,1},{1,0},{2,3},{3,2},{4,5},{5,4},{6,7},{7,6},{8,9},{9,8},{10,11... | collective-permute-start | bytes 1572872 | tf_op jit(solution)/shard_map/ppermute | solution.py:658
  45.2 1.5 %copy-start.7 = (f32[2,2,2,432,128]{4,3,2,1,0:T(8,128)S(1)}, f32[2,2,2,432,128]{4,3,2,1,0:T(8,128)}, u32[]{:S(2)}) copy-start(f32[2,2,2,432,128]{4,3,2,1,0:T(8,128)} %copy-done.6) | copy-start | bytes 5308420
  46.7 8.9 %copy-start.14 = (s32[8]{0:T(128)S(1)}, s32[8]{0:T(128)}, u32[]{:S(2)}) copy-start(s32[8]{0:T(128)} %copy-done.12) | copy-start | bytes 100
  49.3 0.8 copy-start.8
  50.1 0.8 copy-start.10
  50.9 15.3 %collective-permute-start.11 = (f32[2,2,216,128]{3,2,1,0:T(8,128)}, f32[2,2,216,128]{3,2,1,0:T(8,128)}, u32[]{:S(2)}, u32[]{:S(2)}) collective-permute-start(f32[2,2,216,128]{3,2,1,0:T(8,128)} %get-tuple-element.58.refs_3_), channel_id=1, source_target_pairs={{0,4},{2,6},{4,0},{6,2},{8,12},{10,14},{12,8},{14,10},{16,20},{18,... | collective-permute-start | bytes 1327112 | tf_op jit(solution)/shard_map/ppermute | solution.py:563
  53.2 14.4 %collective-permute-start.12 = (f32[2,2,216,128]{3,2,1,0:T(8,128)}, f32[2,2,216,128]{3,2,1,0:T(8,128)}, u32[]{:S(2)}, u32[]{:S(2)}) collective-permute-start(f32[2,2,216,128]{3,2,1,0:T(8,128)} %get-tuple-element.59.refs_4_), channel_id=1, source_target_pairs={{0,8},{2,10},{4,12},{6,14},{8,0},{10,2},{12,4},{14,6},{16,24},{18,... | collective-permute-start | bytes 1327112 | tf_op jit(solution)/shard_map/ppermute | solution.py:563
  55.0 16.8 %collective-permute-start.9 = (bf16[14,128,128]{2,1,0:T(8,128)(2,1)}, bf16[14,128,128]{2,1,0:T(8,128)(2,1)}, u32[]{:S(2)}, u32[]{:S(2)}) collective-permute-start(bf16[14,128,128]{2,1,0:T(8,128)(2,1)} %collective-permute-done.8.refs_3_), channel_id=1, source_target_pairs={{0,2},{2,0},{4,6},{6,4},{8,10},{10,8},{12,14},{14,12},{16,18},{18,... | collective-permute-start | bytes 1376264 | tf_op jit(solution)/shard_map/ppermute | solution.py:563
  55.0 16.8 %collective-permute-start.6 = (bf16[1120,128]{1,0:T(8,128)(2,1)}, bf16[1120,128]{1,0:T(8,128)(2,1)}, u32[]{:S(2)}, u32[]{:S(2)}) collective-permute-start(bf16[1120,128]{1,0:T(8,128)(2,1)} %get-tuple-element.54.refs_0_), channel_id=1, source_target_pairs={{0,1},{1,0},{2,3},{3,2},{4,5},{5,4},{6,7},{7,6},{8,9},{9,8},{10,11... | collective-permute-start | bytes 860168 | tf_op jit(solution)/shard_map/ppermute | solution.py:680
  55.6 10.6 %copy-start.11 = (f32[2,2,216,128]{3,2,1,0:T(8,128)S(1)}, f32[2,2,216,128]{3,2,1,0:T(8,128)}, u32[]{:S(2)}) copy-start(f32[2,2,216,128]{3,2,1,0:T(8,128)} %copy-done.10) | copy-start | bytes 1327108
  55.6 12.0 %copy-start.9 = (f32[2,2,216,128]{3,2,1,0:T(8,128)S(1)}, f32[2,2,216,128]{3,2,1,0:T(8,128)}, u32[]{:S(2)}) copy-start(f32[2,2,216,128]{3,2,1,0:T(8,128)} %copy-done.8) | copy-start | bytes 1327108
  64.5 7.3 %copy-start.5 = (bf16[2048,128]{1,0:T(8,128)(2,1)S(1)}, bf16[2048,128]{1,0:T(8,128)(2,1)}, u32[]{:S(2)}) copy-start(bf16[2048,128]{1,0:T(8,128)(2,1)} %copy-done.4) | copy-start | bytes 1572868
  67.2 14.9 %collective-permute-start.13 = (f32[2,216,128]{2,1,0:T(8,128)S(1)}, f32[2,216,128]{2,1,0:T(8,128)S(1)}, u32[]{:S(2)}, u32[]{:S(2)}) collective-permute-start(f32[2,216,128]{2,1,0:T(8,128)S(1)} %get-tuple-element.63.refs_6_), channel_id=1, source_target_pairs={{0,8},{2,10},{4,12},{6,14},{8,0},{10,2},{12,4},{14,6},{16,24},{18,... | collective-permute-start | bytes 663560 | tf_op jit(solution)/shard_map/ppermute | solution.py:563
  68.6 15.4 %collective-permute-start.15 = (f32[2,216,128]{2,1,0:T(8,128)S(1)}, f32[2,216,128]{2,1,0:T(8,128)S(1)}, u32[]{:S(2)}, u32[]{:S(2)}) collective-permute-start(f32[2,216,128]{2,1,0:T(8,128)S(1)} %get-tuple-element.65.refs_7_), channel_id=1, source_target_pairs={{0,16},{2,18},{4,20},{6,22},{8,24},{10,26},{12,28},{14,30},{16,0},... | collective-permute-start | bytes 663560 | tf_op jit(solution)/shard_map/ppermute | solution.py:563
  82.2 7.7 %collective-permute-start.14 = (f32[216,128]{1,0:T(8,128)S(1)}, f32[216,128]{1,0:T(8,128)S(1)}, u32[]{:S(2)}, u32[]{:S(2)}) collective-permute-start(f32[216,128]{1,0:T(8,128)S(1)} %get-tuple-element.70), channel_id=1, source_target_pairs={{0,16},{2,18},{4,20},{6,22},{8,24},{10,26},{12,28},{14,30},{16,0},... | collective-permute-start | bytes 331784 | tf_op jit(solution)/shard_map/ppermute | solution.py:563
  84.0 5.9 %collective-permute-start.16 = (f32[216,128]{1,0:T(8,128)S(1)}, f32[216,128]{1,0:T(8,128)S(1)}, u32[]{:S(2)}, u32[]{:S(2)}) collective-permute-start(f32[216,128]{1,0:T(8,128)S(1)} %get-tuple-element.73), channel_id=1, source_target_pairs={{0,4},{2,6},{4,0},{6,2},{8,12},{10,14},{12,8},{14,10},{16,20},{18,... | collective-permute-start | bytes 331784 | tf_op jit(solution)/shard_map/ppermute | solution.py:563
